TPU v7x, 32 devices: a whole 2x2x4 slice. The times are simulated.
32 devices in a mesh: dp: 8 (over y, x, core), tensor: 4 (over z).
Axes of the slice: x: 2, y: 2, z: 4, core: 2. Of those that a mesh axis runs over, the one named last changes fastest.
Arguments:
- block_input: float32 [4096, 2048], P(('dp', 'tensor'))
- out_grad: float32 [4096, 2048], P(('dp', 'tensor')), may hold values from -6 to 6
- segments: int32 [4096], P('dp'), may hold values from 0 to 4, never falling along the last dimension, each value on 1 to 2000 neighbouring positions
- routes: int32 [4096, 6], P('dp'), may hold values from 0 to 15, all different within a row; in each aligned block of 128 rows (0 to 127, 128 to 255, ...) at most 72 rows name the same one
- route_weight: float32 [4096, 6], P('dp'), may hold values from 0.1 to 0.6
- norm_attn: bfloat16 [2048], P(('dp', 'tensor')), may hold values from 0.5 to 1.5
- query_down: bfloat16 [2048, 1536], P(('dp', 'tensor')), may hold values from -0.125 to 0.125
- query_norm: bfloat16 [1536], P(('dp', 'tensor')), may hold values from 0.5 to 1.5
- query_up: bfloat16 [1536, 3072], P('dp', 'tensor'), may hold values from -0.15625 to 0.15625
- latent_down: bfloat16 [2048, 576], P(('dp', 'tensor')), may hold values from -0.125 to 0.125
- latent_norm: bfloat16 [512], P(('dp', 'tensor')), may hold values from 0.5 to 1.5
- latent_up: bfloat16 [512, 4096], P('dp', 'tensor'), may hold values from -0.25 to 0.25
- out_proj: bfloat16 [2048, 2048], P('dp', 'tensor'), may hold values from -1 to 1
- norm_ffn: bfloat16 [2048], P(('dp', 'tensor')), may hold values from 0.5 to 1.5
- shared_gate: bfloat16 [2048, 2816], P('dp', 'tensor'), may hold values from -0.125 to 0.125
- shared_up: bfloat16 [2048, 2816], P('dp', 'tensor'), may hold values from -0.125 to 0.125
- shared_down: bfloat16 [2048, 2816], P('dp', 'tensor'), may hold values from -0.109375 to 0.109375
- expert_gate: bfloat16 [16, 2048, 1408], P('dp', None, 'tensor'), may hold values from -0.125 to 0.125
- expert_up: bfloat16 [16, 2048, 1408], P('dp', None, 'tensor'), may hold values from -0.125 to 0.125
- expert_down: bfloat16 [16, 2048, 1408], P('dp', None, 'tensor'), may hold values from -0.15625 to 0.15625
Outputs:
- block_output: float32 [4096, 2048], P(('dp', 'tensor'))
- input_grad: float32 [4096, 2048], P(('dp', 'tensor'))
- grad_norm_attn: float32 [2048], P(('dp', 'tensor'))
- grad_query_down: float32 [2048, 1536], P(('dp', 'tensor'))
- grad_query_norm: float32 [1536], P(('dp', 'tensor'))
- grad_query_up: float32 [1536, 3072], P('dp', 'tensor')
- grad_latent_down: float32 [2048, 576], P(('dp', 'tensor'))
- grad_latent_norm: float32 [512], P(('dp', 'tensor'))
- grad_latent_up: float32 [512, 4096], P('dp', 'tensor')
- grad_out_proj: float32 [2048, 2048], P('dp', 'tensor')
- grad_norm_ffn: float32 [2048], P(('dp', 'tensor'))
- grad_shared_gate: float32 [2048, 2816], P('dp', 'tensor')
- grad_shared_up: float32 [2048, 2816], P('dp', 'tensor')
- grad_shared_down: float32 [2048, 2816], P('dp', 'tensor')
- grad_expert_gate: float32 [16, 2048, 1408], P('dp', None, 'tensor')
- grad_expert_up: float32 [16, 2048, 1408], P('dp', None, 'tensor')
- grad_expert_down: float32 [16, 2048, 1408], P('dp', None, 'tensor')
Inputs may be any that keep to these rules, and one draw needn't show every extreme that they name: `segments`: segment numbers never fall along the tokens; a segment holds at most 2000 tokens and at most half of all tokens. `routes`: each row names 6 different experts. In each aligned block of 128 rows no expert is named by more than 72 rows, a bound that some block reaches.
All inputs are finite; a program needn't handle non-finite values.
Results may differ from a plain program's by a relative error of at most 0.024.
Values may be sent and summed in bfloat16 or wider, within the bound.
No kernel may reach another device: no remote copies, remote signals or barrier semaphores. Data moves between devices by JAX's collectives and lax.ppermute only.
A program may use at most 384 MiB of HBM per device.

v0:
```python
import math

import jax
import jax.numpy as jnp
from jax import lax
from jax.sharding import PartitionSpec as P

NOPE = 128
ROPE = 64
VDIM = 128
KVRANK = 512
TOPK = 6
SEQ = 512


EPS = 1e-06
THETA = 50000.0


def as_half(values):
    return values.astype(jnp.bfloat16)


def as_single(values):
    return values.astype(jnp.float32)


def product(left, right):
    return jnp.dot(left, right, preferred_element_type=jnp.float32)


def contract_rows(left, right):
    return lax.dot_general(
        left, right, (((0,), (0,)), ((), ())), preferred_element_type=jnp.float32
    )


def against_rows(left, right):
    return lax.dot_general(
        left, right, (((1,), (1,)), ((), ())), preferred_element_type=jnp.float32
    )


def rms_scale(values):
    return lax.rsqrt(jnp.mean(values * values, axis=-1, keepdims=True) + EPS)


def norm_back(grad, normed, scale, gain):
    scaled = grad * gain
    return scale * (scaled - normed * jnp.mean(scaled * normed, axis=-1, keepdims=True))


def angles(positions):
    half = ROPE // 2
    freq = THETA ** (-jnp.arange(half, dtype=jnp.float32) * 2.0 / ROPE)
    phase = as_single(positions)[:, None] * freq[None, :]
    return (jnp.cos(phase), jnp.sin(phase))


def rotate(values, cosine, sine):
    half = values.shape[-1] // 2
    first = values[..., :half]
    second = values[..., half:]
    return jnp.concatenate(
        [first * cosine - second * sine, second * cosine + first * sine], axis=-1
    )


def unrotate(values, cosine, sine):
    half = values.shape[-1] // 2
    first = values[..., :half]
    second = values[..., half:]
    return jnp.concatenate(
        [first * cosine + second * sine, second * cosine - first * sine], axis=-1
    )


def score_block(query_nope, query_rope, key_nope, rope_key, mask):
    scale = 1.0 / math.sqrt(NOPE + ROPE)
    scores = jnp.einsum("qhd,khd->hqk", query_nope, key_nope, preferred_element_type=jnp.float32)
    scores = scores + jnp.einsum(
        "qhd,kd->hqk", query_rope, rope_key, preferred_element_type=jnp.float32
    )
    return jnp.where(mask[None], scores * scale, -jnp.inf)


def slot_table(route_rows, weight_rows, blocks, capacity, experts):
    count = route_rows.shape[0]
    flat_route = route_rows.reshape(blocks, -1)
    onehot = (flat_route[:, :, None] == jnp.arange(experts, dtype=jnp.int32)[None, None, :]).astype(
        jnp.int32
    )
    before = jnp.cumsum(onehot, axis=1) - onehot
    rank = jnp.sum(before * onehot, axis=2)
    block_id = jnp.arange(blocks, dtype=jnp.int32)[:, None]
    slot = (flat_route * (blocks * capacity) + block_id * capacity + rank).reshape(-1)
    token = jnp.repeat(jnp.arange(count, dtype=jnp.int32), route_rows.shape[1])
    total = experts * blocks * capacity
    source = jnp.full((total,), count, jnp.int32).at[slot].set(token)
    weight = jnp.zeros((total,), jnp.float32).at[slot].set(as_single(weight_rows).reshape(-1))
    return (slot, source, weight)


def pad_rows(rows):
    return jnp.concatenate([rows, jnp.zeros((1, rows.shape[1]), rows.dtype)], axis=0)


def exchange_slots(block):
    return lax.all_to_all(block, "dp", split_axis=0, concat_axis=0, tiled=True)


def gather_rows(rows):
    return lax.all_gather(rows, "tensor", axis=0, tiled=True)


def sum_rows(term_fn, own_rows):
    return lax.psum_scatter(
        term_fn(jnp.int32(0), own_rows * lax.axis_size("tensor")).astype(jnp.bfloat16),
        "tensor",
        scatter_dimension=0,
        tiled=True,
    ).astype(jnp.float32)


def body(
    block_input,
    out_grad,
    segments,
    routes,
    route_weight,
    norm_attn,
    query_down,
    query_norm,
    query_up,
    latent_down,
    latent_norm,
    latent_up,
    out_proj,
    norm_ffn,
    shared_gate,
    shared_up,
    shared_down,
    expert_gate,
    expert_up,
    expert_down,
):
    tensor_count = lax.axis_size("tensor")
    dp_count = lax.axis_size("dp")
    quarter = lax.axis_index("tensor")
    own_rows = block_input.shape[0]
    group_rows = segments.shape[0]
    local_experts = expert_gate.shape[0]
    experts = local_experts * dp_count
    capacity = own_rows * TOPK * 3 // (2 * experts)
    model = block_input.shape[1]
    down_q, down_kv, gain_attn, gain_query, gain_key, gain_ffn = (
        lax.all_gather(query_down, ("dp", "tensor"), axis=0, tiled=True),
        lax.all_gather(latent_down, ("dp", "tensor"), axis=0, tiled=True),
        lax.all_gather(norm_attn, ("dp", "tensor"), axis=0, tiled=True),
        lax.all_gather(query_norm, ("dp", "tensor"), axis=0, tiled=True),
        lax.all_gather(latent_norm, ("dp", "tensor"), axis=0, tiled=True),
        lax.all_gather(norm_ffn, ("dp", "tensor"), axis=0, tiled=True),
    )
    gain_attn = as_single(gain_attn)
    gain_query = as_single(gain_query)
    gain_key = as_single(gain_key)
    gain_ffn = as_single(gain_ffn)
    scale_in = rms_scale(block_input)
    normed_in = block_input * scale_in
    hidden_in = as_half(normed_in * gain_attn)
    query_raw = product(hidden_in, down_q)
    scale_query = rms_scale(query_raw)
    normed_query = query_raw * scale_query
    query_latent = as_half(normed_query * gain_query)
    latent_raw = product(hidden_in, down_kv)
    key_raw = latent_raw[:, :KVRANK]
    scale_key = rms_scale(key_raw)
    normed_key = key_raw * scale_key
    key_latent = as_half(normed_key * gain_key)
    own_positions = (quarter * own_rows + jnp.arange(own_rows, dtype=jnp.int32)) % SEQ
    cos_own, sin_own = angles(own_positions)
    rope_own = as_half(rotate(latent_raw[:, KVRANK:], cos_own, sin_own))
    up_q, up_kv, proj_out, gate_sh, up_sh, down_sh = (
        lax.all_gather(query_up, "dp", axis=0, tiled=True),
        lax.all_gather(latent_up, "dp", axis=0, tiled=True),
        lax.all_gather(out_proj, "dp", axis=0, tiled=True),
        lax.all_gather(shared_gate, "dp", axis=0, tiled=True),
        lax.all_gather(shared_up, "dp", axis=0, tiled=True),
        lax.all_gather(shared_down, "dp", axis=0, tiled=True),
    )
    query_all, key_all, rope_all = (
        lax.all_gather(query_latent, "tensor", axis=0, tiled=True),
        lax.all_gather(key_latent, "tensor", axis=0, tiled=True),
        lax.all_gather(rope_own, "tensor", axis=0, tiled=True),
    )
    heads = up_q.shape[1] // (NOPE + ROPE)
    cos_all, sin_all = angles(jnp.arange(group_rows, dtype=jnp.int32) % SEQ)
    query_full = product(query_all, up_q).reshape(group_rows, heads, NOPE + ROPE)
    query_nope = as_half(query_full[..., :NOPE])
    query_rope = as_half(rotate(query_full[..., NOPE:], cos_all[:, None, :], sin_all[:, None, :]))
    key_value = as_half(product(key_all, up_kv)).reshape(group_rows, heads, NOPE + VDIM)
    key_nope = key_value[..., :NOPE]
    values = key_value[..., NOPE:]
    places = jnp.arange(SEQ, dtype=jnp.int32)
    causal = places[:, None] >= places[None, :]
    mask = causal & (segments[:, None] == segments[None, :])
    scores = score_block(query_nope, query_rope, key_nope, rope_all, mask)
    total = jax.nn.logsumexp(scores, axis=-1)
    probs = as_half(jnp.exp(scores - total[..., None]))
    mixed = jnp.einsum("hqk,khd->qhd", probs, values, preferred_element_type=jnp.float32)
    mixed_parts = as_half(mixed)
    attended = mixed_parts.reshape(group_rows, heads * VDIM)

    def attention_term(start, count):
        return against_rows(attended, proj_out)

    mid = block_input + sum_rows(attention_term, own_rows)
    scale_mid = rms_scale(mid)
    normed_mid = mid * scale_mid
    hidden_mid = as_half(normed_mid * gain_ffn)
    hidden_all = gather_rows(hidden_mid)
    shared_gate_val = product(hidden_all, gate_sh)
    shared_up_val = product(hidden_all, up_sh)
    shared_act = as_half(jax.nn.silu(shared_gate_val) * shared_up_val)
    slot_ids, source, slot_weight = slot_table(
        routes, route_weight, tensor_count, capacity, experts
    )
    width = tensor_count * capacity
    send_rows = pad_rows(hidden_all)[source]
    arrived = exchange_slots(send_rows.reshape(dp_count, local_experts * width, model)).reshape(
        dp_count, local_experts, width, model
    )
    gate_e = jnp.einsum("secd,edf->secf", arrived, expert_gate, preferred_element_type=jnp.float32)
    up_e = jnp.einsum("secd,edf->secf", arrived, expert_up, preferred_element_type=jnp.float32)
    act_e = as_half(jax.nn.silu(gate_e) * up_e)
    out_e = jnp.einsum("secf,edf->secd", act_e, expert_down, preferred_element_type=jnp.float32)
    returned = exchange_slots(
        as_half(out_e).reshape(dp_count, local_experts * width, model)
    ).reshape(-1, model)
    picked = as_single(returned[slot_ids]).reshape(group_rows, TOPK, model)
    group_extra = jnp.sum(picked * route_weight[:, :, None], axis=1)

    def ffn_term(start, count):
        term = against_rows(shared_act, down_sh)
        term = term + group_extra
        return term

    block_output = mid + sum_rows(ffn_term, own_rows)
    grad_low = as_half(out_grad)
    grad_all = gather_rows(grad_low)
    d_shared_act = product(grad_all, down_sh)
    grad_down_sh = contract_rows(grad_all, shared_act)
    sigma = jax.nn.sigmoid(shared_gate_val)
    d_gate_sh = as_half(
        d_shared_act * shared_up_val * sigma * (1.0 + shared_gate_val * (1.0 - sigma))
    )
    d_up_sh = as_half(d_shared_act * shared_gate_val * sigma)
    grad_gate_sh = contract_rows(hidden_all, d_gate_sh)
    grad_up_sh = contract_rows(hidden_all, d_up_sh)
    send_grads = as_half(slot_weight[:, None] * as_single(pad_rows(grad_all)[source]))
    arrived_grad = exchange_slots(
        send_grads.reshape(dp_count, local_experts * width, model)
    ).reshape(dp_count, local_experts, width, model)
    d_act_e = jnp.einsum(
        "secd,edf->secf", arrived_grad, expert_down, preferred_element_type=jnp.float32
    )
    grad_expert_down = jnp.einsum(
        "secd,secf->edf", arrived_grad, act_e, preferred_element_type=jnp.float32
    )
    sigma_e = jax.nn.sigmoid(gate_e)
    d_gate_e = as_half(d_act_e * up_e * sigma_e * (1.0 + gate_e * (1.0 - sigma_e)))
    d_up_e = as_half(d_act_e * gate_e * sigma_e)
    grad_expert_gate = jnp.einsum(
        "secd,secf->edf", arrived, d_gate_e, preferred_element_type=jnp.float32
    )
    grad_expert_up = jnp.einsum(
        "secd,secf->edf", arrived, d_up_e, preferred_element_type=jnp.float32
    )
    back_e = jnp.einsum("secf,edf->secd", d_gate_e, expert_gate, preferred_element_type=jnp.float32)
    back_e = back_e + jnp.einsum(
        "secf,edf->secd", d_up_e, expert_up, preferred_element_type=jnp.float32
    )
    back_returned = exchange_slots(
        as_half(back_e).reshape(dp_count, local_experts * width, model)
    ).reshape(-1, model)
    back_group = jnp.sum(
        as_single(back_returned[slot_ids]).reshape(group_rows, TOPK, model), axis=1
    )

    def back_term(start, count):
        term = against_rows(d_gate_sh, gate_sh)
        term = term + against_rows(d_up_sh, up_sh)
        term = term + back_group
        return term

    d_hidden_mid = sum_rows(back_term, own_rows)
    grad_gain_ffn = jnp.sum(d_hidden_mid * normed_mid, axis=0)
    d_mid = out_grad + norm_back(d_hidden_mid, normed_mid, scale_mid, gain_ffn)
    mid_all = gather_rows(as_half(d_mid))
    grad_proj_out = contract_rows(mid_all, attended)
    d_attended = as_half(product(mid_all, proj_out)).reshape(group_rows, heads, VDIM)
    scale = 1.0 / math.sqrt(NOPE + ROPE)
    scores = score_block(query_nope, query_rope, key_nope, rope_all, mask)
    probs = jnp.exp(scores - total[..., None])
    probs_low = as_half(probs)
    value_grads = jnp.einsum(
        "hqk,qhd->khd", probs_low, d_attended, preferred_element_type=jnp.float32
    )
    d_probs = jnp.einsum("qhd,khd->hqk", d_attended, values, preferred_element_type=jnp.float32)
    delta = jnp.sum(probs * d_probs, axis=-1, keepdims=True)
    d_scores = as_half(probs * (d_probs - delta) * scale)
    query_nope_grads = jnp.einsum(
        "hqk,khd->qhd", d_scores, key_nope, preferred_element_type=jnp.float32
    )
    query_rope_grads = jnp.einsum(
        "hqk,kd->qhd", d_scores, rope_all, preferred_element_type=jnp.float32
    )
    key_nope_grads = jnp.einsum(
        "hqk,qhd->khd", d_scores, query_nope, preferred_element_type=jnp.float32
    )
    rope_key_grads = jnp.einsum(
        "hqk,qhd->kd", d_scores, query_rope, preferred_element_type=jnp.float32
    )
    d_query_rope = unrotate(query_rope_grads, cos_all[:, None, :], sin_all[:, None, :])
    d_query = as_half(jnp.concatenate([query_nope_grads, d_query_rope], axis=-1)).reshape(
        group_rows, heads * (NOPE + ROPE)
    )
    grad_up_q = contract_rows(query_all, d_query)
    d_query_latent = against_rows(d_query, up_q)
    d_key_value = as_half(jnp.concatenate([key_nope_grads, value_grads], axis=-1)).reshape(
        group_rows, heads * (NOPE + VDIM)
    )
    grad_up_kv = contract_rows(key_all, d_key_value)
    d_key_latent = against_rows(d_key_value, up_kv)
    latent_q, latent_k, latent_r = (
        lax.psum_scatter(
            d_query_latent.astype(jnp.bfloat16), "tensor", scatter_dimension=0, tiled=True
        ).astype(jnp.float32),
        lax.psum_scatter(
            d_key_latent.astype(jnp.bfloat16), "tensor", scatter_dimension=0, tiled=True
        ).astype(jnp.float32),
        lax.psum_scatter(
            rope_key_grads.astype(jnp.bfloat16), "tensor", scatter_dimension=0, tiled=True
        ).astype(jnp.float32),
    )
    grad_gain_query = jnp.sum(latent_q * normed_query, axis=0)
    d_query_raw = as_half(norm_back(latent_q, normed_query, scale_query, gain_query))
    grad_gain_key = jnp.sum(latent_k * normed_key, axis=0)
    d_key_raw = norm_back(latent_k, normed_key, scale_key, gain_key)
    d_rope_raw = unrotate(latent_r, cos_own, sin_own)
    d_latent_raw = as_half(jnp.concatenate([d_key_raw, d_rope_raw], axis=-1))
    grad_down_q = contract_rows(hidden_in, d_query_raw)
    grad_down_kv = contract_rows(hidden_in, d_latent_raw)
    d_hidden_in = against_rows(d_query_raw, down_q) + against_rows(d_latent_raw, down_kv)
    grad_gain_attn = jnp.sum(d_hidden_in * normed_in, axis=0)
    input_grad = d_mid + norm_back(d_hidden_in, normed_in, scale_in, gain_attn)
    dense_out = (
        lax.psum_scatter(
            grad_up_q.astype(jnp.bfloat16), "dp", scatter_dimension=0, tiled=True
        ).astype(jnp.float32),
        lax.psum_scatter(
            grad_up_kv.astype(jnp.bfloat16), "dp", scatter_dimension=0, tiled=True
        ).astype(jnp.float32),
        lax.psum_scatter(
            grad_proj_out.astype(jnp.bfloat16), "dp", scatter_dimension=0, tiled=True
        ).astype(jnp.float32),
        lax.psum_scatter(
            grad_gate_sh.astype(jnp.bfloat16), "dp", scatter_dimension=0, tiled=True
        ).astype(jnp.float32),
        lax.psum_scatter(
            grad_up_sh.astype(jnp.bfloat16), "dp", scatter_dimension=0, tiled=True
        ).astype(jnp.float32),
        lax.psum_scatter(
            grad_down_sh.astype(jnp.bfloat16), "dp", scatter_dimension=0, tiled=True
        ).astype(jnp.float32),
    )
    down_out = (
        lax.psum_scatter(grad_down_q, ("dp", "tensor"), scatter_dimension=0, tiled=True),
        lax.psum_scatter(grad_down_kv, ("dp", "tensor"), scatter_dimension=0, tiled=True),
        lax.psum_scatter(grad_gain_attn, ("dp", "tensor"), scatter_dimension=0, tiled=True),
        lax.psum_scatter(grad_gain_query, ("dp", "tensor"), scatter_dimension=0, tiled=True),
        lax.psum_scatter(grad_gain_key, ("dp", "tensor"), scatter_dimension=0, tiled=True),
        lax.psum_scatter(grad_gain_ffn, ("dp", "tensor"), scatter_dimension=0, tiled=True),
    )
    return (
        block_output,
        input_grad,
        down_out[2],
        down_out[0],
        down_out[3],
        dense_out[0],
        down_out[1],
        down_out[4],
        dense_out[1],
        dense_out[2],
        down_out[5],
        dense_out[3],
        dense_out[4],
        dense_out[5],
        grad_expert_gate,
        grad_expert_up,
        grad_expert_down,
    )


def solution(mesh):
    in_specs = (
        P(("dp", "tensor"), None),
        P(("dp", "tensor"), None),
        P("dp"),
        P("dp", None),
        P("dp", None),
        P(("dp", "tensor")),
        P(("dp", "tensor"), None),
        P(("dp", "tensor")),
        P("dp", "tensor"),
        P(("dp", "tensor"), None),
        P(("dp", "tensor")),
        P("dp", "tensor"),
        P("dp", "tensor"),
        P(("dp", "tensor")),
        P("dp", "tensor"),
        P("dp", "tensor"),
        P("dp", "tensor"),
        P("dp", None, "tensor"),
        P("dp", None, "tensor"),
        P("dp", None, "tensor"),
    )
    out_specs = (
        P(("dp", "tensor"), None),
        P(("dp", "tensor"), None),
        P(("dp", "tensor")),
        P(("dp", "tensor"), None),
        P(("dp", "tensor")),
        P("dp", "tensor"),
        P(("dp", "tensor"), None),
        P(("dp", "tensor")),
        P("dp", "tensor"),
        P("dp", "tensor"),
        P(("dp", "tensor")),
        P("dp", "tensor"),
        P("dp", "tensor"),
        P("dp", "tensor"),
        P("dp", None, "tensor"),
        P("dp", None, "tensor"),
        P("dp", None, "tensor"),
    )
    return jax.shard_map(body, mesh=mesh, in_specs=in_specs, out_specs=out_specs, check_vma=False)
```

profile of v0, /device:TPU:0, one launch (start us, length us, event | category | flops | bytes accessed | tf_op | source)
XLA Modules:
  0.0 2179.5 jit_solution(3424327539788773947)
XLA Ops:
  13.5 42.7 %all-reduce.11 = (bf16[2048]{0:T(1024)(128)(2,1)S(1)}, bf16[2048]{0:T(1024)(128)(2,1)S(1)}, bf16[512]{0:T(512)(128)(2,1)S(1)}, bf16[1536]{0:T(1024)(128)(2,1)S(1)}) all-reduce(bf16[2048]{0:T(1024)(128)(2,1)S(1)} %dynamic-update-slice.3, bf16[2048]{0:T(1024)(128)(2,1)S(1)} %dynamic-update-slice, ...), channel_id=1, replica_groups=mesh['dp'=8,'tensor'=4] {'dp','tensor'}, use_global_device_ids=true, to_apply=%add.5 | all-reduce | flops 6144 | bytes 24576
  59.6 23.4 %all-gather.17.cloned.1.call-done = bf16[2048,1536]{1,0:T(8,128)(2,1)} async-done(((bf16[64,1536]{1,0:T(8,128)(2,1)}), bf16[2048,1536]{1,0:T(8,128)(2,1)}) %all-gather.17.cloned.1.call-update) | async-done | bytes 6291472 | tf_op jit(solution)/shard_map/all_gather | solution.py:157
  91.1 51.1 %all-gather.13.cloned.1.call-done = bf16[2048,576]{1,0:T(8,128)(2,1)} async-done(((bf16[64,576]{1,0:T(8,128)(2,1)}), bf16[2048,576]{1,0:T(8,128)(2,1)}) %all-gather.13.cloned.1.call-update) | async-done | bytes 2359312 | tf_op jit(solution)/shard_map/all_gather | solution.py:158
  197.0 39.0 %all-gather.19.cloned.1.call-done = bf16[512,1536]{1,0:T(8,128)(2,1)} async-done(((bf16[128,1536]{1,0:T(8,128)(2,1)}), bf16[512,1536]{1,0:T(8,128)(2,1)}) %all-gather.19.cloned.1.call-update) | async-done | bytes 1572880 | tf_op jit(solution)/shard_map/all_gather | solution.py:192
  269.0 43.7 %reduce-scatter.19.cloned.1.call-done = bf16[128,2048]{1,0:T(8,128)(2,1)} async-done(((bf16[512,2048]{1,0:T(8,128)(2,1)}), bf16[128,2048]{1,0:T(8,128)(2,1)}) %reduce-scatter.19.cloned.1.call-update) | async-done | bytes 524304 | tf_op jit(solution)/shard_map/reduce_scatter | solution.py:117
  337.1 24.6 %all-gather.25.cloned.1.call-done = bf16[512,2048]{1,0:T(8,128)(2,1)} async-done(((bf16[128,2048]{1,0:T(8,128)(2,1)}), bf16[512,2048]{1,0:T(8,128)(2,1)}) %all-gather.25.cloned.1.call-update) | async-done | bytes 2097168 | tf_op jit(solution)/shard_map/all_gather | solution.py:113
  364.8 36.9 %gather_fusion = bf16[4608,2048]{1,0:T(8,128)(2,1)} fusion(bf16[513,2048]{1,0:T(8,128)(2,1)} %concatenate.28, s32[5120]{0:T(1024)S(1)} %pad_clamp_fusion), kind=kCustom, calls=%fused_computation | custom fusion | bytes 37767168 | tf_op jit(solution)/shard_map/gather | solution.py:229
  422.6 33.2 %all-gather.33.cloned.1.call-done = bf16[512,2048]{1,0:T(8,128)(2,1)} async-done(((bf16[128,2048]{1,0:T(8,128)(2,1)}), bf16[512,2048]{1,0:T(8,128)(2,1)}) %all-gather.33.cloned.1.call-update) | async-done | bytes 2097168 | tf_op jit(solution)/shard_map/all_gather | solution.py:113
  459.0 37.0 %gather_fusion.2 = bf16[4608,2048]{1,0:T(8,128)(2,1)} fusion(bf16[513,2048]{1,0:T(8,128)(2,1)} %concatenate.29, s32[5120]{0:T(1024)S(1)} %pad_clamp_fusion), kind=kCustom, calls=%fused_computation.2 | custom fusion | bytes 37767168 | tf_op jit(solution)/shard_map/gather | solution.py:260
  513.7 100.5 %all-to-all-done = bf16[8,576,2048]{2,1,0:T(8,128)(2,1)} async-done(((bf16[8,576,2048]{2,1,0:T(8,128)(2,1)}), bf16[8,576,2048]{2,1,0:T(8,128)(2,1)}, u32[]{:S(2)}, u32[]{:S(2)}) %all-to-all-start) | async-done | bytes 18874400 | tf_op jit(solution)/shard_map/all_to_all | solution.py:109
  652.4 174.1 %all-to-all-done.2 = bf16[8,576,2048]{2,1,0:T(8,128)(2,1)} async-done(((bf16[8,576,2048]{2,1,0:T(8,128)(2,1)}), bf16[8,576,2048]{2,1,0:T(8,128)(2,1)}, u32[]{:S(2)}, u32[]{:S(2)}) %all-to-all-start.2) | async-done | bytes 18874400 | tf_op jit(solution)/shard_map/all_to_all | solution.py:109
  862.0 24.9 %fusion.2 = bf16[8,2,288,2048]{3,2,0,1:T(8,128)(2,1)} fusion(f32[2,8,288,2048]{3,2,1,0:T(8,128)} %fusion.31, bf16[8,2,288,352]{3,2,0,1:T(8,128)(2,1)} %get-tuple-element.33, bf16[2,2048,352]{1,2,0:T(8,128)(2,1)} %param.38), kind=kOutput, calls=%fused_computation.11 | convolution fusion | flops 6662651904 | bytes 62750720 | tf_op jit(solution)/shard_map/secf,edf->secd/dot_general | solution.py:280
  912.1 124.5 %all-gather.29.cloned.1.call-done = bf16[2048,704]{0,1:T(8,128)(2,1)} async-done(((bf16[256,704]{0,1:T(8,128)(2,1)}), bf16[2048,704]{0,1:T(8,128)(2,1)}) %all-gather.29.cloned.1.call-update) | async-done | bytes 2883600 | tf_op jit(solution)/shard_map/all_gather | solution.py:188
  1041.8 66.5 %all-gather.27.cloned.1.call-done = bf16[2048,704]{0,1:T(8,128)(2,1)} async-done(((bf16[256,704]{0,1:T(8,128)(2,1)}), bf16[2048,704]{0,1:T(8,128)(2,1)}) %all-gather.27.cloned.1.call-update) | async-done | bytes 2883600 | tf_op jit(solution)/shard_map/all_gather | solution.py:187
  1113.6 39.4 %all-gather.31.cloned.1.call-done = bf16[2048,704]{0,1:T(8,128)(2,1)} async-done(((bf16[256,704]{0,1:T(8,128)(2,1)}), bf16[2048,704]{0,1:T(8,128)(2,1)}) %all-gather.31.cloned.1.call-update) | async-done | bytes 2883600 | tf_op jit(solution)/shard_map/all_gather | solution.py:189
  1164.5 32.9 %gather_fusion.3 = bf16[3072,2048]{1,0:T(8,128)(2,1)} fusion(bf16[4608,2048]{1,0:T(8,128)(2,1)} %bitcast.29, s32[3072]{0:T(1024)S(1)} %broadcast_clamp_fusion), kind=kCustom, calls=%fused_computation.3 | custom fusion | bytes 25178112 | tf_op jit(solution)/shard_map/gather | solution.py:287
  1245.2 41.0 %reduce-scatter.23.cloned.1.call-done = bf16[128,2048]{1,0:T(8,128)(2,1)} async-done(((bf16[512,2048]{1,0:T(8,128)(2,1)}), bf16[128,2048]{1,0:T(8,128)(2,1)}) %reduce-scatter.23.cloned.1.call-update) | async-done | bytes 524304 | tf_op jit(solution)/shard_map/reduce_scatter | solution.py:117
  1292.1 44.5 %all-gather.35.cloned.1.call-done = bf16[512,2048]{1,0:T(8,128)(2,1)} async-done(((bf16[128,2048]{1,0:T(8,128)(2,1)}), bf16[512,2048]{1,0:T(8,128)(2,1)}) %all-gather.35.cloned.1.call-update) | async-done | bytes 2097168 | tf_op jit(solution)/shard_map/all_gather | solution.py:113
  1456.2 210.4 %all-to-all-done.1 = bf16[8,576,2048]{2,1,0:T(8,128)(2,1)} async-done(((bf16[8,576,2048]{2,1,0:T(8,128)(2,1)}), bf16[8,576,2048]{2,1,0:T(8,128)(2,1)}, u32[]{:S(2)}, u32[]{:S(2)}) %all-to-all-start.1) | async-done | bytes 18874400 | tf_op jit(solution)/shard_map/all_to_all | solution.py:109
  1666.6 32.8 %gather_fusion.1 = bf16[3072,2048]{1,0:T(8,128)(2,1)} fusion(bf16[4608,2048]{1,0:T(8,128)(2,1)} %bitcast.20, s32[3072]{0:T(1024)S(1)} %broadcast_clamp_fusion), kind=kCustom, calls=%fused_computation.1 | custom fusion | bytes 25178112 | tf_op jit(solution)/shard_map/gather | solution.py:240
  1699.3 22.2 %reshape.358 = f32[512,6,2048]{2,1,0:T(8,128)} reshape(bf16[3072,2048]{1,0:T(8,128)(2,1)} %gather_fusion.1) | data formatting | bytes 37748736 | tf_op jit(solution)/shard_map/convert_element_type | solution.py:25
  1823.3 37.5 %all-reduce.10 = (f32[2048]{0:T(1024)S(1)}, f32[1536]{0:T(1024)S(1)}, f32[512]{0:T(512)S(1)}, f32[2048]{0:T(1024)S(1)}) all-reduce(f32[2048]{0:T(1024)} %get-tuple-element.19, f32[1536]{0:T(1024)} %get-tuple-element.21, f32[512]{0:T(512)} %get-tuple-element.23, ...), channel_id=8, replica_groups=mesh['dp'=8,'tensor'=4] {'dp','tensor'}, use_global_device_ids=true, to_apply=%region_25.26.clone | all-reduce | flops 6144 | bytes 49152
  1871.6 141.4 %reduce-scatter.31.cloned.1.call-done = f32[64,576]{1,0:T(8,128)} async-done(((f32[2048,576]{1,0:T(8,128)}), f32[64,576]{1,0:T(8,128)}) %reduce-scatter.31.cloned.1.call-update) | async-done | bytes 147472 | tf_op jit(solution)/shard_map/reduce_scatter | solution.py:379
  2013.0 159.8 %reduce-scatter.27.cloned.1.call-done = f32[64,1536]{1,0:T(8,128)} async-done(((f32[2048,1536]{1,0:T(8,128)}), f32[64,1536]{1,0:T(8,128)}) %reduce-scatter.27.cloned.1.call-update) | async-done | bytes 393232 | tf_op jit(solution)/shard_map/reduce_scatter | solution.py:378
  (361 shorter events, 579.9 us)
Async XLA Ops:
  7.9 134.3 %all-gather.13.cloned.1.call-start = ((), (), s32[]{:S(2)}) async-start(), calls=%async_computation.18 | async-start | bytes 2703360 | tf_op jit(solution)/shard_map/all_gather | solution.py:158
  8.7 157.7 %all-gather.15.cloned.1.call-start = ((), (), s32[]{:S(2)}) async-start(), calls=%async_computation.19 | async-start | bytes 1179648 | tf_op jit(solution)/shard_map/all_gather | solution.py:185
  9.4 187.6 %all-gather.21.cloned.1.call-start = ((), (), s32[]{:S(2)}) async-start(), calls=%async_computation.22 | async-start | bytes 2654208 | tf_op jit(solution)/shard_map/all_gather | solution.py:184
  10.0 226.0 %all-gather.19.cloned.1.call-start = ((), (), s32[]{:S(2)}) async-start(), calls=%async_computation.21 | async-start | bytes 1966080 | tf_op jit(solution)/shard_map/all_gather | solution.py:192
  88.7 175.8 %all-gather.23.cloned.1.call-start = ((), (), s32[]{:S(2)}) async-start(), calls=%async_computation.23 | async-start | bytes 2359296 | tf_op jit(solution)/shard_map/all_gather | solution.py:186
  89.3 223.4 %reduce-scatter.19.cloned.1.call-start = ((), (), s32[]{:S(2)}) async-start(), calls=%async_computation.24 | async-start | bytes 2621440 | tf_op jit(solution)/shard_map/reduce_scatter | solution.py:117
  401.8 212.4 %all-to-all-start = ((bf16[8,576,2048]{2,1,0:T(8,128)(2,1)}), bf16[8,576,2048]{2,1,0:T(8,128)(2,1)}, u32[]{:S(2)}, u32[]{:S(2)}) async-start(bf16[8,576,2048]{2,1,0:T(8,128)(2,1)} %bitcast.209), calls=%async_computation.1 | async-start | bytes 37748736 | tf_op jit(solution)/shard_map/all_to_all | solution.py:109
  614.2 212.3 %all-to-all-start.2 = ((bf16[8,576,2048]{2,1,0:T(8,128)(2,1)}), bf16[8,576,2048]{2,1,0:T(8,128)(2,1)}, u32[]{:S(2)}, u32[]{:S(2)}) async-start(bf16[8,576,2048]{2,1,0:T(8,128)(2,1)} %fusion.1), calls=%async_computation.4 | async-start | bytes 37748736 | tf_op jit(solution)/shard_map/all_to_all | solution.py:109
  903.8 260.7 %all-to-all-start.3 = ((bf16[8,576,2048]{2,1,0:T(8,128)(2,1)}), bf16[8,576,2048]{2,1,0:T(8,128)(2,1)}, u32[]{:S(2)}, u32[]{:S(2)}) async-start(bf16[8,576,2048]{2,1,0:T(8,128)(2,1)} %bitcast.212), calls=%async_computation.5 | async-start | bytes 37748736 | tf_op jit(solution)/shard_map/all_to_all | solution.py:109
  910.5 197.9 %all-gather.27.cloned.1.call-start = ((), (), s32[]{:S(2)}) async-start(), calls=%async_computation.26 | async-start | bytes 3244032 | tf_op jit(solution)/shard_map/all_gather | solution.py:187
  911.2 241.8 %all-gather.31.cloned.1.call-start = ((), (), s32[]{:S(2)}) async-start(), calls=%async_computation.28 | async-start | bytes 3244032 | tf_op jit(solution)/shard_map/all_gather | solution.py:189
  911.8 374.4 %reduce-scatter.23.cloned.1.call-start = ((), (), s32[]{:S(2)}) async-start(), calls=%async_computation.31 | async-start | bytes 2621440 | tf_op jit(solution)/shard_map/reduce_scatter | solution.py:117
  1291.5 456.0 %reduce-scatter.45.cloned.1.call-start = ((), (), s32[]{:S(2)}) async-start(), calls=%async_computation.43 | async-start | bytes 163840
  1363.5 385.1 %reduce-scatter.43.cloned.1.call-start = ((), (), s32[]{:S(2)}) async-start(), calls=%async_computation.42 | async-start | bytes 655360
  1368.5 387.6 %reduce-scatter.25.cloned.1.call-start = ((), (), s32[]{:S(2)}) async-start(), calls=%async_computation.33 | async-start | bytes 1966080 | tf_op jit(solution)/shard_map/reduce_scatter | solution.py:336
  1426.5 240.0 %all-to-all-start.1 = ((bf16[8,576,2048]{2,1,0:T(8,128)(2,1)}), bf16[8,576,2048]{2,1,0:T(8,128)(2,1)}, u32[]{:S(2)}, u32[]{:S(2)}) async-start(bf16[8,576,2048]{2,1,0:T(8,128)(2,1)} %bitcast.211), calls=%async_computation.2 | async-start | bytes 37748736 | tf_op jit(solution)/shard_map/all_to_all | solution.py:109
  1432.5 335.1 %reduce-scatter.41.cloned.1.call-start = ((), (), s32[]{:S(2)}) async-start(), calls=%async_computation.41 | async-start | bytes 3244032 | tf_op jit(solution)/shard_map/reduce_scatter | solution.py:373
  1437.7 331.8 %reduce-scatter.37.cloned.1.call-start = ((), (), s32[]{:S(2)}) async-start(), calls=%async_computation.39 | async-start | bytes 3244032 | tf_op jit(solution)/shard_map/reduce_scatter | solution.py:367
  1442.8 328.6 %reduce-scatter.39.cloned.1.call-start = ((), (), s32[]{:S(2)}) async-start(), calls=%async_computation.40 | async-start | bytes 3244032 | tf_op jit(solution)/shard_map/reduce_scatter | solution.py:370
  1448.3 365.5 %reduce-scatter.33.cloned.1.call-start = ((), (), s32[]{:S(2)}) async-start(), calls=%async_computation.37 | async-start | bytes 1179648 | tf_op jit(solution)/shard_map/reduce_scatter | solution.py:361
  1451.6 411.5 %reduce-scatter.35.cloned.1.call-start = ((), (), s32[]{:S(2)}) async-start(), calls=%async_computation.38 | async-start | bytes 2359296 | tf_op jit(solution)/shard_map/reduce_scatter | solution.py:364
  1456.1 409.5 %reduce-scatter.21.cloned.1.call-start = ((), (), s32[]{:S(2)}) async-start(), calls=%async_computation.29 | async-start | bytes 2621440 | tf_op jit(solution)/shard_map/reduce_scatter | solution.py:117
  1747.5 265.5 %reduce-scatter.31.cloned.1.call-start = ((), (), s32[]{:S(2)}) async-start(), calls=%async_computation.36 | async-start | bytes 5406720 | tf_op jit(solution)/shard_map/reduce_scatter | solution.py:379
  1756.1 416.7 %reduce-scatter.27.cloned.1.call-start = ((), (), s32[]{:S(2)}) async-start(), calls=%async_computation.34 | async-start | bytes 12976128 | tf_op jit(solution)/shard_map/reduce_scatter | solution.py:378
  (78 other events, 3005.4 us)
Sparse Core Ops, SparseCore 0:
  10.9 72.0 all-gather.16
  85.9 56.3 all-gather.12
  144.1 22.1 all-gather.14
  168.1 28.8 all-gather.20
  199.0 37.0 all-gather.18
  237.8 26.6 all-gather.22
  269.0 43.6 reduce-scatter.18
  316.7 44.8 all-gather.24
  410.8 45.0 all-gather.32
  912.3 124.2 all-gather.28
  1038.5 69.8 all-gather.26
  1110.1 42.9 all-gather.30
  1245.3 40.8 reduce-scatter.22
  1291.7 44.8 all-gather.34
  1406.3 33.6 reduce-scatter.24
  1443.8 110.4 reduce-scatter.40
  1558.3 72.5 reduce-scatter.36
  1634.6 45.6 reduce-scatter.38
  1684.1 35.9 reduce-scatter.32
  1723.4 41.1 reduce-scatter.34
  1766.8 43.6 reduce-scatter.20
  1813.7 41.5 reduce-scatter.28
  1858.1 154.7 reduce-scatter.30
  2019.4 153.3 reduce-scatter.26
  (2 shorter events, 38.1 us)
where the time goes:
time: 2190 us; the launch traced here: 2180 us
  waiting for transfers between devices  1350 us (62%)
  matrix products  296 us (14%)
  local copies, waits for them, and re-layouts  274 us (13%)
  blocking collectives  108 us (5%)
  other arithmetic  106 us (5%)
  starting transfers between devices  26.6 us (1%)
    all_to_all x4, waiting for transfers between devices, exchange_slots(): return lax.all_to_all(block, 'dp', split_axis=0, concat_axis=0, tiled=True)  485 us
    reduce_scatter x1, waiting for transfers between devices, body(): lax.psum_scatter(grad_down_q, ('dp', 'tensor'), scatter_dimension=0, tile...  160 us
    reduce_scatter x1, waiting for transfers between devices, body(): lax.psum_scatter(grad_down_kv, ('dp', 'tensor'), scatter_dimension=0, til...  141 us
    all_gather x1, waiting for transfers between devices, body(): lax.all_gather(shared_up, 'dp', axis=0, tiled=True)  125 us
    all_gather x3, waiting for transfers between devices, gather_rows(): return lax.all_gather(rows, 'tensor', axis=0, tiled=True)  102 us
    reduce_scatter x3, waiting for transfers between devices, sum_rows(): lax.psum_scatter(term_fn(jnp.int32(0), own_rows * lax.axis_size('tensor')...  84.7 us
    unnamed x2, blocking collectives  80.2 us
    all_gather x1, waiting for transfers between devices, body(): lax.all_gather(shared_gate, 'dp', axis=0, tiled=True)  66.5 us
  transfers between devices with their start and end apart: 30, of which 19 were waited for; matrix products, arithmetic and copies ran while one was open for 20% of the time, Pallas kernels for 0%

commit v1 on v0

v1 whole, which is shorter than its diff:
```python
import math

import jax
import jax.numpy as jnp
from jax import lax
from jax.sharding import PartitionSpec as P

NOPE = 128
ROPE = 64
VDIM = 128
KVRANK = 512
SEQ = 512


EPS = 1e-06
THETA = 50000.0


def as_half(values):
    return values.astype(jnp.bfloat16)


def as_single(values):
    return values.astype(jnp.float32)


def product(left, right):
    return jnp.dot(left, right, preferred_element_type=jnp.float32)


def contract_rows(left, right):
    return lax.dot_general(
        left, right, (((0,), (0,)), ((), ())), preferred_element_type=jnp.float32
    )


def against_rows(left, right):
    return lax.dot_general(
        left, right, (((1,), (1,)), ((), ())), preferred_element_type=jnp.float32
    )


def rms_scale(values):
    return lax.rsqrt(jnp.mean(values * values, axis=-1, keepdims=True) + EPS)


def norm_back(grad, normed, scale, gain):
    scaled = grad * gain
    return scale * (scaled - normed * jnp.mean(scaled * normed, axis=-1, keepdims=True))


def angles(positions):
    half = ROPE // 2
    freq = THETA ** (-jnp.arange(half, dtype=jnp.float32) * 2.0 / ROPE)
    phase = as_single(positions)[:, None] * freq[None, :]
    return (jnp.cos(phase), jnp.sin(phase))


def rotate(values, cosine, sine):
    half = values.shape[-1] // 2
    first = values[..., :half]
    second = values[..., half:]
    return jnp.concatenate(
        [first * cosine - second * sine, second * cosine + first * sine], axis=-1
    )


def unrotate(values, cosine, sine):
    half = values.shape[-1] // 2
    first = values[..., :half]
    second = values[..., half:]
    return jnp.concatenate(
        [first * cosine + second * sine, second * cosine - first * sine], axis=-1
    )


def score_block(query_nope, query_rope, key_nope, rope_key, mask):
    scale = 1.0 / math.sqrt(NOPE + ROPE)
    scores = jnp.einsum("qhd,khd->hqk", query_nope, key_nope, preferred_element_type=jnp.float32)
    scores = scores + jnp.einsum(
        "qhd,kd->hqk", query_rope, rope_key, preferred_element_type=jnp.float32
    )
    return jnp.where(mask[None], scores * scale, -jnp.inf)


LANES = 128


def padded_width(width):
    return -(-width // LANES) * LANES


def swap(rows, mask):
    count = lax.axis_size("dp")
    return lax.ppermute(rows, "dp", [(i, i ^ mask) for i in range(count)])


def four_chips():
    return lax.axis_size("dp") == 2 * 2 * 2


def fetch_chunks(rows):
    half = rows.shape[0] // 2
    along = swap(rows, 2)
    across = swap(rows, 4)
    side = swap(rows, 1)
    first = swap(along[:half], 4)
    second = swap(across[half:], 2)
    corner = jnp.concatenate([first, second], axis=0)
    return {
        0: rows,
        1: side,
        2: along,
        3: swap(along, 1),
        4: across,
        5: swap(across, 1),
        6: corner,
        7: swap(corner, 1),
    }


def spread(rows):
    if four_chips():
        chunks = fetch_chunks(rows)
        return [jnp.concatenate([chunks[m], chunks[m | 1]], axis=0) for m in (0, 2, 4, 6)]
    rounds = max(1, lax.axis_size("dp") // 8)
    size = rows.shape[0] // rounds
    return [rows[i * size : (i + 1) * size] for i in range(rounds)]


def ready(blocks, before):
    if four_chips():
        return blocks
    if before is not None:
        blocks, _ = lax.optimization_barrier((blocks, before))
    return tuple(lax.all_gather(block, "dp", axis=0, tiled=True) for block in blocks)


def hand_over(block):
    if four_chips():
        return block
    return lax.psum_scatter(block, "dp", scatter_dimension=0, tiled=True)


def collect(blocks):
    if four_chips():
        total = None
        for mask, block in zip((0, 2, 4, 6), blocks):
            count = block.shape[0] // 2
            other = swap(block[count:], 1)
            part = as_single(block[:count]) + as_single(other)
            if mask:
                part = as_single(swap(as_half(part), mask))
            total = part if total is None else total + part
        return total
    return as_single(jnp.concatenate(blocks, axis=0))


def gather_ordered(rows):
    if not four_chips():
        return lax.all_gather(rows, "dp", axis=0, tiled=True)
    place = lax.axis_index("dp")
    count = rows.shape[0]
    whole = jnp.zeros((count * lax.axis_size("dp"), rows.shape[1]), rows.dtype)
    for mask, chunk in fetch_chunks(rows).items():
        whole = lax.dynamic_update_slice(whole, chunk, ((place ^ mask) * count, 0))
    return whole


def scatter_ordered(rows):
    if not four_chips():
        return lax.psum_scatter(rows, "dp", scatter_dimension=0, tiled=True)
    place = lax.axis_index("dp")
    count = rows.shape[0] // lax.axis_size("dp")

    def part(mask):
        return lax.dynamic_slice_in_dim(rows, (place ^ mask) * count, count, axis=0)

    blocks = [jnp.concatenate([part(m), part(m | 1)], axis=0) for m in (0, 2, 4, 6)]
    return as_half(collect(blocks))


def gather_rows(rows):
    return lax.all_gather(rows, "tensor", axis=0, tiled=True)


def scatter_rows(rows):
    return as_single(
        lax.psum_scatter(as_half(rows), "tensor", scatter_dimension=0, tiled=True)
    )


def exchange(block):
    return lax.all_to_all(block, "dp", split_axis=0, concat_axis=0, tiled=True)


def split_units(weights):
    dp_count = lax.axis_size("dp")
    rows, units = weights[0].shape
    share = units // dp_count
    stacked = jnp.stack(weights).reshape(3, rows, dp_count, share).transpose(2, 0, 1, 3)
    got = exchange(stacked.reshape(dp_count, 3 * rows, share)).reshape(dp_count, 3, rows, share)
    return got.transpose(1, 0, 2, 3).reshape(3, dp_count * rows, share)


def join_units(grads):
    dp_count = lax.axis_size("dp")
    all_rows, share = grads[0].shape
    rows = all_rows // dp_count
    stacked = jnp.stack(grads).reshape(3, dp_count, rows, share).transpose(1, 0, 2, 3)
    got = exchange(stacked.reshape(dp_count, 3 * rows, share)).reshape(dp_count, 3, rows, share)
    return got.transpose(1, 2, 0, 3).reshape(3, rows, dp_count * share)


def pad_columns(values, width):
    return jnp.pad(values, ((0, 0), (0, width - values.shape[1])))


def join_columns(experts_weight, shared_slice):
    wide = padded_width(experts_weight.shape[2])
    parts = [pad_columns(experts_weight[e], wide) for e in range(experts_weight.shape[0])]
    parts.append(pad_columns(shared_slice, padded_width(shared_slice.shape[1])))
    return jnp.concatenate(parts, axis=1)


def body(
    block_input,
    out_grad,
    segments,
    routes,
    route_weight,
    norm_attn,
    query_down,
    query_norm,
    query_up,
    latent_down,
    latent_norm,
    latent_up,
    out_proj,
    norm_ffn,
    shared_gate,
    shared_up,
    shared_down,
    expert_gate,
    expert_up,
    expert_down,
):
    dp_count = lax.axis_size("dp")
    place = lax.axis_index("dp")
    quarter = lax.axis_index("tensor")
    own_rows = block_input.shape[0]
    group_rows = segments.shape[0]
    local_experts, model, expert_units = expert_gate.shape
    experts = local_experts * dp_count
    q_rank = query_down.shape[1]
    raw_width = q_rank + latent_down.shape[1]
    shard = query_down.shape[0]
    q_shard = query_norm.shape[0]

    packed_own = jnp.concatenate(
        [
            query_down,
            latent_down,
            norm_attn[:, None],
            norm_ffn[:, None],
            jnp.concatenate([query_norm, latent_norm])[:, None],
        ],
        axis=1,
    )
    packed = gather_ordered(gather_rows(packed_own))
    up_q = gather_ordered(query_up)
    up_kv = gather_ordered(latent_up)
    proj_out = lax.all_gather(out_proj, "dp", axis=0, tiled=True)
    gains = as_single(packed[:, raw_width:]).T
    gain_attn = gains[0]
    gain_ffn = gains[1]
    rank_gains = gains[2].reshape(-1, shard)
    gain_query = rank_gains[:, :q_shard].reshape(-1)
    gain_key = rank_gains[:, q_shard:].reshape(-1)

    chosen = routes[:, :, None] == jnp.arange(experts, dtype=jnp.int32)[None, None, :]
    dense_weight = jnp.sum(jnp.where(chosen, route_weight[:, :, None], 0.0), axis=1)
    weight_blocks = spread(dense_weight)
    grad_blocks = spread(gather_rows(as_half(out_grad)))

    sg, su, sd = split_units([shared_gate, shared_up, shared_down])
    cat_gate = join_columns(expert_gate, sg)
    cat_up = join_columns(expert_up, su)
    cat_down = join_columns(expert_down, sd)
    wide = padded_width(expert_units)
    column = jnp.arange(cat_gate.shape[1], dtype=jnp.int32)[None, :]

    scale_in = rms_scale(block_input)
    normed_in = block_input * scale_in
    hidden_in = as_half(normed_in * gain_attn)
    raw = product(hidden_in, packed)
    query_raw = raw[:, :q_rank]
    scale_query = rms_scale(query_raw)
    normed_query = query_raw * scale_query
    query_latent = as_half(normed_query * gain_query)
    key_raw = raw[:, q_rank : q_rank + KVRANK]
    scale_key = rms_scale(key_raw)
    normed_key = key_raw * scale_key
    key_latent = as_half(normed_key * gain_key)
    own_positions = (quarter * own_rows + jnp.arange(own_rows, dtype=jnp.int32)) % SEQ
    cos_own, sin_own = angles(own_positions)
    rope_own = as_half(rotate(raw[:, q_rank + KVRANK : raw_width], cos_own, sin_own))
    latents = gather_rows(jnp.concatenate([query_latent, key_latent, rope_own], axis=1))
    query_all = latents[:, :q_rank]
    key_all = latents[:, q_rank : q_rank + KVRANK]
    rope_all = latents[:, q_rank + KVRANK :]
    heads = up_q.shape[1] // (NOPE + ROPE)
    cos_all, sin_all = angles(jnp.arange(group_rows, dtype=jnp.int32) % SEQ)
    query_full = product(query_all, up_q).reshape(group_rows, heads, NOPE + ROPE)
    query_nope = as_half(query_full[..., :NOPE])
    query_rope = as_half(rotate(query_full[..., NOPE:], cos_all[:, None, :], sin_all[:, None, :]))
    key_value = as_half(product(key_all, up_kv)).reshape(group_rows, heads, NOPE + VDIM)
    key_nope = key_value[..., :NOPE]
    values = key_value[..., NOPE:]
    places = jnp.arange(SEQ, dtype=jnp.int32)
    causal = places[:, None] >= places[None, :]
    mask = causal & (segments[:, None] == segments[None, :])
    scores = score_block(query_nope, query_rope, key_nope, rope_all, mask)
    total = jax.nn.logsumexp(scores, axis=-1)
    probs = as_half(jnp.exp(scores - total[..., None]))
    mixed = jnp.einsum("hqk,khd->qhd", probs, values, preferred_element_type=jnp.float32)
    attended = as_half(mixed).reshape(group_rows, heads * VDIM)
    mid = block_input + scatter_rows(against_rows(attended, proj_out))
    scale_mid = rms_scale(mid)
    normed_mid = mid * scale_mid
    hidden_mid = as_half(normed_mid * gain_ffn)

    hidden_blocks = spread(gather_rows(hidden_mid))
    back_blocks = []
    act_blocks = []
    grad_gate = grad_up = grad_down = None
    for blocks in zip(hidden_blocks, grad_blocks, weight_blocks):
        hidden, grad, weights = ready(blocks, (back_blocks[-1], more) if back_blocks else None)
        mine = lax.dynamic_slice_in_dim(weights, place * local_experts, local_experts, axis=1)
        factor = jnp.ones((1, 1), jnp.float32)
        for e in range(local_experts):
            inside = (column >= e * wide) & (column < (e + 1) * wide)
            factor = jnp.where(inside, mine[:, e : e + 1], factor)
        gate_val = product(hidden, cat_gate)
        up_val = product(hidden, cat_up)
        d_act = product(grad, cat_down) * factor
        sigma = jax.nn.sigmoid(gate_val)
        act = as_half(gate_val * sigma * up_val)
        act = as_half(as_single(act) * factor)
        d_gate = as_half(d_act * up_val * sigma * (1.0 + gate_val * (1.0 - sigma)))
        d_up = as_half(d_act * gate_val * sigma)
        back = as_half(against_rows(d_gate, cat_gate) + against_rows(d_up, cat_up))
        back_blocks.append(hand_over(back))
        act_blocks.append(act)
        more = (
            contract_rows(hidden, d_gate),
            contract_rows(hidden, d_up),
            contract_rows(grad, act),
        )
        if grad_gate is None:
            grad_gate, grad_up, grad_down = more
        else:
            grad_gate, grad_up, grad_down = (
                grad_gate + more[0],
                grad_up + more[1],
                grad_down + more[2],
            )
    d_hidden_mid = scatter_rows(collect(back_blocks))

    def cut(grads):
        return jnp.stack(
            [grads[:, e * wide : e * wide + expert_units] for e in range(local_experts)]
        )

    share = sg.shape[1]
    grad_gate_sh, grad_up_sh, grad_down_sh = as_single(
        join_units(
            [
                as_half(g[:, local_experts * wide : local_experts * wide + share])
                for g in (grad_gate, grad_up, grad_down)
            ]
        )
    )

    grad_gain_ffn = jnp.sum(d_hidden_mid * normed_mid, axis=0)
    d_mid = out_grad + norm_back(d_hidden_mid, normed_mid, scale_mid, gain_ffn)
    mid_low = as_half(d_mid)
    act_blocks, mid_low = lax.optimization_barrier((act_blocks, mid_low))
    out_blocks = []
    for act in act_blocks:
        if out_blocks and not four_chips():
            act, _ = lax.optimization_barrier((act, out_blocks[-1]))
        out_blocks.append(hand_over(as_half(against_rows(act, cat_down))))
    block_output = mid + scatter_rows(collect(out_blocks))

    mid_all = gather_rows(mid_low)
    grad_proj_out = contract_rows(mid_all, attended)
    d_attended = as_half(product(mid_all, proj_out)).reshape(group_rows, heads, VDIM)
    scale = 1.0 / math.sqrt(NOPE + ROPE)
    scores = score_block(query_nope, query_rope, key_nope, rope_all, mask)
    probs = jnp.exp(scores - total[..., None])
    probs_low = as_half(probs)
    value_grads = jnp.einsum(
        "hqk,qhd->khd", probs_low, d_attended, preferred_element_type=jnp.float32
    )
    d_probs = jnp.einsum("qhd,khd->hqk", d_attended, values, preferred_element_type=jnp.float32)
    delta = jnp.sum(probs * d_probs, axis=-1, keepdims=True)
    d_scores = as_half(probs * (d_probs - delta) * scale)
    query_nope_grads = jnp.einsum(
        "hqk,khd->qhd", d_scores, key_nope, preferred_element_type=jnp.float32
    )
    query_rope_grads = jnp.einsum(
        "hqk,kd->qhd", d_scores, rope_all, preferred_element_type=jnp.float32
    )
    key_nope_grads = jnp.einsum(
        "hqk,qhd->khd", d_scores, query_nope, preferred_element_type=jnp.float32
    )
    rope_key_grads = jnp.einsum(
        "hqk,qhd->kd", d_scores, query_rope, preferred_element_type=jnp.float32
    )
    d_query_rope = unrotate(query_rope_grads, cos_all[:, None, :], sin_all[:, None, :])
    d_query = as_half(jnp.concatenate([query_nope_grads, d_query_rope], axis=-1)).reshape(
        group_rows, heads * (NOPE + ROPE)
    )
    grad_up_q = contract_rows(query_all, d_query)
    d_query_latent = against_rows(d_query, up_q)
    d_key_value = as_half(jnp.concatenate([key_nope_grads, value_grads], axis=-1)).reshape(
        group_rows, heads * (NOPE + VDIM)
    )
    grad_up_kv = contract_rows(key_all, d_key_value)
    d_key_latent = against_rows(d_key_value, up_kv)
    d_latents = scatter_rows(
        jnp.concatenate(
            [as_half(d_query_latent), as_half(d_key_latent), as_half(rope_key_grads)], axis=1
        )
    )
    latent_q = d_latents[:, :q_rank]
    latent_k = d_latents[:, q_rank : q_rank + KVRANK]
    latent_r = d_latents[:, q_rank + KVRANK :]
    grad_gain_query = jnp.sum(latent_q * normed_query, axis=0)
    d_query_raw = norm_back(latent_q, normed_query, scale_query, gain_query)
    grad_gain_key = jnp.sum(latent_k * normed_key, axis=0)
    d_key_raw = norm_back(latent_k, normed_key, scale_key, gain_key)
    d_rope_raw = unrotate(latent_r, cos_own, sin_own)
    extra = packed.shape[1] - raw_width
    d_raw = as_half(
        jnp.concatenate(
            [d_query_raw, d_key_raw, d_rope_raw, jnp.zeros((own_rows, extra), jnp.float32)], axis=1
        )
    )
    d_hidden_in = against_rows(d_raw, packed)
    grad_gain_attn = jnp.sum(d_hidden_in * normed_in, axis=0)
    input_grad = d_mid + norm_back(d_hidden_in, normed_in, scale_in, gain_attn)
    rank_grads = jnp.concatenate(
        [grad_gain_query.reshape(-1, q_shard), grad_gain_key.reshape(-1, shard - q_shard)], axis=1
    ).reshape(-1)
    gain_grads = jnp.stack([grad_gain_attn, grad_gain_ffn, rank_grads], axis=1)
    packed_grads = contract_rows(hidden_in, d_raw) + jnp.pad(gain_grads, ((0, 0), (raw_width, 0)))
    down_out = scatter_rows(scatter_ordered(as_half(packed_grads)))
    gains_out = down_out[:, raw_width:]

    def scatter_dense(grads):
        return as_single(
            lax.psum_scatter(as_half(grads), "dp", scatter_dimension=0, tiled=True)
        )

    return (
        block_output,
        input_grad,
        gains_out[:, 0],
        down_out[:, :q_rank],
        gains_out[:q_shard, 2],
        scatter_dense(grad_up_q),
        down_out[:, q_rank:raw_width],
        gains_out[q_shard:, 2],
        scatter_dense(grad_up_kv),
        scatter_dense(grad_proj_out),
        gains_out[:, 1],
        grad_gate_sh,
        grad_up_sh,
        grad_down_sh,
        cut(grad_gate),
        cut(grad_up),
        cut(grad_down),
    )


def solution(mesh):
    in_specs = (
        P(("dp", "tensor"), None),
        P(("dp", "tensor"), None),
        P("dp"),
        P("dp", None),
        P("dp", None),
        P(("dp", "tensor")),
        P(("dp", "tensor"), None),
        P(("dp", "tensor")),
        P("dp", "tensor"),
        P(("dp", "tensor"), None),
        P(("dp", "tensor")),
        P("dp", "tensor"),
        P("dp", "tensor"),
        P(("dp", "tensor")),
        P("dp", "tensor"),
        P("dp", "tensor"),
        P("dp", "tensor"),
        P("dp", None, "tensor"),
        P("dp", None, "tensor"),
        P("dp", None, "tensor"),
    )
    out_specs = (
        P(("dp", "tensor"), None),
        P(("dp", "tensor"), None),
        P(("dp", "tensor")),
        P(("dp", "tensor"), None),
        P(("dp", "tensor")),
        P("dp", "tensor"),
        P(("dp", "tensor"), None),
        P(("dp", "tensor")),
        P("dp", "tensor"),
        P("dp", "tensor"),
        P(("dp", "tensor")),
        P("dp", "tensor"),
        P("dp", "tensor"),
        P("dp", "tensor"),
        P("dp", None, "tensor"),
        P("dp", None, "tensor"),
        P("dp", None, "tensor"),
    )
    return jax.shard_map(body, mesh=mesh, in_specs=in_specs, out_specs=out_specs, check_vma=False)
```

time: 2190 us -> 1130 us (0.52)
  waiting for transfers between devices: 1350 us -> 428 us
  local copies, waits for them, and re-layouts: 274 us -> 150 us
  blocking collectives: 108 us -> 0 us
  matrix products: 296 us -> 378 us
  starting transfers between devices: 26.6 us -> 58.1 us
    all_to_all x4 -> x2, waiting for transfers between devices: 485 us -> 0.01 us  [exchange(): return lax.all_to_all(block, 'dp', split_axis=0, concat_axis=0, tiled=True)]
    all_gather x9 -> x1, waiting for transfers between devices: 375 us -> 0.02 us  [body(): proj_out = lax.all_gather(out_proj, 'dp', axis=0, tiled=True)]
    reduce_scatter x12 -> x6, waiting for transfers between devices: 386 us -> 22.7 us  [the longest x3 22.7 us: scatter_rows(): lax.psum_scatter(as_half(rows), 'tensor', scatter_dimension=0, tiled=True)]
    ppermute x0 -> x69, waiting for transfers between devices: none -> 321 us  [swap(): return lax.ppermute(rows, 'dp', [(i, i ^ mask) for i in range(count)])]
    dot_general x9 -> x0, matrix products: 148 us -> none  [the longest x1 24.9 us: body(): jnp.einsum('secf,edf->secd', d_up_e, expert_up, preferred_element_type=jn...]
    gather x4 -> x0, local copies, waits for them, and re-layouts: 140 us -> none  [the longest x1 37 us: body(): pad_rows(grad_all)[source]]
    dot_general x8 -> x16, matrix products: 37.1 us -> 121 us  [contract_rows(): lax.dot_general(left, right, (((0,), (0,)), ((), ())), preferred_element_...]
    unnamed x2 -> x0, blocking collectives: 80.2 us -> none
  transfers between devices with their start and end apart: 30 -> 85, of which waited for: 19 -> 29; matrix products, arithmetic and copies ran while one was open for 20% -> 46% of each run, Pallas kernels for 0% -> 0%
where the time goes in v1:
time: 1130 us; the launch traced here: 1120 us
  waiting for transfers between devices  428 us (38%)
  matrix products  378 us (33%)
  local copies, waits for them, and re-layouts  150 us (13%)
  other arithmetic  87.2 us (8%)
  starting transfers between devices  58.1 us (5%)
  between operations  16.6 us (1%)
    ppermute x69, waiting for transfers between devices, swap(): return lax.ppermute(rows, 'dp', [(i, i ^ mask) for i in range(count)])  321 us
    dot_general x16, matrix products, contract_rows(): lax.dot_general(left, right, (((0,), (0,)), ((), ())), preferred_element_...  121 us
    dot_general x16, matrix products, product(): return jnp.dot(left, right, preferred_element_type=jnp.float32)  114 us
    dot_general x16, matrix products, against_rows(): lax.dot_general(left, right, (((1,), (1,)), ((), ())), preferred_element_...  101 us
    all_gather x5, waiting for transfers between devices, gather_rows(): return lax.all_gather(rows, 'tensor', axis=0, tiled=True)  83.6 us
    unnamed x336, local copies, waits for them, and re-layouts  50.4 us
    ppermute x69, starting transfers between devices, swap(): return lax.ppermute(rows, 'dp', [(i, i ^ mask) for i in range(count)])  47.8 us
    convert_element_type x15, other arithmetic, as_half(): return values.astype(jnp.bfloat16)  35.3 us
  transfers between devices with their start and end apart: 85, of which 29 were waited for; matrix products, arithmetic and copies ran while one was open for 46% of the time, Pallas kernels for 0%

profile of v1, /device:TPU:0, one launch (start us, length us, event | category | flops | bytes accessed | tf_op | source)
XLA Modules:
  0.0 1118.3 jit_solution(51891139218508171)
XLA Ops:
  11.6 31.9 %all-gather.7.cloned.1.call-done = bf16[256,2115]{1,0:T(8,128)(2,1)} async-done(((bf16[64,2115]{1,0:T(8,128)(2,1)}), bf16[256,2115]{1,0:T(8,128)(2,1)}) %all-gather.7.cloned.1.call-update) | async-done | bytes 1082896 | tf_op jit(solution)/shard_map/all_gather | solution.py:184
  49.6 20.9 %collective-permute-done.1 = bf16[256,2115]{0,1:T(8,128)(2,1)} collective-permute-done((bf16[256,2115]{0,1:T(8,128)(2,1)S(1)}, bf16[256,2115]{0,1:T(8,128)(2,1)}, u32[]{:S(2)}, u32[]{:S(2)}) %collective-permute-start.1) | collective-permute-done | bytes 1082912 | tf_op jit(solution)/shard_map/ppermute | solution.py:95
  198.4 18.5 %all-gather.15.cloned.1.call-done = bf16[512,2048]{1,0:T(8,128)(2,1)} async-done(((bf16[128,2048]{1,0:T(8,128)(2,1)}), bf16[512,2048]{1,0:T(8,128)(2,1)}) %all-gather.15.cloned.1.call-update) | async-done | bytes 2097168 | tf_op jit(solution)/shard_map/all_gather | solution.py:184
  230.2 35.5 %collective-permute-done.42 = bf16[512,2048]{1,0:T(8,128)(2,1)} collective-permute-done((bf16[512,2048]{1,0:T(8,128)(2,1)}, bf16[512,2048]{1,0:T(8,128)(2,1)}, u32[]{:S(2)}, u32[]{:S(2)}) %collective-permute-start.42) | collective-permute-done | bytes 2097184 | tf_op jit(solution)/shard_map/ppermute | solution.py:95
  284.0 9.7 fusion.137
  311.1 16.9 %all-gather.13.cloned.1.call-done = bf16[512,2048]{1,0:T(8,128)(2,1)} async-done(((bf16[128,2048]{1,0:T(8,128)(2,1)}), bf16[512,2048]{1,0:T(8,128)(2,1)}) %all-gather.13.cloned.1.call-update) | async-done | bytes 2097168 | tf_op jit(solution)/shard_map/all_gather | solution.py:184
  330.9 9.6 fusion.139
  350.0 27.4 %collective-permute-done.26 = bf16[512,2048]{1,0:T(8,128)(2,1)S(1)} collective-permute-done((bf16[512,2048]{1,0:T(8,128)(2,1)}, bf16[512,2048]{1,0:T(8,128)(2,1)S(1)}, u32[]{:S(2)}, u32[]{:S(2)}) %collective-permute-start.26) | collective-permute-done | bytes 2097184 | tf_op jit(solution)/shard_map/ppermute | solution.py:95
  424.1 20.2 %multiply_convert_fusion.7 = (bf16[1024,896]{1,0:T(8,128)(2,1)}, bf16[1024,896]{1,0:T(8,128)(2,1)}, bf16[1024,896]{1,0:T(8,128)(2,1)}, bf16[1024,896]{1,0:T(8,12...) fusion(f32[1024,896]{1,0:T(8,128)} %fusion.131, ...), kind=kOutput, calls=%fused_computation.62 | convolution fusion | flops 3815899136 | bytes 51930880 | tf_op jit(solution)/shard_map/dot_general | solution.py:28
  444.4 10.6 fusion.142
  496.9 10.3 multiply_convert_fusion.1
  539.9 42.3 %collective-permute-done.49 = bf16[512,2048]{1,0:T(8,128)(2,1)S(1)} collective-permute-done((bf16[512,2048]{1,0:T(8,128)(2,1)S(1)}, bf16[512,2048]{1,0:T(8,128)(2,1)S(1)}, u32[]{:S(2)}, u32[]{:S(2)}) %collective-permute-start.49) | collective-permute-done | bytes 2097184 | tf_op jit(solution)/shard_map/ppermute | solution.py:95
  585.6 43.7 %collective-permute-done.54 = bf16[512,2048]{1,0:T(8,128)(2,1)S(1)} collective-permute-done((bf16[512,2048]{1,0:T(8,128)(2,1)S(1)}, bf16[512,2048]{1,0:T(8,128)(2,1)S(1)}, u32[]{:S(2)}, u32[]{:S(2)}) %collective-permute-start.54) | collective-permute-done | bytes 2097184 | tf_op jit(solution)/shard_map/ppermute | solution.py:95
  635.0 9.9 fusion.152
  654.4 22.7 %reduce-scatter.15.cloned.1.call-done = bf16[128,2048]{1,0:T(8,128)(2,1)} async-done(((bf16[512,2048]{1,0:T(8,128)(2,1)}), bf16[128,2048]{1,0:T(8,128)(2,1)}) %reduce-scatter.15.cloned.1.call-update) | async-done | bytes 524304 | tf_op jit(solution)/shard_map/reduce_scatter | solution.py:189
  681.7 9.9 fusion.149
  710.1 16.3 %all-gather.17.cloned.1.call-done = bf16[512,2048]{1,0:T(8,128)(2,1)} async-done(((bf16[128,2048]{1,0:T(8,128)(2,1)}), bf16[512,2048]{1,0:T(8,128)(2,1)}) %all-gather.17.cloned.1.call-update) | async-done | bytes 2097168 | tf_op jit(solution)/shard_map/all_gather | solution.py:184
  794.5 16.7 %add_add_fusion.1 = f32[2048,896]{0,1:T(8,128)} fusion(f32[2048,896]{0,1:T(8,128)} %fusion.151, f32[2048,896]{0,1:T(8,128)} %fusion.149, f32[2048,896]{0,1:T(8,128)} %fusion.150, bf16[1024,2048]{1,0:T(8,128)(2,1)S(1)} %copy-done.9, f32[1024,896]{1,0:T(8,128)} %fusion.135, f32[1024,896]{1,0:T(8,128)S(1)} %copy-done.33, f32[1024]{0:T(1024)S(1)} %bitcast.273, ...), kind=kOutput, calls=%fused_computation.21 | convolution fusion | flops 3771858944 | bytes 40904448 | tf_op jit(solution)/shard_map/dot_general | solution.py:32
  880.9 13.0 %add_add_fusion = f32[2048,896]{0,1:T(8,128)} fusion(f32[2048,896]{0,1:T(8,128)} %fusion.154, f32[2048,896]{0,1:T(8,128)} %fusion.152, f32[2048,896]{0,1:T(8,128)} %fusion.153, bf16[1024,2048]{1,0:T(8,128)(2,1)S(1)} %copy-done.59, bf16[1024,896]{1,0:T(8,128)(2,1)} %get-tuple-element.24), kind=kOutput, calls=%fused_computation.20 | convolution fusion | flops 3763601408 | bytes 35389440 | tf_op jit(solution)/shard_map/dot_general | solution.py:32
  893.9 21.7 %collective-permute-done.61 = bf16[512,2048]{1,0:T(8,128)(2,1)} collective-permute-done((bf16[512,2048]{1,0:T(8,128)(2,1)S(1)}, bf16[512,2048]{1,0:T(8,128)(2,1)}, u32[]{:S(2)}, u32[]{:S(2)}) %collective-permute-start.61) | collective-permute-done | bytes 2097184 | tf_op jit(solution)/shard_map/ppermute | solution.py:95
  915.5 48.1 %collective-permute-done.59 = bf16[512,2048]{1,0:T(8,128)(2,1)} collective-permute-done((bf16[512,2048]{1,0:T(8,128)(2,1)}, bf16[512,2048]{1,0:T(8,128)(2,1)}, u32[]{:S(2)}, u32[]{:S(2)}) %collective-permute-start.59) | collective-permute-done | bytes 2097184 | tf_op jit(solution)/shard_map/ppermute | solution.py:95
  991.4 10.3 add_add_fusion.2
  1033.5 21.5 %collective-permute-done.68 = bf16[256,2115]{0,1:T(8,128)(2,1)S(1)} collective-permute-done((bf16[256,2115]{0,1:T(8,128)(2,1)S(1)}, bf16[256,2115]{0,1:T(8,128)(2,1)S(1)}, u32[]{:S(2)}, u32[]{:S(2)}) %collective-permute-start.68) | collective-permute-done | bytes 1082912 | tf_op jit(solution)/shard_map/ppermute | solution.py:95
  1055.0 22.4 %collective-permute-done.66 = bf16[256,2115]{0,1:T(8,128)(2,1)S(1)} collective-permute-done((bf16[256,2115]{0,1:T(8,128)(2,1)S(1)}, bf16[256,2115]{0,1:T(8,128)(2,1)S(1)}, u32[]{:S(2)}, u32[]{:S(2)}) %collective-permute-start.66) | collective-permute-done | bytes 1082912 | tf_op jit(solution)/shard_map/ppermute | solution.py:95
  (738 shorter events, 591.8 us)
Async XLA Ops:
  11.5 157.5 %all-gather.9.cloned.1.call-start = ((), (), s32[]{:S(2)}) async-start(), calls=%async_computation.11 | async-start | bytes 2703360 | tf_op jit(solution)/shard_map/all_gather | solution.py:184
  94.3 91.7 %all-gather.11.cloned.1.call-start = ((), (), s32[]{:S(2)}) async-start(), calls=%async_computation.12 | async-start | bytes 2359296 | tf_op jit(solution)/shard_map/all_gather | solution.py:273
  107.9 84.3 %all-to-all-start = ((bf16[8,768,88]{1,2,0:T(8,128)(2,1)}), bf16[8,768,88]{1,2,0:T(8,128)(2,1)}, u32[]{:S(2)}, u32[]{:S(2)}) async-start(bf16[8,768,88]{1,2,0:T(8,128)(2,1)} %reshape.301), calls=%async_computation.1 | async-start | bytes 2162688 | tf_op jit(solution)/shard_map/all_to_all | solution.py:194
  112.1 104.8 %all-gather.15.cloned.1.call-start = ((), (), s32[]{:S(2)}) async-start(), calls=%async_computation.15 | async-start | bytes 2621440 | tf_op jit(solution)/shard_map/all_gather | solution.py:184
  113.1 167.6 %reduce-scatter.13.cloned.1.call-start = ((), (), s32[]{:S(2)}) async-start(), calls=%async_computation.13 | async-start | bytes 2621440 | tf_op jit(solution)/shard_map/reduce_scatter | solution.py:189
  190.4 137.5 %all-gather.13.cloned.1.call-start = ((), (), s32[]{:S(2)}) async-start(), calls=%async_computation.14 | async-start | bytes 2621440 | tf_op jit(solution)/shard_map/all_gather | solution.py:184
  223.3 55.8 %collective-permute-start.40 = (bf16[512,2048]{1,0:T(8,128)(2,1)S(1)}, bf16[512,2048]{1,0:T(8,128)(2,1)S(1)}, u32[]{:S(2)}, u32[]{:S(2)}) collective-permute-start(bf16[512,2048]{1,0:T(8,128)(2,1)S(1)} %copy-done.48), channel_id=1, source_target_pairs={{0,4},{4,0},{8,12},{12,8},{16,20},{20,16},{24,28},{28,24},{1,5},{5... | collective-permute-start | bytes 6291464 | tf_op jit(solution)/shard_map/ppermute | solution.py:95
  284.0 393.1 %reduce-scatter.15.cloned.1.call-start = ((), (), s32[]{:S(2)}) async-start(), calls=%async_computation.16 | async-start | bytes 2621440 | tf_op jit(solution)/shard_map/reduce_scatter | solution.py:189
  327.9 51.8 %collective-permute-start.24 = (bf16[512,2048]{1,0:T(8,128)(2,1)}, bf16[512,2048]{1,0:T(8,128)(2,1)S(1)}, u32[]{:S(2)}, u32[]{:S(2)}) collective-permute-start(bf16[512,2048]{1,0:T(8,128)(2,1)} %all-gather.13.cloned.1.call-done), channel_id=1, source_target_pairs={{0,4},{4,0},{8,12},{12,8},{16,20},{20,16},{24,28},{28,24},{1,5},{5... | collective-permute-start | bytes 6291464 | tf_op jit(solution)/shard_map/ppermute | solution.py:95
  403.9 84.9 %collective-permute-start.36 = (bf16[512,2048]{1,0:T(8,128)(2,1)}, bf16[512,2048]{1,0:T(8,128)(2,1)}, u32[]{:S(2)}, u32[]{:S(2)}) collective-permute-start(bf16[512,2048]{1,0:T(8,128)(2,1)} %pad_maximum_fusion.4), channel_id=1, source_target_pairs={{0,4},{4,0},{8,12},{12,8},{16,20},{20,16},{24,28},{28,24},{1,5},{5... | collective-permute-start | bytes 6291464 | tf_op jit(solution)/shard_map/ppermute | solution.py:95
  464.5 69.2 %collective-permute-start.48 = (bf16[512,2048]{1,0:T(8,128)(2,1)}, bf16[512,2048]{1,0:T(8,128)(2,1)S(1)}, u32[]{:S(2)}, u32[]{:S(2)}) collective-permute-start(bf16[512,2048]{1,0:T(8,128)(2,1)} %slice.389), channel_id=1, source_target_pairs={{0,4},{4,0},{8,12},{12,8},{16,20},{20,16},{24,28},{28,24},{1,5},{5... | collective-permute-start | bytes 6291464 | tf_op jit(solution)/shard_map/ppermute | solution.py:95
  481.1 55.1 %collective-permute-start.44 = (bf16[512,2048]{1,0:T(8,128)(2,1)}, bf16[512,2048]{1,0:T(8,128)(2,1)S(1)}, u32[]{:S(2)}, u32[]{:S(2)}) collective-permute-start(bf16[512,2048]{1,0:T(8,128)(2,1)} %slice.387), channel_id=1, source_target_pairs={{0,4},{4,0},{8,12},{12,8},{16,20},{20,16},{24,28},{28,24},{1,5},{5... | collective-permute-start | bytes 6291464 | tf_op jit(solution)/shard_map/ppermute | solution.py:95
  539.3 90.0 %collective-permute-start.54 = (bf16[512,2048]{1,0:T(8,128)(2,1)S(1)}, bf16[512,2048]{1,0:T(8,128)(2,1)S(1)}, u32[]{:S(2)}, u32[]{:S(2)}) collective-permute-start(bf16[512,2048]{1,0:T(8,128)(2,1)S(1)} %add_convert_fusion.9), channel_id=1, source_target_pairs={{0,24},{4,28},{8,16},{12,20},{16,8},{20,12},{24,0},{28,4},{1,25},{... | collective-permute-start | bytes 6291464 | tf_op jit(solution)/shard_map/ppermute | solution.py:95
  634.5 91.9 %all-gather.17.cloned.1.call-start = ((), (), s32[]{:S(2)}) async-start(), calls=%async_computation.18 | async-start | bytes 2621440 | tf_op jit(solution)/shard_map/all_gather | solution.py:184
  681.4 290.0 %reduce-scatter.25.cloned.1.call-start = ((), (), s32[]{:S(2)}) async-start(), calls=%async_computation.22 | async-start | bytes 2785280
  778.3 319.8 %reduce-scatter.21.cloned.1.call-start = ((), (), s32[]{:S(2)}) async-start(), calls=%async_computation.20 | async-start | bytes 1179648 | tf_op jit(solution)/shard_map/reduce_scatter | solution.py:464
  814.1 285.6 %reduce-scatter.23.cloned.1.call-start = ((), (), s32[]{:S(2)}) async-start(), calls=%async_computation.21 | async-start | bytes 2359296 | tf_op jit(solution)/shard_map/reduce_scatter | solution.py:464
  836.8 264.7 %reduce-scatter.19.cloned.1.call-start = ((), (), s32[]{:S(2)}) async-start(), calls=%async_computation.19 | async-start | bytes 2654208 | tf_op jit(solution)/shard_map/reduce_scatter | solution.py:464
  860.3 55.2 %collective-permute-start.61 = (bf16[512,2048]{1,0:T(8,128)(2,1)S(1)}, bf16[512,2048]{1,0:T(8,128)(2,1)}, u32[]{:S(2)}, u32[]{:S(2)}) collective-permute-start(bf16[512,2048]{1,0:T(8,128)(2,1)S(1)} %add_convert_fusion.5), channel_id=1, source_target_pairs={{0,24},{4,28},{8,16},{12,20},{16,8},{20,12},{24,0},{28,4},{1,25},{... | collective-permute-start | bytes 6291464 | tf_op jit(solution)/shard_map/ppermute | solution.py:95
  866.4 97.2 %collective-permute-start.59 = (bf16[512,2048]{1,0:T(8,128)(2,1)}, bf16[512,2048]{1,0:T(8,128)(2,1)}, u32[]{:S(2)}, u32[]{:S(2)}) collective-permute-start(bf16[512,2048]{1,0:T(8,128)(2,1)} %add_convert_fusion.6), channel_id=1, source_target_pairs={{0,16},{4,20},{8,24},{12,28},{16,0},{20,4},{24,8},{28,12},{1,17},{... | collective-permute-start | bytes 6291464 | tf_op jit(solution)/shard_map/ppermute | solution.py:95
  869.9 233.4 %reduce-scatter.17.cloned.1.call-start = ((), (), s32[]{:S(2)}) async-start(), calls=%async_computation.17 | async-start | bytes 2621440 | tf_op jit(solution)/shard_map/reduce_scatter | solution.py:189
  873.4 91.3 %collective-permute-start.57 = (bf16[512,2048]{1,0:T(8,128)(2,1)S(1)}, bf16[512,2048]{1,0:T(8,128)(2,1)S(1)}, u32[]{:S(2)}, u32[]{:S(2)}) collective-permute-start(bf16[512,2048]{1,0:T(8,128)(2,1)S(1)} %add_convert_fusion.7), channel_id=1, source_target_pairs={{0,8},{4,12},{8,0},{12,4},{16,24},{20,28},{24,16},{28,20},{1,9},{5... | collective-permute-start | bytes 6291464 | tf_op jit(solution)/shard_map/ppermute | solution.py:95
  1011.6 75.6 %all-to-all-start.1 = ((bf16[8,768,88]{1,2,0:T(8,128)(2,1)}), bf16[8,768,88]{1,2,0:T(8,128)(2,1)S(1)}, u32[]{:S(2)}, u32[]{:S(2)}) async-start(bf16[8,768,88]{1,2,0:T(8,128)(2,1)} %reshape.306), calls=%async_computation.7 | async-start | bytes 2162688 | tf_op jit(solution)/shard_map/all_to_all | solution.py:194
  1015.4 91.3 %reduce-scatter.27.cloned.1.call-start = ((), (), s32[]{:S(2)}) async-start(), calls=%async_computation.23 | async-start | bytes 1392640
  (215 other events, 3141.0 us)
Sparse Core Ops, SparseCore 0:
  11.6 31.7 all-gather.6
  94.4 46.9 all-gather.8
  143.2 27.9 all-gather.10
  173.2 43.6 all-gather.14
  219.6 42.4 reduce-scatter.12
  284.1 43.7 all-gather.12
  634.6 42.3 reduce-scatter.14
  681.5 44.8 all-gather.16
  778.4 44.4 reduce-scatter.24
  826.5 35.3 reduce-scatter.20
  865.1 68.8 reduce-scatter.22
  937.3 42.6 reduce-scatter.18
  982.2 43.6 reduce-scatter.16
  1081.3 24.9 reduce-scatter.26

commit v2 on v1

--- a/solution.py
+++ b/solution.py
@@ -3,6 +3,7 @@
 import jax
 import jax.numpy as jnp
 from jax import lax
+from jax.experimental.layout import Layout, with_layout_constraint
 from jax.sharding import PartitionSpec as P
 
 NOPE = 128
@@ -83,11 +84,18 @@
     return jnp.where(mask[None], scores * scale, -jnp.inf)
 
 
-LANES = 128
-
-
-def padded_width(width):
-    return -(-width // LANES) * LANES
+def after(value, *before):
+    return lax.optimization_barrier((value, before))[0]
+
+
+def fold_rows(rows, base):
+    _, width = rows.shape
+    return rows.reshape(-1, base, width).transpose(1, 0, 2).reshape(base, -1)
+
+
+def unfold_rows(rows, times):
+    base = rows.shape[0]
+    return rows.reshape(base, times, -1).transpose(1, 0, 2).reshape(base * times, -1)
 
 
 def swap(rows, mask):
@@ -119,41 +127,35 @@
     }
 
 
-def spread(rows):
-    if four_chips():
-        chunks = fetch_chunks(rows)
-        return [jnp.concatenate([chunks[m], chunks[m | 1]], axis=0) for m in (0, 2, 4, 6)]
-    rounds = max(1, lax.axis_size("dp") // 8)
-    size = rows.shape[0] // rounds
-    return [rows[i * size : (i + 1) * size] for i in range(rounds)]
-
-
-def ready(blocks, before):
-    if four_chips():
-        return blocks
-    if before is not None:
-        blocks, _ = lax.optimization_barrier((blocks, before))
-    return tuple(lax.all_gather(block, "dp", axis=0, tiled=True) for block in blocks)
-
-
-def hand_over(block):
-    if four_chips():
-        return block
+CHIPS = (0, 2, 4, 6)
+
+
+def both_cores(rows):
+    return jnp.concatenate([rows, swap(rows, 1)], axis=0)
+
+
+def pair_sum(block):
+    count = block.shape[0] // 2
+    return as_half(as_single(block[:count]) + as_single(swap(block[count:], 1)))
+
+
+def send_part(part, mask):
+    return swap(part, mask) if mask else part
+
+
+def add_parts(parts):
+    total = as_single(parts[0])
+    for part in parts[1:]:
+        total = total + as_single(part)
+    return as_half(total)
+
+
+def scatter_plane(block):
     return lax.psum_scatter(block, "dp", scatter_dimension=0, tiled=True)
 
 
-def collect(blocks):
-    if four_chips():
-        total = None
-        for mask, block in zip((0, 2, 4, 6), blocks):
-            count = block.shape[0] // 2
-            other = swap(block[count:], 1)
-            part = as_single(block[:count]) + as_single(other)
-            if mask:
-                part = as_single(swap(as_half(part), mask))
-            total = part if total is None else total + part
-        return total
-    return as_single(jnp.concatenate(blocks, axis=0))
+def gather_plane(block):
+    return lax.all_gather(block, "dp", axis=0, tiled=True)
 
 
 def gather_ordered(rows):
@@ -164,20 +166,40 @@
     whole = jnp.zeros((count * lax.axis_size("dp"), rows.shape[1]), rows.dtype)
     for mask, chunk in fetch_chunks(rows).items():
         whole = lax.dynamic_update_slice(whole, chunk, ((place ^ mask) * count, 0))
-    return whole
-
-
-def scatter_ordered(rows):
+    return with_layout_constraint(whole, Layout(major_to_minor=(0, 1)))
+
+
+def reorder(values, axis):
     if not four_chips():
-        return lax.psum_scatter(rows, "dp", scatter_dimension=0, tiled=True)
+        return values
     place = lax.axis_index("dp")
+    count = lax.axis_size("dp")
+    size = values.shape[axis] // count
+    return jnp.concatenate(
+        [
+            lax.dynamic_slice_in_dim(values, (place ^ m) * size, size, axis=axis)
+            for m in range(count)
+        ],
+        axis=axis,
+    )
+
+
+def gather_reordered(rows):
+    if not four_chips():
+        return gather_plane(rows)
+    chunks = fetch_chunks(rows)
+    return jnp.concatenate([chunks[m] for m in range(len(chunks))], axis=0)
+
+
+def parts_of(rows):
     count = rows.shape[0] // lax.axis_size("dp")
 
     def part(mask):
-        return lax.dynamic_slice_in_dim(rows, (place ^ mask) * count, count, axis=0)
-
-    blocks = [jnp.concatenate([part(m), part(m | 1)], axis=0) for m in (0, 2, 4, 6)]
-    return as_half(collect(blocks))
+        return rows[mask * count : (mask + 1) * count]
+
+    return [
+        as_half(as_single(part(m)) + as_single(swap(part(m | 1), 1))) for m in CHIPS
+    ]
 
 
 def gather_rows(rows):
@@ -198,32 +220,29 @@
     dp_count = lax.axis_size("dp")
     rows, units = weights[0].shape
     share = units // dp_count
-    stacked = jnp.stack(weights).reshape(3, rows, dp_count, share).transpose(2, 0, 1, 3)
-    got = exchange(stacked.reshape(dp_count, 3 * rows, share)).reshape(dp_count, 3, rows, share)
-    return got.transpose(1, 0, 2, 3).reshape(3, dp_count * rows, share)
+    stacked = jnp.stack([w.T for w in weights]).reshape(3, dp_count, share, rows)
+    stacked = stacked.transpose(1, 0, 2, 3).reshape(dp_count, 3 * share, rows)
+    got = exchange(stacked).reshape(dp_count, 3, share, rows)
+    return got.transpose(1, 2, 0, 3).reshape(3, share, dp_count * rows)
 
 
 def join_units(grads):
     dp_count = lax.axis_size("dp")
-    all_rows, share = grads[0].shape
+    share, all_rows = grads[0].shape
     rows = all_rows // dp_count
-    stacked = jnp.stack(grads).reshape(3, dp_count, rows, share).transpose(1, 0, 2, 3)
-    got = exchange(stacked.reshape(dp_count, 3 * rows, share)).reshape(dp_count, 3, rows, share)
-    return got.transpose(1, 2, 0, 3).reshape(3, rows, dp_count * share)
-
-
-def pad_columns(values, width):
-    return jnp.pad(values, ((0, 0), (0, width - values.shape[1])))
-
-
-def join_columns(experts_weight, shared_slice):
-    wide = padded_width(experts_weight.shape[2])
-    parts = [pad_columns(experts_weight[e], wide) for e in range(experts_weight.shape[0])]
-    parts.append(pad_columns(shared_slice, padded_width(shared_slice.shape[1])))
-    return jnp.concatenate(parts, axis=1)
-
-
-def body(
+    stacked = jnp.stack(grads).reshape(3, share, dp_count, rows).transpose(2, 0, 1, 3)
+    got = exchange(stacked.reshape(dp_count, 3 * share, rows)).reshape(dp_count, 3, share, rows)
+    return [g.T for g in got.transpose(1, 0, 2, 3).reshape(3, dp_count * share, rows)]
+
+
+def join_rows(experts_weight, shared_slice):
+    count, model, units = experts_weight.shape
+    return jnp.concatenate(
+        [experts_weight.swapaxes(1, 2).reshape(count * units, model), shared_slice], axis=0
+    )
+
+
+def layer(
     block_input,
     out_grad,
     segments,
@@ -267,31 +286,53 @@
         ],
         axis=1,
     )
-    packed = gather_ordered(gather_rows(packed_own))
-    up_q = gather_ordered(query_up)
-    up_kv = gather_ordered(latent_up)
-    proj_out = lax.all_gather(out_proj, "dp", axis=0, tiled=True)
+    packed_line = gather_rows(packed_own)
+    base = latent_up.shape[0]
+    denses = (query_up, latent_up, out_proj)
+    times = [w.shape[0] // base for w in denses]
+    ends = [0]
+    for w in denses:
+        ends.append(ends[-1] + w.size // base)
+    chosen = routes[:, :, None] == jnp.arange(experts, dtype=jnp.int32)[None, None, :]
+    dense_weight = jnp.sum(jnp.where(chosen, route_weight[:, :, None], 0.0), axis=1)
+    upper = as_half(dense_weight)
+    terms = jnp.concatenate([upper, as_half(dense_weight - as_single(upper))], axis=1)
+    folds = [fold_rows(w, base) for w in (*denses, terms)]
+    folded = gather_ordered(jnp.concatenate(after(folds, packed_own), axis=1))
+
+    def unfold_whole(index):
+        part = folded[:, ends[index] : ends[index + 1]]
+        width = denses[index].shape[1]
+        part = part.reshape(dp_count, base, times[index], width).transpose(0, 2, 1, 3)
+        return part.reshape(-1, width)
+
+    packed_line, folded = lax.optimization_barrier((packed_line, folded))
+    up_q, up_kv, proj_out = (unfold_whole(i) for i in range(3))
+    terms_all = folded[:, ends[3] :].reshape(dp_count, base, group_rows // base, 2, experts)
+    mine_terms = lax.dynamic_slice_in_dim(terms_all, place * local_experts, local_experts, axis=4)
+    mine_terms = as_single(mine_terms).transpose(0, 2, 1, 3, 4)
+    weights_all = jnp.sum(mine_terms, axis=3).reshape(-1, local_experts)
+    packed = gather_reordered(packed_line)
+    grad_line = gather_rows(after(as_half(out_grad), packed_line))
     gains = as_single(packed[:, raw_width:]).T
     gain_attn = gains[0]
-    gain_ffn = gains[1]
-    rank_gains = gains[2].reshape(-1, shard)
+    gain_ffn, rank_gains = reorder(gains[1:], 1)
+    rank_gains = rank_gains.reshape(-1, shard)
     gain_query = rank_gains[:, :q_shard].reshape(-1)
     gain_key = rank_gains[:, q_shard:].reshape(-1)
 
-    chosen = routes[:, :, None] == jnp.arange(experts, dtype=jnp.int32)[None, None, :]
-    dense_weight = jnp.sum(jnp.where(chosen, route_weight[:, :, None], 0.0), axis=1)
-    weight_blocks = spread(dense_weight)
-    grad_blocks = spread(gather_rows(as_half(out_grad)))
-
-    sg, su, sd = split_units([shared_gate, shared_up, shared_down])
-    cat_gate = join_columns(expert_gate, sg)
-    cat_up = join_columns(expert_up, su)
-    cat_down = join_columns(expert_down, sd)
-    wide = padded_width(expert_units)
-    column = jnp.arange(cat_gate.shape[1], dtype=jnp.int32)[None, :]
+    sg, su, sd = split_units(after([shared_gate, shared_up, shared_down], packed))
+    grad_line = after(grad_line, sg)
+    cat_gate = join_rows(expert_gate, sg)
+    cat_up = join_rows(expert_up, su)
+    cat_down = join_rows(expert_down, sd)
+    if four_chips():
+        grad_chunks = [grad_line] + [swap(grad_line, m) for m in CHIPS[1:]]
+
+    column = jnp.arange(local_experts * expert_units + shared_gate.shape[1] // dp_count)[None, :]
 
     scale_in = rms_scale(block_input)
-    normed_in = block_input * scale_in
+    normed_in = reorder(block_input * scale_in, 1)
     hidden_in = as_half(normed_in * gain_attn)
     raw = product(hidden_in, packed)
     query_raw = raw[:, :q_rank]
@@ -305,7 +346,8 @@
     own_positions = (quarter * own_rows + jnp.arange(own_rows, dtype=jnp.int32)) % SEQ
     cos_own, sin_own = angles(own_positions)
     rope_own = as_half(rotate(raw[:, q_rank + KVRANK : raw_width], cos_own, sin_own))
-    latents = gather_rows(jnp.concatenate([query_latent, key_latent, rope_own], axis=1))
+    latents_own = jnp.concatenate([query_latent, key_latent, rope_own], axis=1)
+    latents = gather_rows(after(latents_own, grad_line))
     query_all = latents[:, :q_rank]
     key_all = latents[:, q_rank : q_rank + KVRANK]
     rope_all = latents[:, q_rank + KVRANK :]
@@ -325,77 +367,133 @@
     probs = as_half(jnp.exp(scores - total[..., None]))
     mixed = jnp.einsum("hqk,khd->qhd", probs, values, preferred_element_type=jnp.float32)
     attended = as_half(mixed).reshape(group_rows, heads * VDIM)
-    mid = block_input + scatter_rows(against_rows(attended, proj_out))
+    projected = against_rows(attended, proj_out)
+    mid = block_input + scatter_rows(projected)
     scale_mid = rms_scale(mid)
     normed_mid = mid * scale_mid
     hidden_mid = as_half(normed_mid * gain_ffn)
 
-    hidden_blocks = spread(gather_rows(hidden_mid))
-    back_blocks = []
-    act_blocks = []
-    grad_gate = grad_up = grad_down = None
-    for blocks in zip(hidden_blocks, grad_blocks, weight_blocks):
-        hidden, grad, weights = ready(blocks, (back_blocks[-1], more) if back_blocks else None)
-        mine = lax.dynamic_slice_in_dim(weights, place * local_experts, local_experts, axis=1)
+    hidden_line = gather_rows(hidden_mid)
+
+    def expert_block(hidden, d_act_raw, grad, mine, before=()):
         factor = jnp.ones((1, 1), jnp.float32)
         for e in range(local_experts):
-            inside = (column >= e * wide) & (column < (e + 1) * wide)
+            inside = (column >= e * expert_units) & (column < (e + 1) * expert_units)
             factor = jnp.where(inside, mine[:, e : e + 1], factor)
-        gate_val = product(hidden, cat_gate)
-        up_val = product(hidden, cat_up)
-        d_act = product(grad, cat_down) * factor
+        gate_val = against_rows(hidden, cat_gate)
+        hidden, gate_val = after((hidden, gate_val), before)
+        up_val = against_rows(hidden, cat_up)
+        d_act = d_act_raw * factor
         sigma = jax.nn.sigmoid(gate_val)
         act = as_half(gate_val * sigma * up_val)
         act = as_half(as_single(act) * factor)
         d_gate = as_half(d_act * up_val * sigma * (1.0 + gate_val * (1.0 - sigma)))
         d_up = as_half(d_act * gate_val * sigma)
-        back = as_half(against_rows(d_gate, cat_gate) + against_rows(d_up, cat_up))
-        back_blocks.append(hand_over(back))
-        act_blocks.append(act)
-        more = (
-            contract_rows(hidden, d_gate),
-            contract_rows(hidden, d_up),
-            contract_rows(grad, act),
+        back = product(d_gate, cat_gate)
+        back = as_half(back + product(d_up, cat_up))
+        more = (hidden, grad, d_gate, d_up, act)
+        return back, more
+
+    def weight_grads(sums, more):
+        hidden, grad, d_gate, d_up, act = more
+        new = (
+            contract_rows(d_gate, hidden),
+            contract_rows(d_up, hidden),
+            contract_rows(act, grad),
         )
-        if grad_gate is None:
-            grad_gate, grad_up, grad_down = more
-        else:
-            grad_gate, grad_up, grad_down = (
-                grad_gate + more[0],
-                grad_up + more[1],
-                grad_down + more[2],
+        return new if sums is None else tuple(x + y for x, y in zip(sums, new))
+
+    def sum_over(terms):
+        total = terms[0]
+        for term in terms[1:]:
+            total = total + term
+        return total
+
+    sums = None
+    act_blocks = []
+    out_parts = []
+    if four_chips():
+        def block_weights(mask):
+            far = [
+                lax.dynamic_slice_in_dim(weights_all, (place ^ m) * group_rows, group_rows, axis=0)
+                for m in (mask, mask | 1)
+            ]
+            return jnp.concatenate(far, axis=0)
+
+        grad_chunks = after(grad_chunks, projected)
+        grad_blocks = [both_cores(chunk) for chunk in grad_chunks]
+        raw_blocks = [against_rows(grad, cat_down) for grad in grad_blocks]
+        mine_blocks = [block_weights(m) for m in CHIPS]
+        hidden_line, raw_blocks, mine_blocks = lax.optimization_barrier(
+            (hidden_line, raw_blocks, mine_blocks)
+        )
+        half = group_rows // 2
+        along = swap(hidden_line, 2)
+        across = swap(hidden_line, 4)
+        back, more = expert_block(
+            both_cores(hidden_line), raw_blocks[0], grad_blocks[0], mine_blocks[0]
+        )
+        mores = [more]
+        own_back = back
+        along, across = after((along, across), back)
+        corner = [swap(along[:half], 4), swap(across[half:], 2)]
+        corner = jnp.concatenate(corner, axis=0)
+        arrived = []
+        before = ()
+        for i, chunk in enumerate((along, across, corner), 1):
+            back, more = expert_block(
+                both_cores(after(chunk, back)), raw_blocks[i], grad_blocks[i], mine_blocks[i], before
             )
-    d_hidden_mid = scatter_rows(collect(back_blocks))
-
-    def cut(grads):
-        return jnp.stack(
-            [grads[:, e * wide : e * wide + expert_units] for e in range(local_experts)]
-        )
-
-    share = sg.shape[1]
-    grad_gate_sh, grad_up_sh, grad_down_sh = as_single(
-        join_units(
-            [
-                as_half(g[:, local_experts * wide : local_experts * wide + share])
-                for g in (grad_gate, grad_up, grad_down)
-            ]
-        )
-    )
+            mores.append(more)
+            part = pair_sum(back)
+            before = (part,)
+            arrived.append(swap(part, CHIPS[i]))
+        grad_gate = sum_over([contract_rows(more[2], more[0]) for more in mores])
+        grad_up = sum_over([contract_rows(more[3], more[0]) for more in mores])
+        arrived[-1], grad_gate, grad_up = lax.optimization_barrier((arrived[-1], grad_gate, grad_up))
+        back_sum = add_parts([pair_sum(own_back), *arrived])
+        act_blocks = [more[4] for more in mores]
+    else:
+        rounds = max(1, dp_count // 8)
+        size = group_rows // rounds
+        rounds_weights = weights_all.reshape(dp_count, rounds, size, local_experts)
+        backs = []
+        for i in range(rounds):
+            rows = (hidden_line[i * size : (i + 1) * size], grad_line[i * size : (i + 1) * size])
+            if backs:
+                rows = after(rows, backs[-1], sums)
+            hidden, grad = (gather_plane(r) for r in rows)
+            mine = rounds_weights[:, i].reshape(-1, local_experts)
+            back, more = expert_block(hidden, against_rows(grad, cat_down), grad, mine)
+            sums = weight_grads(sums, more)
+            act_blocks.append(more[4])
+            backs.append(scatter_plane(back))
+        back_sum = jnp.concatenate(backs, axis=0)
+    d_hidden_mid = scatter_rows(back_sum)
 
     grad_gain_ffn = jnp.sum(d_hidden_mid * normed_mid, axis=0)
     d_mid = out_grad + norm_back(d_hidden_mid, normed_mid, scale_mid, gain_ffn)
     mid_low = as_half(d_mid)
-    act_blocks, mid_low = lax.optimization_barrier((act_blocks, mid_low))
-    out_blocks = []
-    for act in act_blocks:
-        if out_blocks and not four_chips():
-            act, _ = lax.optimization_barrier((act, out_blocks[-1]))
-        out_blocks.append(hand_over(as_half(against_rows(act, cat_down))))
-    block_output = mid + scatter_rows(collect(out_blocks))
+    act_blocks = after(act_blocks, back_sum)
+    if four_chips():
+        out_parts = [pair_sum(as_half(product(act, cat_down))) for act in act_blocks]
+    else:
+        for act in act_blocks:
+            if out_parts:
+                act = after(act, out_parts[-1])
+            out_parts.append(scatter_plane(as_half(product(act, cat_down))))
 
     mid_all = gather_rows(mid_low)
+    if four_chips():
+        late_acts = after(act_blocks, mid_low)
+        grad_down = sum_over([contract_rows(a, g) for a, g in zip(late_acts, grad_blocks)])
+        sums = (grad_gate, grad_up, grad_down)
+    mid_all = after(mid_all, sums)
+    shared_sums = after([as_half(g[local_experts * expert_units :]) for g in sums], mid_all)
+    shared_grads = join_units(shared_sums)
     grad_proj_out = contract_rows(mid_all, attended)
-    d_attended = as_half(product(mid_all, proj_out)).reshape(group_rows, heads, VDIM)
+    d_attended = product(mid_all, proj_out)
+    d_attended = as_half(d_attended).reshape(group_rows, heads, VDIM)
     scale = 1.0 / math.sqrt(NOPE + ROPE)
     scores = score_block(query_nope, query_rope, key_nope, rope_all, mask)
     probs = jnp.exp(scores - total[..., None])
@@ -429,11 +527,31 @@
     )
     grad_up_kv = contract_rows(key_all, d_key_value)
     d_key_latent = against_rows(d_key_value, up_kv)
-    d_latents = scatter_rows(
-        jnp.concatenate(
-            [as_half(d_query_latent), as_half(d_key_latent), as_half(rope_key_grads)], axis=1
-        )
-    )
+    d_latents_own = jnp.concatenate(
+        [as_half(d_query_latent), as_half(d_key_latent), as_half(rope_key_grads)], axis=1
+    )
+    d_latents_own, shared_grads = lax.optimization_barrier((d_latents_own, shared_grads))
+    d_latents = scatter_rows(d_latents_own)
+    sums = after(sums, d_latents_own)
+    grad_gate, grad_up, grad_down = sums
+
+    def fold_whole(grads, index):
+        width = denses[index].shape[1]
+        part = as_half(grads).reshape(dp_count, times[index], base, width).transpose(0, 2, 1, 3)
+        return part.reshape(dp_count * base, -1)
+
+    dense_grads = (grad_up_q, grad_up_kv, grad_proj_out)
+    folded_grads = jnp.concatenate([fold_whole(g, i) for i, g in enumerate(dense_grads)], axis=1)
+    folded_grads = after(folded_grads, d_latents_own)
+    if four_chips():
+        dense_own = parts_of(reorder(folded_grads, 0))
+        dense_parts = [send_part(p, m) for p, m in zip(dense_own, CHIPS)]
+        out_parts = [send_part(p, m) for p, m in zip(out_parts, CHIPS)]
+        out_sum = add_parts(out_parts)
+    else:
+        dense_sums = scatter_plane(folded_grads)
+        out_sum = jnp.concatenate(out_parts, axis=0)
+    block_output = mid + scatter_rows(after(out_sum, d_latents_own))
     latent_q = d_latents[:, :q_rank]
     latent_k = d_latents[:, q_rank : q_rank + KVRANK]
     latent_r = d_latents[:, q_rank + KVRANK :]
@@ -450,19 +568,31 @@
     )
     d_hidden_in = against_rows(d_raw, packed)
     grad_gain_attn = jnp.sum(d_hidden_in * normed_in, axis=0)
-    input_grad = d_mid + norm_back(d_hidden_in, normed_in, scale_in, gain_attn)
+    input_grad = d_mid + reorder(norm_back(d_hidden_in, normed_in, scale_in, gain_attn), 1)
     rank_grads = jnp.concatenate(
         [grad_gain_query.reshape(-1, q_shard), grad_gain_key.reshape(-1, shard - q_shard)], axis=1
     ).reshape(-1)
-    gain_grads = jnp.stack([grad_gain_attn, grad_gain_ffn, rank_grads], axis=1)
-    packed_grads = contract_rows(hidden_in, d_raw) + jnp.pad(gain_grads, ((0, 0), (raw_width, 0)))
-    down_out = scatter_rows(scatter_ordered(as_half(packed_grads)))
+    late_grads = reorder(jnp.stack([grad_gain_ffn, rank_grads]), 1)
+    gain_grads = jnp.concatenate([grad_gain_attn[None], late_grads], axis=0).T
+    packed_grads = contract_rows(hidden_in, d_raw)
+    packed_grads = packed_grads + jnp.pad(gain_grads, ((0, 0), (raw_width, 0)))
+    if four_chips():
+        packed_parts = [send_part(p, m) for p, m in zip(parts_of(as_half(packed_grads)), CHIPS)]
+        packed_sums = add_parts(packed_parts)
+        dense_sums = add_parts(after(dense_parts, packed_sums))
+    else:
+        packed_sums = scatter_plane(as_half(packed_grads))
+    down_out = scatter_rows(packed_sums)
+    up_q_out, up_kv_out, proj_grad_out = (
+        as_single(unfold_rows(dense_sums[:, ends[i] : ends[i + 1]], times[i])) for i in range(3)
+    )
+    grad_gate_sh, grad_up_sh, grad_down_sh = (as_single(g) for g in shared_grads)
     gains_out = down_out[:, raw_width:]
 
-    def scatter_dense(grads):
-        return as_single(
-            lax.psum_scatter(as_half(grads), "dp", scatter_dimension=0, tiled=True)
-        )
+    routed_units = local_experts * expert_units
+
+    def cut(grads):
+        return grads[:routed_units].reshape(local_experts, expert_units, model).swapaxes(1, 2)
 
     return (
         block_output,
@@ -470,11 +600,11 @@
         gains_out[:, 0],
         down_out[:, :q_rank],
         gains_out[:q_shard, 2],
-        scatter_dense(grad_up_q),
+        up_q_out,
         down_out[:, q_rank:raw_width],
         gains_out[q_shard:, 2],
-        scatter_dense(grad_up_kv),
-        scatter_dense(grad_proj_out),
+        up_kv_out,
+        proj_grad_out,
         gains_out[:, 1],
         grad_gate_sh,
         grad_up_sh,
@@ -527,4 +657,4 @@
         P("dp", None, "tensor"),
         P("dp", None, "tensor"),
     )
-    return jax.shard_map(body, mesh=mesh, in_specs=in_specs, out_specs=out_specs, check_vma=False)
+    return jax.shard_map(layer, mesh=mesh, in_specs=in_specs, out_specs=out_specs, check_vma=False)

time: 1130 us -> 1030 us (0.912)
  matrix products: 378 us -> 306 us
  waiting for transfers between devices: 428 us -> 361 us
  local copies, waits for them, and re-layouts: 150 us -> 185 us
  other arithmetic: 87.2 us -> 101 us
    dot_general x16, matrix products: 121 us -> 88 us  [contract_rows(): lax.dot_general(left, right, (((0,), (0,)), ((), ())), preferred_element_...]
    ppermute x69 -> x59, waiting for transfers between devices: 321 us -> 289 us  [swap(): return lax.ppermute(rows, 'dp', [(i, i ^ mask) for i in range(count)])]
    convert_element_type x15 -> x22, other arithmetic: 35.3 us -> 66.6 us  [as_half(): return values.astype(jnp.bfloat16)]
    all_gather x5, waiting for transfers between devices: 83.6 us -> 57.9 us  [gather_rows(): return lax.all_gather(rows, 'tensor', axis=0, tiled=True)]
    dot_general x16, matrix products: 101 us -> 75.4 us  [against_rows(): lax.dot_general(left, right, (((1,), (1,)), ((), ())), preferred_element_...]
    slice x20 -> x31, local copies, waits for them, and re-layouts: 14.8 us -> 34.8 us  [the longest x3 12.3 us: cut(): grads[:routed_units].reshape(local_experts, expert_units, model)]
    another operation x16 -> x5, local copies, waits for them, and re-layouts: 18.5 us -> 2.38 us  [the longest x1 1.27 us: join_units(): got.transpose(1, 0, 2, 3).reshape(3, dp_count * share, rows)]
    reduce_scatter x3, waiting for transfers between devices: 22.7 us -> 6.67 us  [scatter_rows(): lax.psum_scatter(as_half(rows), 'tensor', scatter_dimension=0, tiled=True)]
  transfers between devices with their start and end apart: 85 -> 71, of which waited for: 29 -> 28; matrix products, arithmetic and copies ran while one was open for 46% -> 48% of each run, Pallas kernels for 0% -> 0%
where the time goes in v2:
time: 1030 us; the launch traced here: 1020 us
  waiting for transfers between devices  361 us (35%)
  matrix products  306 us (30%)
  local copies, waits for them, and re-layouts  185 us (18%)
  other arithmetic  101 us (10%)
  starting transfers between devices  50.6 us (5%)
  between operations  16.9 us (2%)
    ppermute x59, waiting for transfers between devices, swap(): return lax.ppermute(rows, 'dp', [(i, i ^ mask) for i in range(count)])  289 us
    dot_general x16, matrix products, product(): return jnp.dot(left, right, preferred_element_type=jnp.float32)  101 us
    dot_general x16, matrix products, contract_rows(): lax.dot_general(left, right, (((0,), (0,)), ((), ())), preferred_element_...  88 us
    dot_general x16, matrix products, against_rows(): lax.dot_general(left, right, (((1,), (1,)), ((), ())), preferred_element_...  75.4 us
    convert_element_type x22, other arithmetic, as_half(): return values.astype(jnp.bfloat16)  66.6 us
    unnamed x344, local copies, waits for them, and re-layouts  63.2 us
    all_gather x5, waiting for transfers between devices, gather_rows(): return lax.all_gather(rows, 'tensor', axis=0, tiled=True)  57.9 us
    ppermute x59, starting transfers between devices, swap(): return lax.ppermute(rows, 'dp', [(i, i ^ mask) for i in range(count)])  41.3 us
  transfers between devices with their start and end apart: 71, of which 28 were waited for; matrix products, arithmetic and copies ran while one was open for 48% of the time, Pallas kernels for 0%

profile of v2, /device:TPU:0, one launch (start us, length us, event | category | flops | bytes accessed | tf_op | source)
XLA Modules:
  0.0 1019.7 jit_solution(17448776928588186645)
XLA Ops:
  23.8 14.6 %collective-permute-done.1 = bf16[64,5632]{1,0:T(8,128)(2,1)} collective-permute-done((bf16[64,5632]{1,0:T(8,128)(2,1)}, bf16[64,5632]{1,0:T(8,128)(2,1)}, u32[]{:S(2)}, u32[]{:S(2)}) %collective-permute-start.1) | collective-permute-done | bytes 720928 | tf_op jit(solution)/shard_map/ppermute | solution.py:103
  68.8 16.1 %collective-permute-done.9 = bf16[256,2115]{0,1:T(8,128)(2,1)} collective-permute-done((bf16[256,2115]{0,1:T(8,128)(2,1)}, bf16[256,2115]{0,1:T(8,128)(2,1)}, u32[]{:S(2)}, u32[]{:S(2)}) %collective-permute-start.9) | collective-permute-done | bytes 1082912 | tf_op jit(solution)/shard_map/ppermute | solution.py:103
  176.2 18.5 %all-gather.10.cloned.1.call-done = bf16[512,2112]{0,1:T(8,128)(2,1)} async-done(((bf16[128,2112]{0,1:T(8,128)(2,1)}), bf16[512,2112]{0,1:T(8,128)(2,1)}) %all-gather.10.cloned.1.call-update) | async-done | bytes 2162704 | tf_op jit(solution)/shard_map/all_gather | solution.py:206
  221.5 44.2 %collective-permute-done.17 = bf16[512,2048]{1,0:T(8,128)(2,1)} collective-permute-done((bf16[512,2048]{1,0:T(8,128)(2,1)}, bf16[512,2048]{1,0:T(8,128)(2,1)}, u32[]{:S(2)}, u32[]{:S(2)}) %collective-permute-start.17) | collective-permute-done | bytes 2097184 | tf_op jit(solution)/shard_map/ppermute | solution.py:103
  292.5 8.4 fusion.123
  317.0 21.2 %all-gather.12.cloned.1.call-done = bf16[512,2048]{1,0:T(8,128)(2,1)} async-done(((bf16[128,2048]{1,0:T(8,128)(2,1)}), bf16[512,2048]{1,0:T(8,128)(2,1)}) %all-gather.12.cloned.1.call-update) | async-done | bytes 2097168 | tf_op jit(solution)/shard_map/all_gather | solution.py:206
  372.1 15.5 %collective-permute-done.24 = bf16[512,2048]{1,0:T(8,128)(2,1)S(1)} collective-permute-done((bf16[512,2048]{1,0:T(8,128)(2,1)}, bf16[512,2048]{1,0:T(8,128)(2,1)S(1)}, u32[]{:S(2)}, u32[]{:S(2)}) %collective-permute-start.24) | collective-permute-done | bytes 2097184 | tf_op jit(solution)/shard_map/ppermute | solution.py:103
  425.3 23.1 %collective-permute-done.30 = bf16[256,2048]{1,0:T(8,128)(2,1)S(1)} collective-permute-done((bf16[256,2048]{1,0:T(8,128)(2,1)S(1)}, bf16[256,2048]{1,0:T(8,128)(2,1)S(1)}, u32[]{:S(2)}, u32[]{:S(2)}) %collective-permute-start.30) | collective-permute-done | bytes 1048608 | tf_op jit(solution)/shard_map/ppermute | solution.py:103
  477.0 8.2 add_convert_fusion.2
  511.4 8.1 multiply_convert_fusion.2
  527.7 11.6 %add_convert_fusion.1 = bf16[1024,2048]{1,0:T(8,128)(2,1)S(1)} fusion(f32[1024,2048]{1,0:T(8,128)} %fusion.112, bf16[88,2048]{1,0:T(8,128)(2,1)S(1)} %bitcast.320, bf16[704,2048]{1,0:T(8,128)(2,1)} %bitcast.359, f32[1024,792]{0,1:T(8,128)} %copy-done.31, f32[1024,792]{0,1:T(8,128)} %copy-done.30, f32[1024]{0:T(1024)S(1)} %bitcast.338, ...), kind=kOutput, calls=%fused_computation.2 | convolution fusion | flops 3339870208 | bytes 22324784 | tf_op jit(solution)/shard_map/dot_general | solution.py:29
  540.7 8.2 fusion.139
  565.3 9.5 add_add_fusion.2
  574.8 14.4 %add_add_fusion.1 = f32[792,2048]{1,0:T(8,128)} fusion(f32[792,2048]{1,0:T(8,128)} %fusion.140, f32[792,2048]{1,0:T(8,128)S(1)} %fusion.138, f32[792,2048]{1,0:T(8,128)} %fusion.139, bf16[1024,2048]{1,0:T(8,128)(2,1)S(1)} %constant_dynamic-update-slice_fusion.41, f32[1024,792]{0,1:T(8,128)} %copy-done.31, f32[1024,792]{0,1:T(8,128)} %copy-done.30, ...), kind=kOutput, calls=%fused_computation.7 | convolution fusion | flops 3334053888 | bytes 36644400 | tf_op jit(solution)/shard_map/dot_general | solution.py:33
  589.2 53.9 %collective-permute-done.37 = bf16[512,2048]{1,0:T(8,128)(2,1)} collective-permute-done((bf16[512,2048]{1,0:T(8,128)(2,1)}, bf16[512,2048]{1,0:T(8,128)(2,1)}, u32[]{:S(2)}, u32[]{:S(2)}) %collective-permute-start.37) | collective-permute-done | bytes 2097184 | tf_op jit(solution)/shard_map/ppermute | solution.py:103
  643.1 10.9 %collective-permute-done.35 = bf16[512,2048]{1,0:T(8,128)(2,1)} collective-permute-done((bf16[512,2048]{1,0:T(8,128)(2,1)}, bf16[512,2048]{1,0:T(8,128)(2,1)}, u32[]{:S(2)}, u32[]{:S(2)}) %collective-permute-start.35) | collective-permute-done | bytes 2097184 | tf_op jit(solution)/shard_map/ppermute | solution.py:103
  733.3 18.2 %all-gather.14.cloned.1.call-done = bf16[512,2048]{1,0:T(8,128)(2,1)} async-done(((bf16[128,2048]{1,0:T(8,128)(2,1)}), bf16[512,2048]{1,0:T(8,128)(2,1)}) %all-gather.14.cloned.1.call-update) | async-done | bytes 2097168 | tf_op jit(solution)/shard_map/all_gather | solution.py:206
  759.7 8.8 fusion.36
  768.5 8.7 fusion.40
  781.5 8.7 fusion.28
  839.1 26.6 %collective-permute-done.42 = bf16[512,2048]{1,0:T(8,128)(2,1)S(1)} collective-permute-done((bf16[512,2048]{1,0:T(8,128)(2,1)S(1)}, bf16[512,2048]{1,0:T(8,128)(2,1)S(1)}, u32[]{:S(2)}, u32[]{:S(2)}) %collective-permute-start.42) | collective-permute-done | bytes 2097184 | tf_op jit(solution)/shard_map/ppermute | solution.py:103
  937.5 14.2 %collective-permute-done.51 = bf16[256,2115]{0,1:T(8,128)(2,1)} collective-permute-done((bf16[256,2115]{0,1:T(8,128)(2,1)}, bf16[256,2115]{0,1:T(8,128)(2,1)}, u32[]{:S(2)}, u32[]{:S(2)}) %collective-permute-start.51) | collective-permute-done | bytes 1082912 | tf_op jit(solution)/shard_map/ppermute | solution.py:103
  952.4 22.6 %collective-permute-done.49 = bf16[256,2115]{0,1:T(8,128)(2,1)} collective-permute-done((bf16[256,2115]{0,1:T(8,128)(2,1)}, bf16[256,2115]{0,1:T(8,128)(2,1)}, u32[]{:S(2)}, u32[]{:S(2)}) %collective-permute-start.49) | collective-permute-done | bytes 1082912 | tf_op jit(solution)/shard_map/ppermute | solution.py:103
  979.8 23.2 %collective-permute-done.56 = bf16[64,5376]{1,0:T(8,128)(2,1)S(1)} collective-permute-done((bf16[64,5376]{1,0:T(8,128)(2,1)}, bf16[64,5376]{1,0:T(8,128)(2,1)S(1)}, u32[]{:S(2)}, u32[]{:S(2)}) %collective-permute-start.56) | collective-permute-done | bytes 688160 | tf_op jit(solution)/shard_map/ppermute | solution.py:103
  (738 shorter events, 585.3 us)
Async XLA Ops:
  11.5 136.3 %all-gather.8.cloned.1.call-start = ((), (), s32[]{:S(2)}) async-start(), calls=%async_computation.8 | async-start | bytes 2621440 | tf_op jit(solution)/shard_map/all_gather | solution.py:206
  130.1 64.6 %all-gather.10.cloned.1.call-start = ((), (), s32[]{:S(2)}) async-start(), calls=%async_computation.9 | async-start | bytes 2703360 | tf_op jit(solution)/shard_map/all_gather | solution.py:206
  147.8 141.4 %reduce-scatter.10.cloned.1.call-start = ((), (), s32[]{:S(2)}) async-start(), calls=%async_computation.10 | async-start | bytes 2621440 | tf_op jit(solution)/shard_map/reduce_scatter | solution.py:211
  173.2 92.6 %collective-permute-start.17 = (bf16[512,2048]{1,0:T(8,128)(2,1)}, bf16[512,2048]{1,0:T(8,128)(2,1)}, u32[]{:S(2)}, u32[]{:S(2)}) collective-permute-start(bf16[512,2048]{1,0:T(8,128)(2,1)} %all-gather.8.cloned.1.call-done), channel_id=1, source_target_pairs={{0,16},{4,20},{8,24},{12,28},{16,0},{20,4},{24,8},{28,12},{1,17},{... | collective-permute-start | bytes 6291464 | tf_op jit(solution)/shard_map/ppermute | solution.py:103
  173.8 91.9 %collective-permute-start.18 = (bf16[512,2048]{1,0:T(8,128)(2,1)}, bf16[512,2048]{1,0:T(8,128)(2,1)}, u32[]{:S(2)}, u32[]{:S(2)}) collective-permute-start(bf16[512,2048]{1,0:T(8,128)(2,1)} %all-gather.8.cloned.1.call-done), channel_id=1, source_target_pairs={{0,24},{4,28},{8,16},{12,20},{16,8},{20,12},{24,0},{28,4},{1,25},{... | collective-permute-start | bytes 6291464 | tf_op jit(solution)/shard_map/ppermute | solution.py:103
  214.7 123.5 %all-gather.12.cloned.1.call-start = ((), (), s32[]{:S(2)}) async-start(), calls=%async_computation.11 | async-start | bytes 2621440 | tf_op jit(solution)/shard_map/all_gather | solution.py:206
  292.4 410.4 %reduce-scatter.12.cloned.1.call-start = ((), (), s32[]{:S(2)}) async-start(), calls=%async_computation.12 | async-start | bytes 2621440 | tf_op jit(solution)/shard_map/reduce_scatter | solution.py:211
  492.2 150.9 %collective-permute-start.33 = (bf16[512,2048]{1,0:T(8,128)(2,1)}, bf16[512,2048]{1,0:T(8,128)(2,1)}, u32[]{:S(2)}, u32[]{:S(2)}) collective-permute-start(bf16[512,2048]{1,0:T(8,128)(2,1)} %slice.370), channel_id=1, source_target_pairs={{0,4},{4,0},{8,12},{12,8},{16,20},{20,16},{24,28},{28,24},{1,5},{5... | collective-permute-start | bytes 6291464 | tf_op jit(solution)/shard_map/ppermute | solution.py:103
  548.9 94.2 %collective-permute-start.34 = (bf16[512,2048]{1,0:T(8,128)(2,1)}, bf16[512,2048]{1,0:T(8,128)(2,1)}, u32[]{:S(2)}, u32[]{:S(2)}) collective-permute-start(bf16[512,2048]{1,0:T(8,128)(2,1)} %add_convert_fusion.14), channel_id=1, source_target_pairs={{0,8},{4,12},{8,0},{12,4},{16,24},{20,28},{24,16},{28,20},{1,9},{5... | collective-permute-start | bytes 6291464 | tf_op jit(solution)/shard_map/ppermute | solution.py:103
  561.1 92.9 %collective-permute-start.35 = (bf16[512,2048]{1,0:T(8,128)(2,1)}, bf16[512,2048]{1,0:T(8,128)(2,1)}, u32[]{:S(2)}, u32[]{:S(2)}) collective-permute-start(bf16[512,2048]{1,0:T(8,128)(2,1)} %add_convert_fusion.13), channel_id=1, source_target_pairs={{0,16},{4,20},{8,24},{12,28},{16,0},{20,4},{24,8},{28,12},{1,17},{... | collective-permute-start | bytes 6291464 | tf_op jit(solution)/shard_map/ppermute | solution.py:103
  564.8 78.4 %collective-permute-start.37 = (bf16[512,2048]{1,0:T(8,128)(2,1)}, bf16[512,2048]{1,0:T(8,128)(2,1)}, u32[]{:S(2)}, u32[]{:S(2)}) collective-permute-start(bf16[512,2048]{1,0:T(8,128)(2,1)} %add_convert_fusion.11), channel_id=1, source_target_pairs={{0,24},{4,28},{8,16},{12,20},{16,8},{20,12},{24,0},{28,4},{1,25},{... | collective-permute-start | bytes 6291464 | tf_op jit(solution)/shard_map/ppermute | solution.py:103
  661.1 90.3 %all-gather.14.cloned.1.call-start = ((), (), s32[]{:S(2)}) async-start(), calls=%async_computation.13 | async-start | bytes 2621440 | tf_op jit(solution)/shard_map/all_gather | solution.py:206
  680.7 135.3 %collective-permute-start.41 = (bf16[512,2048]{1,0:T(8,128)(2,1)}, bf16[512,2048]{1,0:T(8,128)(2,1)}, u32[]{:S(2)}, u32[]{:S(2)}) collective-permute-start(bf16[512,2048]{1,0:T(8,128)(2,1)} %slice.378), channel_id=1, source_target_pairs={{0,4},{4,0},{8,12},{12,8},{16,20},{20,16},{24,28},{28,24},{1,5},{5... | collective-permute-start | bytes 6291464 | tf_op jit(solution)/shard_map/ppermute | solution.py:103
  687.0 132.9 %collective-permute-start.39 = (bf16[512,2048]{1,0:T(8,128)(2,1)}, bf16[512,2048]{1,0:T(8,128)(2,1)}, u32[]{:S(2)}, u32[]{:S(2)}) collective-permute-start(bf16[512,2048]{1,0:T(8,128)(2,1)} %slice.376), channel_id=1, source_target_pairs={{0,4},{4,0},{8,12},{12,8},{16,20},{20,16},{24,28},{28,24},{1,5},{5... | collective-permute-start | bytes 6291464 | tf_op jit(solution)/shard_map/ppermute | solution.py:103
  694.6 143.9 %collective-permute-start.38 = (bf16[512,2048]{1,0:T(8,128)(2,1)}, bf16[512,2048]{1,0:T(8,128)(2,1)}, u32[]{:S(2)}, u32[]{:S(2)}) collective-permute-start(bf16[512,2048]{1,0:T(8,128)(2,1)} %slice.374), channel_id=1, source_target_pairs={{0,4},{4,0},{8,12},{12,8},{16,20},{20,16},{24,28},{28,24},{1,5},{5... | collective-permute-start | bytes 6291464 | tf_op jit(solution)/shard_map/ppermute | solution.py:103
  697.4 141.7 %collective-permute-start.44 = (bf16[512,2048]{1,0:T(8,128)(2,1)}, bf16[512,2048]{1,0:T(8,128)(2,1)}, u32[]{:S(2)}, u32[]{:S(2)}) collective-permute-start(bf16[512,2048]{1,0:T(8,128)(2,1)} %add_convert_fusion.6), channel_id=1, source_target_pairs={{0,24},{4,28},{8,16},{12,20},{16,8},{20,12},{24,0},{28,4},{1,25},{... | collective-permute-start | bytes 6291464 | tf_op jit(solution)/shard_map/ppermute | solution.py:103
  798.9 98.3 %reduce-scatter.16.cloned.1.call-start = ((), (), s32[]{:S(2)}) async-start(), calls=%async_computation.15 | async-start | bytes 2785280
  815.9 116.9 %reduce-scatter.14.cloned.1.call-start = ((), (), s32[]{:S(2)}) async-start(), calls=%async_computation.14 | async-start | bytes 2621440 | tf_op jit(solution)/shard_map/reduce_scatter | solution.py:211
  838.5 52.5 %collective-permute-start.57 = (bf16[64,5376]{1,0:T(8,128)(2,1)}, bf16[64,5376]{1,0:T(8,128)(2,1)}, u32[]{:S(2)}, u32[]{:S(2)}) collective-permute-start(bf16[64,5376]{1,0:T(8,128)(2,1)} %get-tuple-element.302), channel_id=1, source_target_pairs={{0,4},{4,0},{8,12},{12,8},{16,20},{20,16},{24,28},{28,24},{1,5},{5... | collective-permute-start | bytes 2064392 | tf_op jit(solution)/shard_map/ppermute | solution.py:103
  838.5 52.5 %collective-permute-start.55 = (bf16[64,5376]{1,0:T(8,128)(2,1)}, bf16[64,5376]{1,0:T(8,128)(2,1)}, u32[]{:S(2)}, u32[]{:S(2)}) collective-permute-start(bf16[64,5376]{1,0:T(8,128)(2,1)} %get-tuple-element.303), channel_id=1, source_target_pairs={{0,4},{4,0},{8,12},{12,8},{16,20},{20,16},{24,28},{28,24},{1,5},{5... | collective-permute-start | bytes 2064392 | tf_op jit(solution)/shard_map/ppermute | solution.py:103
  839.0 52.0 %collective-permute-start.53 = (bf16[64,5376]{1,0:T(8,128)(2,1)S(1)}, bf16[64,5376]{1,0:T(8,128)(2,1)}, u32[]{:S(2)}, u32[]{:S(2)}) collective-permute-start(bf16[64,5376]{1,0:T(8,128)(2,1)S(1)} %get-tuple-element.304), channel_id=1, source_target_pairs={{0,4},{4,0},{8,12},{12,8},{16,20},{20,16},{24,28},{28,24},{1,5},{5... | collective-permute-start | bytes 2064392 | tf_op jit(solution)/shard_map/ppermute | solution.py:103
  891.0 116.8 %reduce-scatter.18.cloned.1.call-start = ((), (), s32[]{:S(2)}) async-start(), calls=%async_computation.16 | async-start | bytes 1392640
  895.6 84.2 %collective-permute-start.54 = (bf16[64,5376]{1,0:T(8,128)(2,1)}, bf16[64,5376]{1,0:T(8,128)(2,1)}, u32[]{:S(2)}, u32[]{:S(2)}) collective-permute-start(bf16[64,5376]{1,0:T(8,128)(2,1)} %get-tuple-element.300), channel_id=1, source_target_pairs={{0,8},{4,12},{8,0},{12,4},{16,24},{20,28},{24,16},{28,20},{1,9},{5... | collective-permute-start | bytes 2064392 | tf_op jit(solution)/shard_map/ppermute | solution.py:103
  936.0 67.0 %collective-permute-start.56 = (bf16[64,5376]{1,0:T(8,128)(2,1)}, bf16[64,5376]{1,0:T(8,128)(2,1)S(1)}, u32[]{:S(2)}, u32[]{:S(2)}) collective-permute-start(bf16[64,5376]{1,0:T(8,128)(2,1)} %get-tuple-element.299), channel_id=1, source_target_pairs={{0,16},{4,20},{8,24},{12,28},{16,0},{20,4},{24,8},{28,12},{1,17},{... | collective-permute-start | bytes 2064392 | tf_op jit(solution)/shard_map/ppermute | solution.py:103
  (193 other events, 2852.0 us)
Sparse Core Ops, SparseCore 0:
  11.6 31.7 all-gather.5
  67.8 45.9 all-gather.7
  147.9 46.7 all-gather.9
  214.8 41.8 reduce-scatter.9
  292.5 45.6 all-gather.11
  661.3 41.5 reduce-scatter.11
  706.6 44.8 all-gather.13
  816.1 43.4 reduce-scatter.15
  891.1 41.7 reduce-scatter.13
  979.9 25.4 reduce-scatter.17

commit v3 on v2

--- a/solution.py
+++ b/solution.py
@@ -158,15 +158,26 @@
     return lax.all_gather(block, "dp", axis=0, tiled=True)
 
 
-def gather_ordered(rows):
+def row_major(values):
+    return with_layout_constraint(values, Layout(major_to_minor=(0, 1)))
+
+
+def fetch_list(rows):
     if not four_chips():
-        return lax.all_gather(rows, "dp", axis=0, tiled=True)
+        return [lax.all_gather(rows, "dp", axis=0, tiled=True)]
+    chunks = fetch_chunks(rows)
+    return [chunks[m] for m in range(len(chunks))]
+
+
+def assemble(chunks):
+    if len(chunks) == 1:
+        return chunks[0]
     place = lax.axis_index("dp")
-    count = rows.shape[0]
-    whole = jnp.zeros((count * lax.axis_size("dp"), rows.shape[1]), rows.dtype)
-    for mask, chunk in fetch_chunks(rows).items():
+    count, width = chunks[0].shape
+    whole = jnp.zeros((count * len(chunks), width), chunks[0].dtype)
+    for mask, chunk in enumerate(chunks):
         whole = lax.dynamic_update_slice(whole, chunk, ((place ^ mask) * count, 0))
-    return with_layout_constraint(whole, Layout(major_to_minor=(0, 1)))
+    return row_major(whole)
 
 
 def reorder(values, axis):
@@ -184,13 +195,6 @@
     )
 
 
-def gather_reordered(rows):
-    if not four_chips():
-        return gather_plane(rows)
-    chunks = fetch_chunks(rows)
-    return jnp.concatenate([chunks[m] for m in range(len(chunks))], axis=0)
-
-
 def parts_of(rows):
     count = rows.shape[0] // lax.axis_size("dp")
 
@@ -233,6 +237,10 @@
     stacked = jnp.stack(grads).reshape(3, share, dp_count, rows).transpose(2, 0, 1, 3)
     got = exchange(stacked.reshape(dp_count, 3 * share, rows)).reshape(dp_count, 3, share, rows)
     return [g.T for g in got.transpose(1, 0, 2, 3).reshape(3, dp_count * share, rows)]
+
+
+def pad_rows(rows):
+    return jnp.pad(rows, ((0, -rows.shape[0] % 16), (0, 0)))
 
 
 def join_rows(experts_weight, shared_slice):
@@ -298,7 +306,7 @@
     upper = as_half(dense_weight)
     terms = jnp.concatenate([upper, as_half(dense_weight - as_single(upper))], axis=1)
     folds = [fold_rows(w, base) for w in (*denses, terms)]
-    folded = gather_ordered(jnp.concatenate(after(folds, packed_own), axis=1))
+    folded_chunks = fetch_list(jnp.concatenate(after(folds, packed_own), axis=1))
 
     def unfold_whole(index):
         part = folded[:, ends[index] : ends[index + 1]]
@@ -306,35 +314,46 @@
         part = part.reshape(dp_count, base, times[index], width).transpose(0, 2, 1, 3)
         return part.reshape(-1, width)
 
-    packed_line, folded = lax.optimization_barrier((packed_line, folded))
+    packed_line, folded_chunks = lax.optimization_barrier((packed_line, folded_chunks))
+    packed_chunks = fetch_list(row_major(packed_line))
+    folded = assemble(folded_chunks)
     up_q, up_kv, proj_out = (unfold_whole(i) for i in range(3))
     terms_all = folded[:, ends[3] :].reshape(dp_count, base, group_rows // base, 2, experts)
     mine_terms = lax.dynamic_slice_in_dim(terms_all, place * local_experts, local_experts, axis=4)
     mine_terms = as_single(mine_terms).transpose(0, 2, 1, 3, 4)
     weights_all = jnp.sum(mine_terms, axis=3).reshape(-1, local_experts)
-    packed = gather_reordered(packed_line)
     grad_line = gather_rows(after(as_half(out_grad), packed_line))
-    gains = as_single(packed[:, raw_width:]).T
-    gain_attn = gains[0]
-    gain_ffn, rank_gains = reorder(gains[1:], 1)
+    grad_sent = after(grad_line, packed_chunks)
+    shared_units = split_units(after([shared_gate, shared_up, shared_down], packed_chunks))
+    if four_chips():
+        grad_chunks = [grad_sent] + [swap(grad_sent, m) for m in CHIPS[1:]]
+
+    scale_in = rms_scale(block_input)
+    normed_in = reorder(block_input * scale_in, 1)
+    raw = None
+    hidden_pieces = []
+    gain_pieces = []
+    for i, chunk in enumerate(packed_chunks):
+        size = chunk.shape[0]
+        normed_piece = normed_in[:, i * size : (i + 1) * size]
+        chunk, normed_piece = lax.optimization_barrier((chunk, normed_piece))
+        piece_gains = as_single(chunk[:, raw_width:]).T
+        piece = as_half(normed_piece * piece_gains[0])
+        more = product(piece, chunk)
+        raw = more if raw is None else raw + more
+        hidden_pieces.append(piece)
+        gain_pieces.append(piece_gains)
+    late_gains = gain_pieces[0][1:]
+    if four_chips():
+        late_gains = jnp.zeros((2, model), jnp.float32)
+        for mask, piece_gains in enumerate(gain_pieces):
+            late_gains = lax.dynamic_update_slice(
+                late_gains, piece_gains[1:], (0, (place ^ mask) * piece_gains.shape[1])
+            )
+    gain_ffn, rank_gains = late_gains
     rank_gains = rank_gains.reshape(-1, shard)
     gain_query = rank_gains[:, :q_shard].reshape(-1)
     gain_key = rank_gains[:, q_shard:].reshape(-1)
-
-    sg, su, sd = split_units(after([shared_gate, shared_up, shared_down], packed))
-    grad_line = after(grad_line, sg)
-    cat_gate = join_rows(expert_gate, sg)
-    cat_up = join_rows(expert_up, su)
-    cat_down = join_rows(expert_down, sd)
-    if four_chips():
-        grad_chunks = [grad_line] + [swap(grad_line, m) for m in CHIPS[1:]]
-
-    column = jnp.arange(local_experts * expert_units + shared_gate.shape[1] // dp_count)[None, :]
-
-    scale_in = rms_scale(block_input)
-    normed_in = reorder(block_input * scale_in, 1)
-    hidden_in = as_half(normed_in * gain_attn)
-    raw = product(hidden_in, packed)
     query_raw = raw[:, :q_rank]
     scale_query = rms_scale(query_raw)
     normed_query = query_raw * scale_query
@@ -348,6 +367,9 @@
     rope_own = as_half(rotate(raw[:, q_rank + KVRANK : raw_width], cos_own, sin_own))
     latents_own = jnp.concatenate([query_latent, key_latent, rope_own], axis=1)
     latents = gather_rows(after(latents_own, grad_line))
+    hidden_in = jnp.concatenate(after(hidden_pieces, latents_own), axis=1)
+    packed = jnp.concatenate(after(packed_chunks, latents_own), axis=0)
+    gain_attn = jnp.concatenate([g[0] for g in after(gain_pieces, latents_own)])
     query_all = latents[:, :q_rank]
     key_all = latents[:, q_rank : q_rank + KVRANK]
     rope_all = latents[:, q_rank + KVRANK :]
@@ -369,6 +391,12 @@
     attended = as_half(mixed).reshape(group_rows, heads * VDIM)
     projected = against_rows(attended, proj_out)
     mid = block_input + scatter_rows(projected)
+    sg, su, sd = (pad_rows(w) for w in after(shared_units, projected))
+    cat_gate = join_rows(expert_gate, sg)
+    cat_up = join_rows(expert_up, su)
+    cat_down = join_rows(expert_down, sd)
+    cat_both = jnp.concatenate([cat_gate, cat_up], axis=0)
+    column = jnp.arange(cat_gate.shape[0])[None, :]
     scale_mid = rms_scale(mid)
     normed_mid = mid * scale_mid
     hidden_mid = as_half(normed_mid * gain_ffn)
@@ -389,8 +417,8 @@
         act = as_half(as_single(act) * factor)
         d_gate = as_half(d_act * up_val * sigma * (1.0 + gate_val * (1.0 - sigma)))
         d_up = as_half(d_act * gate_val * sigma)
-        back = product(d_gate, cat_gate)
-        back = as_half(back + product(d_up, cat_up))
+        back = product(jnp.concatenate([d_gate, d_up], axis=1), cat_both)
+        back = as_half(back)
         more = (hidden, grad, d_gate, d_up, act)
         return back, more
 
@@ -489,8 +517,9 @@
         grad_down = sum_over([contract_rows(a, g) for a, g in zip(late_acts, grad_blocks)])
         sums = (grad_gate, grad_up, grad_down)
     mid_all = after(mid_all, sums)
-    shared_sums = after([as_half(g[local_experts * expert_units :]) for g in sums], mid_all)
-    shared_grads = join_units(shared_sums)
+    first_shared = local_experts * expert_units
+    share = shared_units[0].shape[0]
+    shared_sums = [as_half(g[first_shared : first_shared + share]) for g in sums]
     grad_proj_out = contract_rows(mid_all, attended)
     d_attended = product(mid_all, proj_out)
     d_attended = as_half(d_attended).reshape(group_rows, heads, VDIM)
@@ -530,8 +559,9 @@
     d_latents_own = jnp.concatenate(
         [as_half(d_query_latent), as_half(d_key_latent), as_half(rope_key_grads)], axis=1
     )
-    d_latents_own, shared_grads = lax.optimization_barrier((d_latents_own, shared_grads))
+    shared_grads = join_units(after(shared_sums, d_latents_own))
     d_latents = scatter_rows(d_latents_own)
+    d_latents, shared_grads = lax.optimization_barrier((d_latents, shared_grads))
     sums = after(sums, d_latents_own)
     grad_gate, grad_up, grad_down = sums
 

time: 1030 us -> 1090 us (1.058)
  local copies, waits for them, and re-layouts: 185 us -> 250 us
  waiting for transfers between devices: 361 us -> 326 us
  other arithmetic: 101 us -> 121 us
    all_gather x5, waiting for transfers between devices: 57.9 us -> 36.1 us  [gather_rows(): return lax.all_gather(rows, 'tensor', axis=0, tiled=True)]
    optimization_barrier x1 -> x7, local copies, waits for them, and re-layouts: 0.09 us -> 14.4 us  [after(): return lax.optimization_barrier((value, before))[0]]
    dot_general x16 -> x19, matrix products: 101 us -> 87.8 us  [product(): return jnp.dot(left, right, preferred_element_type=jnp.float32)]
    ppermute x8 -> x2, local copies, waits for them, and re-layouts: 13.7 us -> 2.11 us  [swap(): return lax.ppermute(rows, 'dp', [(i, i ^ mask) for i in range(count)])]
    unnamed x344 -> x407, local copies, waits for them, and re-layouts: 63.2 us -> 74.4 us
    convert_element_type x22 -> x31, other arithmetic: 66.6 us -> 74.1 us  [as_half(): return values.astype(jnp.bfloat16)]
  transfers between devices with their start and end apart: 71 -> 71, of which waited for: 28 -> 27; matrix products, arithmetic and copies ran while one was open for 48% -> 55% of each run, Pallas kernels for 0% -> 0%
where the time goes in v3:
time: 1090 us; the launch traced here: 1080 us
  waiting for transfers between devices  326 us (30%)
  matrix products  308 us (28%)
  local copies, waits for them, and re-layouts  250 us (23%)
  other arithmetic  121 us (11%)
  starting transfers between devices  54.4 us (5%)
  between operations  17.4 us (2%)
    ppermute x59, waiting for transfers between devices, swap(): return lax.ppermute(rows, 'dp', [(i, i ^ mask) for i in range(count)])  284 us
    dot_general x16, matrix products, contract_rows(): lax.dot_general(left, right, (((0,), (0,)), ((), ())), preferred_element_...  98.9 us
    dot_general x19, matrix products, product(): return jnp.dot(left, right, preferred_element_type=jnp.float32)  87.8 us
    unnamed x407, local copies, waits for them, and re-layouts  74.4 us
    convert_element_type x31, other arithmetic, as_half(): return values.astype(jnp.bfloat16)  74.1 us
    dot_general x16, matrix products, against_rows(): lax.dot_general(left, right, (((1,), (1,)), ((), ())), preferred_element_...  73.4 us
    ppermute x59, starting transfers between devices, swap(): return lax.ppermute(rows, 'dp', [(i, i ^ mask) for i in range(count)])  45.1 us
    all_gather x5, waiting for transfers between devices, gather_rows(): return lax.all_gather(rows, 'tensor', axis=0, tiled=True)  36.1 us
  transfers between devices with their start and end apart: 71, of which 27 were waited for; matrix products, arithmetic and copies ran while one was open for 55% of the time, Pallas kernels for 0%

profile of v3, /device:TPU:0, one launch (start us, length us, event | category | flops | bytes accessed | tf_op | source)
XLA Modules:
  0.0 1076.9 jit_solution(841470872151655380)
XLA Ops:
  24.2 11.2 %collective-permute-done.1 = bf16[64,5632]{1,0:T(8,128)(2,1)} collective-permute-done((bf16[64,5632]{1,0:T(8,128)(2,1)}, bf16[64,5632]{1,0:T(8,128)(2,1)}, u32[]{:S(2)}, u32[]{:S(2)}) %collective-permute-start.1) | collective-permute-done | bytes 720928 | tf_op jit(solution)/shard_map/ppermute | solution.py:103
  73.6 17.1 %collective-permute-done.9 = bf16[256,2115]{0,1:T(8,128)(2,1)} collective-permute-done((bf16[256,2115]{0,1:T(8,128)(2,1)}, bf16[256,2115]{0,1:T(8,128)(2,1)}, u32[]{:S(2)}, u32[]{:S(2)}) %collective-permute-start.9) | collective-permute-done | bytes 1082912 | tf_op jit(solution)/shard_map/ppermute | solution.py:103
  215.9 12.0 %collective-permute-done.16 = bf16[512,2048]{1,0:T(8,128)(2,1)} collective-permute-done((bf16[512,2048]{1,0:T(8,128)(2,1)}, bf16[512,2048]{1,0:T(8,128)(2,1)}, u32[]{:S(2)}, u32[]{:S(2)}) %collective-permute-start.16) | collective-permute-done | bytes 2097184 | tf_op jit(solution)/shard_map/ppermute | solution.py:103
  228.0 44.7 %collective-permute-done.17 = bf16[512,2048]{1,0:T(8,128)(2,1)} collective-permute-done((bf16[512,2048]{1,0:T(8,128)(2,1)}, bf16[512,2048]{1,0:T(8,128)(2,1)}, u32[]{:S(2)}, u32[]{:S(2)}) %collective-permute-start.17) | collective-permute-done | bytes 2097184 | tf_op jit(solution)/shard_map/ppermute | solution.py:103
  357.5 13.9 %all-gather.12.cloned.1.call-done = bf16[512,2048]{1,0:T(8,128)(2,1)} async-done(((bf16[128,2048]{1,0:T(8,128)(2,1)}), bf16[512,2048]{1,0:T(8,128)(2,1)}) %all-gather.12.cloned.1.call-update) | async-done | bytes 2097168 | tf_op jit(solution)/shard_map/all_gather | solution.py:210
  414.6 12.1 %convolution_convert_fusion.3 = bf16[1024,2048]{1,0:T(8,128)(2,1)} fusion(bf16[1024,800]{0,1:T(8,128)(2,1)S(1)} %get-tuple-element.393, bf16[1024,800]{0,1:T(8,128)(2,1)} %get-tuple-element.391, bf16[96,2048]{1,0:T(8,128)(2,1)S(1)} %pad.16, bf16[704,2048]{1,0:T(8,128)(2,1)} %bitcast.369, bf16[96,2048]{1,0:T(8,128)(2,1)S(1)} %pad.15, ...), kind=kOutput, calls=%fused_computation.30 | convolution fusion | flops 6745751552 | bytes 14024704 | tf_op jit(solution)/shard_map/dot_general | solution.py:29
  426.7 12.9 %collective-permute-done.24 = bf16[512,2048]{1,0:T(8,128)(2,1)S(1)} collective-permute-done((bf16[512,2048]{1,0:T(8,128)(2,1)}, bf16[512,2048]{1,0:T(8,128)(2,1)S(1)}, u32[]{:S(2)}, u32[]{:S(2)}) %collective-permute-start.24) | collective-permute-done | bytes 2097184 | tf_op jit(solution)/shard_map/ppermute | solution.py:103
  463.2 9.8 convolution_convert_fusion.2
  483.0 21.7 %collective-permute-done.30 = bf16[256,2048]{1,0:T(8,128)(2,1)S(1)} collective-permute-done((bf16[256,2048]{1,0:T(8,128)(2,1)S(1)}, bf16[256,2048]{1,0:T(8,128)(2,1)S(1)}, u32[]{:S(2)}, u32[]{:S(2)}) %collective-permute-start.30) | collective-permute-done | bytes 1048608 | tf_op jit(solution)/shard_map/ppermute | solution.py:103
  526.7 10.4 convolution_convert_fusion.1
  577.6 11.2 %convolution_convert_fusion = bf16[1024,2048]{1,0:T(8,128)(2,1)S(1)} fusion(bf16[1024,800]{0,1:T(8,128)(2,1)S(1)} %get-tuple-element.384, bf16[1024,800]{0,1:T(8,128)(2,1)} %get-tuple-element.382, bf16[96,2048]{1,0:T(8,128)(2,1)S(1)} %copy-done.115, bf16[704,2048]{1,0:T(8,128)(2,1)} %bitcast.371, bf16[96,2048]{1,0:T(8,128)(2,1)S(1)} %copy-done.112, ...), kind=kOutput, calls=%fused_computation.27 | convolution fusion | flops 6745751552 | bytes 14024704 | tf_op jit(solution)/shard_map/dot_general | solution.py:29
  613.7 14.7 %add_add_fusion.2 = f32[800,2048]{1,0:T(8,128)} fusion(f32[800,2048]{1,0:T(8,128)} %fusion.162, f32[800,2048]{1,0:T(8,128)} %fusion.160, f32[800,2048]{1,0:T(8,128)} %fusion.161, bf16[1024,800]{0,1:T(8,128)(2,1)} %get-tuple-element.382, bf16[1024,2048]{1,0:T(8,128)(2,1)} %copy-done.69), kind=kOutput, calls=%fused_computation.6 | convolution fusion | flops 3360358400 | bytes 32047104 | tf_op jit(solution)/shard_map/dot_general | solution.py:33
  628.5 11.9 %add_add_fusion.1 = f32[800,2048]{1,0:T(8,128)} fusion(f32[800,2048]{1,0:T(8,128)} %fusion.165, f32[800,2048]{1,0:T(8,128)} %fusion.163, f32[800,2048]{1,0:T(8,128)} %fusion.164, bf16[1024,800]{0,1:T(8,128)(2,1)S(1)} %copy-done.59, bf16[1024,2048]{1,0:T(8,128)(2,1)} %copy-done.69), kind=kOutput, calls=%fused_computation.5 | convolution fusion | flops 3360358400 | bytes 32047104 | tf_op jit(solution)/shard_map/dot_general | solution.py:33
  640.4 52.1 %collective-permute-done.37 = bf16[512,2048]{1,0:T(8,128)(2,1)S(1)} collective-permute-done((bf16[512,2048]{1,0:T(8,128)(2,1)S(1)}, bf16[512,2048]{1,0:T(8,128)(2,1)S(1)}, u32[]{:S(2)}, u32[]{:S(2)}) %collective-permute-start.37) | collective-permute-done | bytes 2097184 | tf_op jit(solution)/shard_map/ppermute | solution.py:103
  692.5 10.7 collective-permute-done.35
  772.4 9.7 add_add_fusion
  782.1 17.6 %all-gather.14.cloned.1.call-done = bf16[512,2048]{1,0:T(8,128)(2,1)} async-done(((bf16[128,2048]{1,0:T(8,128)(2,1)}), bf16[512,2048]{1,0:T(8,128)(2,1)}) %all-gather.14.cloned.1.call-update) | async-done | bytes 2097168 | tf_op jit(solution)/shard_map/all_gather | solution.py:210
  806.1 8.9 fusion.44
  815.0 8.8 fusion.56
  839.4 9.2 fusion.52
  880.9 25.1 %collective-permute-done.42 = bf16[512,2048]{1,0:T(8,128)(2,1)S(1)} collective-permute-done((bf16[512,2048]{1,0:T(8,128)(2,1)S(1)}, bf16[512,2048]{1,0:T(8,128)(2,1)S(1)}, u32[]{:S(2)}, u32[]{:S(2)}) %collective-permute-start.42) | collective-permute-done | bytes 2097184 | tf_op jit(solution)/shard_map/ppermute | solution.py:103
  994.3 13.9 %collective-permute-done.51 = bf16[256,2115]{0,1:T(8,128)(2,1)} collective-permute-done((bf16[256,2115]{0,1:T(8,128)(2,1)}, bf16[256,2115]{0,1:T(8,128)(2,1)}, u32[]{:S(2)}, u32[]{:S(2)}) %collective-permute-start.51) | collective-permute-done | bytes 1082912 | tf_op jit(solution)/shard_map/ppermute | solution.py:103
  1009.6 21.8 %collective-permute-done.49 = bf16[256,2115]{0,1:T(8,128)(2,1)} collective-permute-done((bf16[256,2115]{0,1:T(8,128)(2,1)}, bf16[256,2115]{0,1:T(8,128)(2,1)}, u32[]{:S(2)}, u32[]{:S(2)}) %collective-permute-start.49) | collective-permute-done | bytes 1082912 | tf_op jit(solution)/shard_map/ppermute | solution.py:103
  1036.5 23.4 %collective-permute-done.56 = bf16[64,5376]{1,0:T(8,128)(2,1)S(1)} collective-permute-done((bf16[64,5376]{1,0:T(8,128)(2,1)}, bf16[64,5376]{1,0:T(8,128)(2,1)S(1)}, u32[]{:S(2)}, u32[]{:S(2)}) %collective-permute-start.56) | collective-permute-done | bytes 688160 | tf_op jit(solution)/shard_map/ppermute | solution.py:103
  (846 shorter events, 654.5 us)
Async XLA Ops:
  11.6 128.6 %all-gather.8.cloned.1.call-start = ((), (), s32[]{:S(2)}) async-start(), calls=%async_computation.8 | async-start | bytes 2621440 | tf_op jit(solution)/shard_map/all_gather | solution.py:210
  67.8 119.3 %all-gather.10.cloned.1.call-start = ((), (), s32[]{:S(2)}) async-start(), calls=%async_computation.9 | async-start | bytes 2703360 | tf_op jit(solution)/shard_map/all_gather | solution.py:210
  140.2 182.8 %reduce-scatter.10.cloned.1.call-start = ((), (), s32[]{:S(2)}) async-start(), calls=%async_computation.10 | async-start | bytes 2621440 | tf_op jit(solution)/shard_map/reduce_scatter | solution.py:215
  179.7 93.0 %collective-permute-start.17 = (bf16[512,2048]{1,0:T(8,128)(2,1)}, bf16[512,2048]{1,0:T(8,128)(2,1)}, u32[]{:S(2)}, u32[]{:S(2)}) collective-permute-start(bf16[512,2048]{1,0:T(8,128)(2,1)} %all-gather.8.cloned.1.call-done), channel_id=1, source_target_pairs={{0,16},{4,20},{8,24},{12,28},{16,0},{20,4},{24,8},{28,12},{1,17},{... | collective-permute-start | bytes 6291464 | tf_op jit(solution)/shard_map/ppermute | solution.py:103
  180.1 92.6 %collective-permute-start.18 = (bf16[512,2048]{1,0:T(8,128)(2,1)}, bf16[512,2048]{1,0:T(8,128)(2,1)}, u32[]{:S(2)}, u32[]{:S(2)}) collective-permute-start(bf16[512,2048]{1,0:T(8,128)(2,1)} %all-gather.8.cloned.1.call-done), channel_id=1, source_target_pairs={{0,24},{4,28},{8,16},{12,20},{16,8},{20,12},{24,0},{28,4},{1,25},{... | collective-permute-start | bytes 6291464 | tf_op jit(solution)/shard_map/ppermute | solution.py:103
  279.2 92.2 %all-gather.12.cloned.1.call-start = ((), (), s32[]{:S(2)}) async-start(), calls=%async_computation.11 | async-start | bytes 2621440 | tf_op jit(solution)/shard_map/all_gather | solution.py:210
  326.2 424.9 %reduce-scatter.12.cloned.1.call-start = ((), (), s32[]{:S(2)}) async-start(), calls=%async_computation.12 | async-start | bytes 2621440 | tf_op jit(solution)/shard_map/reduce_scatter | solution.py:215
  545.4 147.1 %collective-permute-start.33 = (bf16[512,2048]{1,0:T(8,128)(2,1)S(1)}, bf16[512,2048]{1,0:T(8,128)(2,1)}, u32[]{:S(2)}, u32[]{:S(2)}) collective-permute-start(bf16[512,2048]{1,0:T(8,128)(2,1)S(1)} %slice.500), channel_id=1, source_target_pairs={{0,4},{4,0},{8,12},{12,8},{16,20},{20,16},{24,28},{28,24},{1,5},{5... | collective-permute-start | bytes 6291464 | tf_op jit(solution)/shard_map/ppermute | solution.py:103
  598.5 93.9 %collective-permute-start.34 = (bf16[512,2048]{1,0:T(8,128)(2,1)S(1)}, bf16[512,2048]{1,0:T(8,128)(2,1)S(1)}, u32[]{:S(2)}, u32[]{:S(2)}) collective-permute-start(bf16[512,2048]{1,0:T(8,128)(2,1)S(1)} %add_convert_fusion.10), channel_id=1, source_target_pairs={{0,8},{4,12},{8,0},{12,4},{16,24},{20,28},{24,16},{28,20},{1,9},{5... | collective-permute-start | bytes 6291464 | tf_op jit(solution)/shard_map/ppermute | solution.py:103
  610.5 92.8 %collective-permute-start.35 = (bf16[512,2048]{1,0:T(8,128)(2,1)S(1)}, bf16[512,2048]{1,0:T(8,128)(2,1)}, u32[]{:S(2)}, u32[]{:S(2)}) collective-permute-start(bf16[512,2048]{1,0:T(8,128)(2,1)S(1)} %add_convert_fusion.9), channel_id=1, source_target_pairs={{0,16},{4,20},{8,24},{12,28},{16,0},{20,4},{24,8},{28,12},{1,17},{... | collective-permute-start | bytes 6291464 | tf_op jit(solution)/shard_map/ppermute | solution.py:103
  612.7 79.7 %collective-permute-start.37 = (bf16[512,2048]{1,0:T(8,128)(2,1)S(1)}, bf16[512,2048]{1,0:T(8,128)(2,1)S(1)}, u32[]{:S(2)}, u32[]{:S(2)}) collective-permute-start(bf16[512,2048]{1,0:T(8,128)(2,1)S(1)} %add_convert_fusion.7), channel_id=1, source_target_pairs={{0,24},{4,28},{8,16},{12,20},{16,8},{20,12},{24,0},{28,4},{1,25},{... | collective-permute-start | bytes 6291464 | tf_op jit(solution)/shard_map/ppermute | solution.py:103
  709.1 90.7 %all-gather.14.cloned.1.call-start = ((), (), s32[]{:S(2)}) async-start(), calls=%async_computation.13 | async-start | bytes 2621440 | tf_op jit(solution)/shard_map/all_gather | solution.py:210
  730.7 124.7 %collective-permute-start.41 = (bf16[512,2048]{1,0:T(8,128)(2,1)}, bf16[512,2048]{1,0:T(8,128)(2,1)}, u32[]{:S(2)}, u32[]{:S(2)}) collective-permute-start(bf16[512,2048]{1,0:T(8,128)(2,1)} %slice.508), channel_id=1, source_target_pairs={{0,4},{4,0},{8,12},{12,8},{16,20},{20,16},{24,28},{28,24},{1,5},{5... | collective-permute-start | bytes 6291464 | tf_op jit(solution)/shard_map/ppermute | solution.py:103
  737.0 123.2 %collective-permute-start.39 = (bf16[512,2048]{1,0:T(8,128)(2,1)}, bf16[512,2048]{1,0:T(8,128)(2,1)}, u32[]{:S(2)}, u32[]{:S(2)}) collective-permute-start(bf16[512,2048]{1,0:T(8,128)(2,1)} %slice.506), channel_id=1, source_target_pairs={{0,4},{4,0},{8,12},{12,8},{16,20},{20,16},{24,28},{28,24},{1,5},{5... | collective-permute-start | bytes 6291464 | tf_op jit(solution)/shard_map/ppermute | solution.py:103
  744.6 135.7 %collective-permute-start.38 = (bf16[512,2048]{1,0:T(8,128)(2,1)}, bf16[512,2048]{1,0:T(8,128)(2,1)}, u32[]{:S(2)}, u32[]{:S(2)}) collective-permute-start(bf16[512,2048]{1,0:T(8,128)(2,1)} %slice.504), channel_id=1, source_target_pairs={{0,4},{4,0},{8,12},{12,8},{16,20},{20,16},{24,28},{28,24},{1,5},{5... | collective-permute-start | bytes 6291464 | tf_op jit(solution)/shard_map/ppermute | solution.py:103
  747.3 133.5 %collective-permute-start.44 = (bf16[512,2048]{1,0:T(8,128)(2,1)}, bf16[512,2048]{1,0:T(8,128)(2,1)}, u32[]{:S(2)}, u32[]{:S(2)}) collective-permute-start(bf16[512,2048]{1,0:T(8,128)(2,1)} %add_convert_fusion.2), channel_id=1, source_target_pairs={{0,24},{4,28},{8,16},{12,20},{16,8},{20,12},{24,0},{28,4},{1,25},{... | collective-permute-start | bytes 6291464 | tf_op jit(solution)/shard_map/ppermute | solution.py:103
  754.7 190.8 %reduce-scatter.16.cloned.1.call-start = ((), (), s32[]{:S(2)}) async-start(), calls=%async_computation.15 | async-start | bytes 2785280
  880.3 56.7 %collective-permute-start.57 = (bf16[64,5376]{1,0:T(8,128)(2,1)}, bf16[64,5376]{1,0:T(8,128)(2,1)}, u32[]{:S(2)}, u32[]{:S(2)}) collective-permute-start(bf16[64,5376]{1,0:T(8,128)(2,1)} %get-tuple-element.398), channel_id=1, source_target_pairs={{0,4},{4,0},{8,12},{12,8},{16,20},{20,16},{24,28},{28,24},{1,5},{5... | collective-permute-start | bytes 2064392 | tf_op jit(solution)/shard_map/ppermute | solution.py:103
  880.3 56.7 %collective-permute-start.55 = (bf16[64,5376]{1,0:T(8,128)(2,1)}, bf16[64,5376]{1,0:T(8,128)(2,1)}, u32[]{:S(2)}, u32[]{:S(2)}) collective-permute-start(bf16[64,5376]{1,0:T(8,128)(2,1)} %get-tuple-element.399), channel_id=1, source_target_pairs={{0,4},{4,0},{8,12},{12,8},{16,20},{20,16},{24,28},{28,24},{1,5},{5... | collective-permute-start | bytes 2064392 | tf_op jit(solution)/shard_map/ppermute | solution.py:103
  880.8 56.2 %collective-permute-start.53 = (bf16[64,5376]{1,0:T(8,128)(2,1)}, bf16[64,5376]{1,0:T(8,128)(2,1)}, u32[]{:S(2)}, u32[]{:S(2)}) collective-permute-start(bf16[64,5376]{1,0:T(8,128)(2,1)} %get-tuple-element.400), channel_id=1, source_target_pairs={{0,4},{4,0},{8,12},{12,8},{16,20},{20,16},{24,28},{28,24},{1,5},{5... | collective-permute-start | bytes 2064392 | tf_op jit(solution)/shard_map/ppermute | solution.py:103
  921.8 67.8 %reduce-scatter.14.cloned.1.call-start = ((), (), s32[]{:S(2)}) async-start(), calls=%async_computation.14 | async-start | bytes 2621440 | tf_op jit(solution)/shard_map/reduce_scatter | solution.py:215
  936.9 127.9 %reduce-scatter.18.cloned.1.call-start = ((), (), s32[]{:S(2)}) async-start(), calls=%async_computation.16 | async-start | bytes 1392640
  941.5 95.0 %collective-permute-start.54 = (bf16[64,5376]{1,0:T(8,128)(2,1)}, bf16[64,5376]{1,0:T(8,128)(2,1)}, u32[]{:S(2)}, u32[]{:S(2)}) collective-permute-start(bf16[64,5376]{1,0:T(8,128)(2,1)} %get-tuple-element.396), channel_id=1, source_target_pairs={{0,8},{4,12},{8,0},{12,4},{16,24},{20,28},{24,16},{28,20},{1,9},{5... | collective-permute-start | bytes 2064392 | tf_op jit(solution)/shard_map/ppermute | solution.py:103
  992.8 67.1 %collective-permute-start.56 = (bf16[64,5376]{1,0:T(8,128)(2,1)}, bf16[64,5376]{1,0:T(8,128)(2,1)S(1)}, u32[]{:S(2)}, u32[]{:S(2)}) collective-permute-start(bf16[64,5376]{1,0:T(8,128)(2,1)} %get-tuple-element.395), channel_id=1, source_target_pairs={{0,16},{4,20},{8,24},{12,28},{16,0},{20,4},{24,8},{28,12},{1,17},{... | collective-permute-start | bytes 2064392 | tf_op jit(solution)/shard_map/ppermute | solution.py:103
  (227 other events, 2882.1 us)
Sparse Core Ops, SparseCore 0:
  11.7 31.8 all-gather.5
  68.0 45.9 all-gather.7
  140.3 46.7 all-gather.9
  216.1 41.8 reduce-scatter.9
  326.3 45.0 all-gather.11
  709.2 41.8 reduce-scatter.11
  754.9 44.8 all-gather.13
  855.5 44.4 reduce-scatter.15
  937.0 42.6 reduce-scatter.13
  1036.6 26.1 reduce-scatter.17

commit v4 on v3

--- a/solution.py
+++ b/solution.py
@@ -390,7 +390,11 @@
     mixed = jnp.einsum("hqk,khd->qhd", probs, values, preferred_element_type=jnp.float32)
     attended = as_half(mixed).reshape(group_rows, heads * VDIM)
     projected = against_rows(attended, proj_out)
-    mid = block_input + scatter_rows(projected)
+    mid_sum = scatter_rows(projected)
+    mid_sum, packed, gain_attn, hidden_in = lax.optimization_barrier(
+        (mid_sum, packed, gain_attn, hidden_in)
+    )
+    mid = block_input + mid_sum
     sg, su, sd = (pad_rows(w) for w in after(shared_units, projected))
     cat_gate = join_rows(expert_gate, sg)
     cat_up = join_rows(expert_up, su)
@@ -499,12 +503,15 @@
         back_sum = jnp.concatenate(backs, axis=0)
     d_hidden_mid = scatter_rows(back_sum)
 
+    if four_chips():
+        out_products = [as_half(product(act, cat_down)) for act in after(act_blocks, back_sum)]
+        d_hidden_mid, out_products = lax.optimization_barrier((d_hidden_mid, out_products))
     grad_gain_ffn = jnp.sum(d_hidden_mid * normed_mid, axis=0)
     d_mid = out_grad + norm_back(d_hidden_mid, normed_mid, scale_mid, gain_ffn)
     mid_low = as_half(d_mid)
     act_blocks = after(act_blocks, back_sum)
     if four_chips():
-        out_parts = [pair_sum(as_half(product(act, cat_down))) for act in act_blocks]
+        out_parts = [pair_sum(out) for out in out_products]
     else:
         for act in act_blocks:
             if out_parts:

time: 1090 us -> 1080 us (level)
  waiting for transfers between devices: 326 us -> 388 us
  local copies, waits for them, and re-layouts: 250 us -> 203 us
  other arithmetic: 121 us -> 81.7 us
  matrix products: 308 us -> 332 us
    all_to_all x2, waiting for transfers between devices: 4.04 us -> 70.9 us  [exchange(): return lax.all_to_all(block, 'dp', split_axis=0, concat_axis=0, tiled=True)]
    ppermute x59, waiting for transfers between devices: 284 us -> 246 us  [swap(): return lax.ppermute(rows, 'dp', [(i, i ^ mask) for i in range(count)])]
    convert_element_type x31 -> x27, other arithmetic: 74.1 us -> 44.3 us  [as_half(): return values.astype(jnp.bfloat16)]
    dot_general x16, matrix products: 73.4 us -> 94.1 us  [against_rows(): lax.dot_general(left, right, (((1,), (1,)), ((), ())), preferred_element_...]
    all_gather x5, waiting for transfers between devices: 36.1 us -> 53.2 us  [gather_rows(): return lax.all_gather(rows, 'tensor', axis=0, tiled=True)]
    reduce_scatter x3, waiting for transfers between devices: 1.79 us -> 17.3 us  [scatter_rows(): lax.psum_scatter(as_half(rows), 'tensor', scatter_dimension=0, tiled=True)]
    unnamed x407 -> x373, local copies, waits for them, and re-layouts: 74.4 us -> 71.6 us
  transfers between devices with their start and end apart: 71 -> 71, of which waited for: 27 -> 23; matrix products, arithmetic and copies ran while one was open for 55% -> 48% of each run, Pallas kernels for 0% -> 0%
where the time goes in v4:
time: 1080 us; the launch traced here: 1070 us
  waiting for transfers between devices  388 us (36%)
  matrix products  332 us (31%)
  local copies, waits for them, and re-layouts  203 us (19%)
  other arithmetic  81.7 us (8%)
  starting transfers between devices  51.9 us (5%)
  between operations  17 us (2%)
    ppermute x59, waiting for transfers between devices, swap(): return lax.ppermute(rows, 'dp', [(i, i ^ mask) for i in range(count)])  246 us
    dot_general x16, matrix products, contract_rows(): lax.dot_general(left, right, (((0,), (0,)), ((), ())), preferred_element_...  102 us
    dot_general x19, matrix products, product(): return jnp.dot(left, right, preferred_element_type=jnp.float32)  95.1 us
    dot_general x16, matrix products, against_rows(): lax.dot_general(left, right, (((1,), (1,)), ((), ())), preferred_element_...  94.1 us
    unnamed x373, local copies, waits for them, and re-layouts  71.6 us
    all_to_all x2, waiting for transfers between devices, exchange(): return lax.all_to_all(block, 'dp', split_axis=0, concat_axis=0, tiled=True)  70.9 us
    all_gather x5, waiting for transfers between devices, gather_rows(): return lax.all_gather(rows, 'tensor', axis=0, tiled=True)  53.2 us
    convert_element_type x27, other arithmetic, as_half(): return values.astype(jnp.bfloat16)  44.3 us
  transfers between devices with their start and end apart: 71, of which 23 were waited for; matrix products, arithmetic and copies ran while one was open for 48% of the time, Pallas kernels for 0%

profile of v4, /device:TPU:0, one launch (start us, length us, event | category | flops | bytes accessed | tf_op | source)
XLA Modules:
  0.0 1073.8 jit_solution(14839578092651906250)
XLA Ops:
  22.2 13.2 %collective-permute-done.1 = bf16[64,5632]{1,0:T(8,128)(2,1)} collective-permute-done((bf16[64,5632]{1,0:T(8,128)(2,1)}, bf16[64,5632]{1,0:T(8,128)(2,1)}, u32[]{:S(2)}, u32[]{:S(2)}) %collective-permute-start.1) | collective-permute-done | bytes 720928 | tf_op jit(solution)/shard_map/ppermute | solution.py:103
  101.3 9.6 collective-permute-done.14
  187.3 29.6 %all-gather.10.cloned.1.call-done = bf16[512,2112]{0,1:T(8,128)(2,1)} async-done(((bf16[128,2112]{0,1:T(8,128)(2,1)}), bf16[512,2112]{0,1:T(8,128)(2,1)}) %all-gather.10.cloned.1.call-update) | async-done | bytes 2162704 | tf_op jit(solution)/shard_map/all_gather | solution.py:210
  237.6 40.7 %collective-permute-done.17 = bf16[512,2048]{1,0:T(8,128)(2,1)} collective-permute-done((bf16[512,2048]{1,0:T(8,128)(2,1)}, bf16[512,2048]{1,0:T(8,128)(2,1)}, u32[]{:S(2)}, u32[]{:S(2)}) %collective-permute-start.17) | collective-permute-done | bytes 2097184 | tf_op jit(solution)/shard_map/ppermute | solution.py:103
  331.6 19.1 %all-gather.12.cloned.1.call-done = bf16[512,2048]{1,0:T(8,128)(2,1)} async-done(((bf16[128,2048]{1,0:T(8,128)(2,1)}), bf16[512,2048]{1,0:T(8,128)(2,1)}) %all-gather.12.cloned.1.call-update) | async-done | bytes 2097168 | tf_op jit(solution)/shard_map/all_gather | solution.py:210
  360.5 9.3 multiply_convert_fusion.7
  369.8 10.5 convolution_convert_fusion.3
  380.3 18.9 %collective-permute-done.25 = bf16[512,2048]{1,0:T(8,128)(2,1)S(1)} collective-permute-done((bf16[512,2048]{1,0:T(8,128)(2,1)}, bf16[512,2048]{1,0:T(8,128)(2,1)S(1)}, u32[]{:S(2)}, u32[]{:S(2)}) %collective-permute-start.25) | collective-permute-done | bytes 2097184 | tf_op jit(solution)/shard_map/ppermute | solution.py:103
  410.0 9.1 multiply_convert_fusion.5
  419.2 10.7 convolution_convert_fusion.2
  432.6 23.1 %collective-permute-done.34 = bf16[256,2048]{1,0:T(8,128)(2,1)S(1)} collective-permute-done((bf16[256,2048]{1,0:T(8,128)(2,1)S(1)}, bf16[256,2048]{1,0:T(8,128)(2,1)S(1)}, u32[]{:S(2)}, u32[]{:S(2)}) %collective-permute-start.34) | collective-permute-done | bytes 1048608 | tf_op jit(solution)/shard_map/ppermute | solution.py:103
  475.3 11.1 %convolution_convert_fusion.1 = bf16[1024,2048]{1,0:T(8,128)(2,1)S(1)} fusion(bf16[1024,800]{0,1:T(8,128)(2,1)S(1)} %get-tuple-element.407, bf16[1024,800]{0,1:T(8,128)(2,1)} %get-tuple-element.406, bf16[96,2048]{1,0:T(8,128)(2,1)S(1)} %pad.16, bf16[704,2048]{1,0:T(8,128)(2,1)} %bitcast.371, bf16[96,2048]{1,0:T(8,128)(2,1)S(1)} %pad.15, ...), kind=kOutput, calls=%fused_computation.28 | convolution fusion | flops 6745751552 | bytes 14024704 | tf_op jit(solution)/shard_map/dot_general | solution.py:29
  525.4 11.2 %convolution_convert_fusion = bf16[1024,2048]{1,0:T(8,128)(2,1)S(1)} fusion(bf16[1024,800]{0,1:T(8,128)(2,1)S(1)} %get-tuple-element.404, bf16[1024,800]{0,1:T(8,128)(2,1)} %get-tuple-element.403, bf16[96,2048]{1,0:T(8,128)(2,1)S(1)} %pad.16, bf16[704,2048]{1,0:T(8,128)(2,1)} %bitcast.372, bf16[96,2048]{1,0:T(8,128)(2,1)S(1)} %pad.15, ...), kind=kOutput, calls=%fused_computation.27 | convolution fusion | flops 6745751552 | bytes 14024704 | tf_op jit(solution)/shard_map/dot_general | solution.py:29
  562.0 15.0 %add_add_fusion.2 = f32[800,2048]{1,0:T(8,128)} fusion(f32[800,2048]{1,0:T(8,128)} %fusion.155, f32[800,2048]{1,0:T(8,128)} %fusion.153, f32[800,2048]{1,0:T(8,128)} %fusion.154, bf16[1024,800]{0,1:T(8,128)(2,1)} %get-tuple-element.403, bf16[1024,2048]{1,0:T(8,128)(2,1)} %copy-done.52), kind=kOutput, calls=%fused_computation.6 | convolution fusion | flops 3360358400 | bytes 32047104 | tf_op jit(solution)/shard_map/dot_general | solution.py:33
  577.0 10.9 %add_add_fusion.1 = f32[800,2048]{1,0:T(8,128)} fusion(f32[800,2048]{1,0:T(8,128)} %fusion.158, f32[800,2048]{1,0:T(8,128)} %fusion.156, f32[800,2048]{1,0:T(8,128)} %fusion.157, bf16[1024,800]{0,1:T(8,128)(2,1)} %copy-done.142, bf16[1024,2048]{1,0:T(8,128)(2,1)S(1)} %copy-done.53), kind=kOutput, calls=%fused_computation.5 | convolution fusion | flops 3360358400 | bytes 32047104 | tf_op jit(solution)/shard_map/dot_general | solution.py:33
  587.9 52.4 %collective-permute-done.37 = bf16[512,2048]{1,0:T(8,128)(2,1)S(1)} collective-permute-done((bf16[512,2048]{1,0:T(8,128)(2,1)S(1)}, bf16[512,2048]{1,0:T(8,128)(2,1)S(1)}, u32[]{:S(2)}, u32[]{:S(2)}) %collective-permute-start.37) | collective-permute-done | bytes 2097184 | tf_op jit(solution)/shard_map/ppermute | solution.py:103
  640.4 11.5 %collective-permute-done.32 = bf16[512,2048]{1,0:T(8,128)(2,1)} collective-permute-done((bf16[512,2048]{1,0:T(8,128)(2,1)S(1)}, bf16[512,2048]{1,0:T(8,128)(2,1)}, u32[]{:S(2)}, u32[]{:S(2)}) %collective-permute-start.32) | collective-permute-done | bytes 2097184 | tf_op jit(solution)/shard_map/ppermute | solution.py:103
  684.8 14.7 %reduce-scatter.12.cloned.1.call-done = bf16[128,2048]{1,0:T(8,128)(2,1)} async-done(((bf16[512,2048]{1,0:T(8,128)(2,1)}), bf16[128,2048]{1,0:T(8,128)(2,1)}) %reduce-scatter.12.cloned.1.call-update) | async-done | bytes 524304 | tf_op jit(solution)/shard_map/reduce_scatter | solution.py:215
  728.7 12.2 %add_add_fusion = f32[800,2048]{1,0:T(8,128)} fusion(f32[800,2048]{1,0:T(8,128)} %fusion.161, f32[800,2048]{1,0:T(8,128)} %fusion.159, f32[800,2048]{1,0:T(8,128)} %fusion.160, bf16[1024,800]{0,1:T(8,128)(2,1)S(1)} %copy-done.141, bf16[1024,2048]{1,0:T(8,128)(2,1)} %constant_dynamic-update-slice_fusion.25), kind=kOutput, calls=%fused_computation.4 | convolution fusion | flops 3360358400 | bytes 32047104 | tf_op jit(solution)/shard_map/dot_general | solution.py:33
  789.2 9.0 fusion.54
  862.4 70.9 %all-to-all-done.1 = bf16[8,264,256]{2,1,0:T(8,128)(2,1)S(1)} async-done(((bf16[8,264,256]{2,1,0:T(8,128)(2,1)}), bf16[8,264,256]{2,1,0:T(8,128)(2,1)S(1)}, u32[]{:S(2)}, u32[]{:S(2)}) %all-to-all-start.1) | async-done | bytes 1081376 | tf_op jit(solution)/shard_map/all_to_all | solution.py:220
  987.5 17.2 %collective-permute-done.51 = bf16[256,2115]{0,1:T(8,128)(2,1)} collective-permute-done((bf16[256,2115]{0,1:T(8,128)(2,1)}, bf16[256,2115]{0,1:T(8,128)(2,1)}, u32[]{:S(2)}, u32[]{:S(2)}) %collective-permute-start.51) | collective-permute-done | bytes 1082912 | tf_op jit(solution)/shard_map/ppermute | solution.py:103
  1006.2 21.8 %collective-permute-done.49 = bf16[256,2115]{0,1:T(8,128)(2,1)} collective-permute-done((bf16[256,2115]{0,1:T(8,128)(2,1)}, bf16[256,2115]{0,1:T(8,128)(2,1)}, u32[]{:S(2)}, u32[]{:S(2)}) %collective-permute-start.49) | collective-permute-done | bytes 1082912 | tf_op jit(solution)/shard_map/ppermute | solution.py:103
  1033.1 23.5 %collective-permute-done.56 = bf16[64,5376]{1,0:T(8,128)(2,1)} collective-permute-done((bf16[64,5376]{1,0:T(8,128)(2,1)}, bf16[64,5376]{1,0:T(8,128)(2,1)}, u32[]{:S(2)}, u32[]{:S(2)}) %collective-permute-start.56) | collective-permute-done | bytes 688160 | tf_op jit(solution)/shard_map/ppermute | solution.py:103
  (804 shorter events, 581.7 us)
Async XLA Ops:
  11.6 154.5 %all-gather.8.cloned.1.call-start = ((), (), s32[]{:S(2)}) async-start(), calls=%async_computation.8 | async-start | bytes 2621440 | tf_op jit(solution)/shard_map/all_gather | solution.py:210
  160.7 119.6 %all-to-all-start = ((bf16[8,264,256]{2,1,0:T(8,128)(2,1)}), bf16[8,264,256]{2,1,0:T(8,128)(2,1)}, u32[]{:S(2)}, u32[]{:S(2)}) async-start(bf16[8,264,256]{2,1,0:T(8,128)(2,1)} %bitcast.286), calls=%async_computation.1 | async-start | bytes 2162688 | tf_op jit(solution)/shard_map/all_to_all | solution.py:220
  166.1 135.2 %reduce-scatter.10.cloned.1.call-start = ((), (), s32[]{:S(2)}) async-start(), calls=%async_computation.10 | async-start | bytes 2621440 | tf_op jit(solution)/shard_map/reduce_scatter | solution.py:215
  185.7 92.6 %collective-permute-start.17 = (bf16[512,2048]{1,0:T(8,128)(2,1)}, bf16[512,2048]{1,0:T(8,128)(2,1)}, u32[]{:S(2)}, u32[]{:S(2)}) collective-permute-start(bf16[512,2048]{1,0:T(8,128)(2,1)} %all-gather.8.cloned.1.call-done), channel_id=1, source_target_pairs={{0,16},{4,20},{8,24},{12,28},{16,0},{20,4},{24,8},{28,12},{1,17},{... | collective-permute-start | bytes 6291464 | tf_op jit(solution)/shard_map/ppermute | solution.py:103
  187.1 91.1 %collective-permute-start.18 = (bf16[512,2048]{1,0:T(8,128)(2,1)}, bf16[512,2048]{1,0:T(8,128)(2,1)}, u32[]{:S(2)}, u32[]{:S(2)}) collective-permute-start(bf16[512,2048]{1,0:T(8,128)(2,1)} %all-gather.8.cloned.1.call-done), channel_id=1, source_target_pairs={{0,24},{4,28},{8,16},{12,20},{16,8},{20,12},{24,0},{28,4},{1,25},{... | collective-permute-start | bytes 6291464 | tf_op jit(solution)/shard_map/ppermute | solution.py:103
  233.5 117.2 %all-gather.12.cloned.1.call-start = ((), (), s32[]{:S(2)}) async-start(), calls=%async_computation.11 | async-start | bytes 2621440 | tf_op jit(solution)/shard_map/all_gather | solution.py:210
  304.6 394.9 %reduce-scatter.12.cloned.1.call-start = ((), (), s32[]{:S(2)}) async-start(), calls=%async_computation.12 | async-start | bytes 2621440 | tf_op jit(solution)/shard_map/reduce_scatter | solution.py:215
  494.5 145.9 %collective-permute-start.24 = (bf16[512,2048]{1,0:T(8,128)(2,1)S(1)}, bf16[512,2048]{1,0:T(8,128)(2,1)}, u32[]{:S(2)}, u32[]{:S(2)}) collective-permute-start(bf16[512,2048]{1,0:T(8,128)(2,1)S(1)} %slice.496), channel_id=1, source_target_pairs={{0,4},{4,0},{8,12},{12,8},{16,20},{20,16},{24,28},{28,24},{1,5},{5... | collective-permute-start | bytes 6291464 | tf_op jit(solution)/shard_map/ppermute | solution.py:103
  546.4 94.0 %collective-permute-start.29 = (bf16[512,2048]{1,0:T(8,128)(2,1)S(1)}, bf16[512,2048]{1,0:T(8,128)(2,1)S(1)}, u32[]{:S(2)}, u32[]{:S(2)}) collective-permute-start(bf16[512,2048]{1,0:T(8,128)(2,1)S(1)} %add_convert_fusion.9), channel_id=1, source_target_pairs={{0,8},{4,12},{8,0},{12,4},{16,24},{20,28},{24,16},{28,20},{1,9},{5... | collective-permute-start | bytes 6291464 | tf_op jit(solution)/shard_map/ppermute | solution.py:103
  559.1 92.8 %collective-permute-start.32 = (bf16[512,2048]{1,0:T(8,128)(2,1)S(1)}, bf16[512,2048]{1,0:T(8,128)(2,1)}, u32[]{:S(2)}, u32[]{:S(2)}) collective-permute-start(bf16[512,2048]{1,0:T(8,128)(2,1)S(1)} %add_convert_fusion.8), channel_id=1, source_target_pairs={{0,16},{4,20},{8,24},{12,28},{16,0},{20,4},{24,8},{28,12},{1,17},{... | collective-permute-start | bytes 6291464 | tf_op jit(solution)/shard_map/ppermute | solution.py:103
  561.4 79.0 %collective-permute-start.37 = (bf16[512,2048]{1,0:T(8,128)(2,1)S(1)}, bf16[512,2048]{1,0:T(8,128)(2,1)S(1)}, u32[]{:S(2)}, u32[]{:S(2)}) collective-permute-start(bf16[512,2048]{1,0:T(8,128)(2,1)S(1)} %add_convert_fusion.7), channel_id=1, source_target_pairs={{0,24},{4,28},{8,16},{12,20},{16,8},{20,12},{24,0},{28,4},{1,25},{... | collective-permute-start | bytes 6291464 | tf_op jit(solution)/shard_map/ppermute | solution.py:103
  657.8 89.7 %all-gather.14.cloned.1.call-start = ((), (), s32[]{:S(2)}) async-start(), calls=%async_computation.13 | async-start | bytes 2621440 | tf_op jit(solution)/shard_map/all_gather | solution.py:210
  702.5 239.9 %reduce-scatter.16.cloned.1.call-start = ((), (), s32[]{:S(2)}) async-start(), calls=%async_computation.15 | async-start | bytes 2785280
  707.9 110.0 %collective-permute-start.41 = (bf16[512,2048]{1,0:T(8,128)(2,1)}, bf16[512,2048]{1,0:T(8,128)(2,1)}, u32[]{:S(2)}, u32[]{:S(2)}) collective-permute-start(bf16[512,2048]{1,0:T(8,128)(2,1)} %slice.425), channel_id=1, source_target_pairs={{0,4},{4,0},{8,12},{12,8},{16,20},{20,16},{24,28},{28,24},{1,5},{5... | collective-permute-start | bytes 6291464 | tf_op jit(solution)/shard_map/ppermute | solution.py:103
  709.8 113.6 %collective-permute-start.39 = (bf16[512,2048]{1,0:T(8,128)(2,1)}, bf16[512,2048]{1,0:T(8,128)(2,1)}, u32[]{:S(2)}, u32[]{:S(2)}) collective-permute-start(bf16[512,2048]{1,0:T(8,128)(2,1)} %slice.423), channel_id=1, source_target_pairs={{0,4},{4,0},{8,12},{12,8},{16,20},{20,16},{24,28},{28,24},{1,5},{5... | collective-permute-start | bytes 6291464 | tf_op jit(solution)/shard_map/ppermute | solution.py:103
  711.4 222.8 %collective-permute-start.38 = (bf16[512,2048]{1,0:T(8,128)(2,1)}, bf16[512,2048]{1,0:T(8,128)(2,1)}, u32[]{:S(2)}, u32[]{:S(2)}) collective-permute-start(bf16[512,2048]{1,0:T(8,128)(2,1)} %slice.421), channel_id=1, source_target_pairs={{0,4},{4,0},{8,12},{12,8},{16,20},{20,16},{24,28},{28,24},{1,5},{5... | collective-permute-start | bytes 6291464 | tf_op jit(solution)/shard_map/ppermute | solution.py:103
  827.0 107.2 %collective-permute-start.44 = (bf16[512,2048]{1,0:T(8,128)(2,1)}, bf16[512,2048]{1,0:T(8,128)(2,1)}, u32[]{:S(2)}, u32[]{:S(2)}) collective-permute-start(bf16[512,2048]{1,0:T(8,128)(2,1)} %add_convert_fusion.2), channel_id=1, source_target_pairs={{0,24},{4,28},{8,16},{12,20},{16,8},{20,12},{24,0},{28,4},{1,25},{... | collective-permute-start | bytes 6291464 | tf_op jit(solution)/shard_map/ppermute | solution.py:103
  829.4 104.8 %collective-permute-start.42 = (bf16[512,2048]{1,0:T(8,128)(2,1)}, bf16[512,2048]{1,0:T(8,128)(2,1)}, u32[]{:S(2)}, u32[]{:S(2)}) collective-permute-start(bf16[512,2048]{1,0:T(8,128)(2,1)} %add_convert_fusion.3), channel_id=1, source_target_pairs={{0,16},{4,20},{8,24},{12,28},{16,0},{20,4},{24,8},{28,12},{1,17},{... | collective-permute-start | bytes 6291464 | tf_op jit(solution)/shard_map/ppermute | solution.py:103
  829.9 104.2 %collective-permute-start.40 = (bf16[512,2048]{1,0:T(8,128)(2,1)}, bf16[512,2048]{1,0:T(8,128)(2,1)}, u32[]{:S(2)}, u32[]{:S(2)}) collective-permute-start(bf16[512,2048]{1,0:T(8,128)(2,1)} %add_convert_fusion.4), channel_id=1, source_target_pairs={{0,8},{4,12},{8,0},{12,4},{16,24},{20,28},{24,16},{28,20},{1,9},{5... | collective-permute-start | bytes 6291464 | tf_op jit(solution)/shard_map/ppermute | solution.py:103
  835.6 97.6 %all-to-all-start.1 = ((bf16[8,264,256]{2,1,0:T(8,128)(2,1)}), bf16[8,264,256]{2,1,0:T(8,128)(2,1)S(1)}, u32[]{:S(2)}, u32[]{:S(2)}) async-start(bf16[8,264,256]{2,1,0:T(8,128)(2,1)} %bitcast.81), calls=%async_computation.4 | async-start | bytes 2162688 | tf_op jit(solution)/shard_map/all_to_all | solution.py:220
  839.3 144.7 %reduce-scatter.14.cloned.1.call-start = ((), (), s32[]{:S(2)}) async-start(), calls=%async_computation.14 | async-start | bytes 2621440 | tf_op jit(solution)/shard_map/reduce_scatter | solution.py:215
  860.5 172.6 %collective-permute-start.54 = (bf16[64,5376]{1,0:T(8,128)(2,1)}, bf16[64,5376]{1,0:T(8,128)(2,1)}, u32[]{:S(2)}, u32[]{:S(2)}) collective-permute-start(bf16[64,5376]{1,0:T(8,128)(2,1)} %get-tuple-element.416), channel_id=1, source_target_pairs={{0,8},{4,12},{8,0},{12,4},{16,24},{20,28},{24,16},{28,20},{1,9},{5... | collective-permute-start | bytes 2064392 | tf_op jit(solution)/shard_map/ppermute | solution.py:103
  942.1 119.7 %reduce-scatter.18.cloned.1.call-start = ((), (), s32[]{:S(2)}) async-start(), calls=%async_computation.16 | async-start | bytes 1392640
  986.1 70.5 %collective-permute-start.56 = (bf16[64,5376]{1,0:T(8,128)(2,1)}, bf16[64,5376]{1,0:T(8,128)(2,1)}, u32[]{:S(2)}, u32[]{:S(2)}) collective-permute-start(bf16[64,5376]{1,0:T(8,128)(2,1)} %get-tuple-element.415), channel_id=1, source_target_pairs={{0,16},{4,20},{8,24},{12,28},{16,0},{20,4},{24,8},{28,12},{1,17},{... | collective-permute-start | bytes 2064392 | tf_op jit(solution)/shard_map/ppermute | solution.py:103
  (205 other events, 2517.0 us)
Sparse Core Ops, SparseCore 0:
  11.7 31.8 all-gather.5
  76.0 46.1 all-gather.7
  167.9 48.9 all-gather.9
  233.7 41.8 reduce-scatter.9
  304.7 45.9 all-gather.11
  657.9 41.5 reduce-scatter.11
  702.6 44.8 all-gather.13
  804.5 44.4 reduce-scatter.15
  942.2 41.6 reduce-scatter.13
  1033.2 26.3 reduce-scatter.17

commit v5 on v3

--- a/solution.py
+++ b/solution.py
@@ -368,8 +368,6 @@
     latents_own = jnp.concatenate([query_latent, key_latent, rope_own], axis=1)
     latents = gather_rows(after(latents_own, grad_line))
     hidden_in = jnp.concatenate(after(hidden_pieces, latents_own), axis=1)
-    packed = jnp.concatenate(after(packed_chunks, latents_own), axis=0)
-    gain_attn = jnp.concatenate([g[0] for g in after(gain_pieces, latents_own)])
     query_all = latents[:, :q_rank]
     key_all = latents[:, q_rank : q_rank + KVRANK]
     rope_all = latents[:, q_rank + KVRANK :]
@@ -499,12 +497,15 @@
         back_sum = jnp.concatenate(backs, axis=0)
     d_hidden_mid = scatter_rows(back_sum)
 
+    if four_chips():
+        out_products = [as_half(product(act, cat_down)) for act in after(act_blocks, back_sum)]
+        d_hidden_mid, out_products = lax.optimization_barrier((d_hidden_mid, out_products))
     grad_gain_ffn = jnp.sum(d_hidden_mid * normed_mid, axis=0)
     d_mid = out_grad + norm_back(d_hidden_mid, normed_mid, scale_mid, gain_ffn)
     mid_low = as_half(d_mid)
     act_blocks = after(act_blocks, back_sum)
     if four_chips():
-        out_parts = [pair_sum(as_half(product(act, cat_down))) for act in act_blocks]
+        out_parts = [pair_sum(out) for out in out_products]
     else:
         for act in act_blocks:
             if out_parts:
@@ -590,15 +591,19 @@
     grad_gain_key = jnp.sum(latent_k * normed_key, axis=0)
     d_key_raw = norm_back(latent_k, normed_key, scale_key, gain_key)
     d_rope_raw = unrotate(latent_r, cos_own, sin_own)
-    extra = packed.shape[1] - raw_width
+    extra = packed_own.shape[1] - raw_width
     d_raw = as_half(
         jnp.concatenate(
             [d_query_raw, d_key_raw, d_rope_raw, jnp.zeros((own_rows, extra), jnp.float32)], axis=1
         )
     )
-    d_hidden_in = against_rows(d_raw, packed)
+    d_hidden_in = jnp.concatenate([against_rows(d_raw, c) for c in packed_chunks], axis=1)
+    scaled_in = jnp.concatenate(
+        [against_rows(d_raw, c) * g[0] for c, g in zip(packed_chunks, gain_pieces)], axis=1
+    )
     grad_gain_attn = jnp.sum(d_hidden_in * normed_in, axis=0)
-    input_grad = d_mid + reorder(norm_back(d_hidden_in, normed_in, scale_in, gain_attn), 1)
+    inner = jnp.mean(scaled_in * normed_in, axis=-1, keepdims=True)
+    input_grad = d_mid + reorder(scale_in * (scaled_in - normed_in * inner), 1)
     rank_grads = jnp.concatenate(
         [grad_gain_query.reshape(-1, q_shard), grad_gain_key.reshape(-1, shard - q_shard)], axis=1
     ).reshape(-1)

time: 1090 us -> 1050 us (0.963)
  local copies, waits for them, and re-layouts: 250 us -> 162 us
  waiting for transfers between devices: 326 us -> 410 us
  other arithmetic: 121 us -> 71.4 us
  matrix products: 308 us -> 331 us
    all_to_all x2, waiting for transfers between devices: 4.04 us -> 82.6 us  [exchange(): return lax.all_to_all(block, 'dp', split_axis=0, concat_axis=0, tiled=True)]
    convert_element_type x31 -> x27, other arithmetic: 74.1 us -> 42.8 us  [as_half(): return values.astype(jnp.bfloat16)]
    dot_general x16 -> x23, matrix products: 73.4 us -> 102 us  [against_rows(): lax.dot_general(left, right, (((1,), (1,)), ((), ())), preferred_element_...]
    unnamed x407 -> x408, local copies, waits for them, and re-layouts: 74.4 us -> 48.9 us
    reduce_scatter x3, waiting for transfers between devices: 1.79 us -> 20.7 us  [scatter_rows(): lax.psum_scatter(as_half(rows), 'tensor', scatter_dimension=0, tiled=True)]
    optimization_barrier x7 -> x1, local copies, waits for them, and re-layouts: 14.4 us -> 0.09 us  [after(): return lax.optimization_barrier((value, before))[0]]
  transfers between devices with their start and end apart: 71 -> 71, of which waited for: 27 -> 30; matrix products, arithmetic and copies ran while one was open for 55% -> 45% of each run, Pallas kernels for 0% -> 0%
where the time goes in v5:
time: 1050 us; the launch traced here: 1040 us
  waiting for transfers between devices  410 us (39%)
  matrix products  331 us (32%)
  local copies, waits for them, and re-layouts  162 us (15%)
  other arithmetic  71.4 us (7%)
  starting transfers between devices  50.9 us (5%)
  between operations  17.6 us (2%)
    ppermute x59, waiting for transfers between devices, swap(): return lax.ppermute(rows, 'dp', [(i, i ^ mask) for i in range(count)])  277 us
    dot_general x16, matrix products, contract_rows(): lax.dot_general(left, right, (((0,), (0,)), ((), ())), preferred_element_...  104 us
    dot_general x23, matrix products, against_rows(): lax.dot_general(left, right, (((1,), (1,)), ((), ())), preferred_element_...  102 us
    all_to_all x2, waiting for transfers between devices, exchange(): return lax.all_to_all(block, 'dp', split_axis=0, concat_axis=0, tiled=True)  82.6 us
    dot_general x19, matrix products, product(): return jnp.dot(left, right, preferred_element_type=jnp.float32)  82.5 us
    unnamed x408, local copies, waits for them, and re-layouts  48.9 us
    convert_element_type x27, other arithmetic, as_half(): return values.astype(jnp.bfloat16)  42.8 us
    ppermute x59, starting transfers between devices, swap(): return lax.ppermute(rows, 'dp', [(i, i ^ mask) for i in range(count)])  42.4 us
  transfers between devices with their start and end apart: 71, of which 30 were waited for; matrix products, arithmetic and copies ran while one was open for 45% of the time, Pallas kernels for 0%

profile of v5, /device:TPU:0, one launch (start us, length us, event | category | flops | bytes accessed | tf_op | source)
XLA Modules:
  0.0 1043.3 jit_solution(11088836348611909548)
XLA Ops:
  22.2 13.2 %collective-permute-done.1 = bf16[64,5632]{1,0:T(8,128)(2,1)} collective-permute-done((bf16[64,5632]{1,0:T(8,128)(2,1)}, bf16[64,5632]{1,0:T(8,128)(2,1)}, u32[]{:S(2)}, u32[]{:S(2)}) %collective-permute-start.1) | collective-permute-done | bytes 720928 | tf_op jit(solution)/shard_map/ppermute | solution.py:103
  67.4 17.6 %collective-permute-done.9 = bf16[256,2115]{0,1:T(8,128)(2,1)S(1)} collective-permute-done((bf16[256,2115]{0,1:T(8,128)(2,1)}, bf16[256,2115]{0,1:T(8,128)(2,1)S(1)}, u32[]{:S(2)}, u32[]{:S(2)}) %collective-permute-start.9) | collective-permute-done | bytes 1082912 | tf_op jit(solution)/shard_map/ppermute | solution.py:103
  89.5 9.6 collective-permute-done.13
  145.4 10.9 %all-gather.10.cloned.1.call-done = bf16[512,2112]{0,1:T(8,128)(2,1)} async-done(((bf16[128,2112]{0,1:T(8,128)(2,1)}), bf16[512,2112]{0,1:T(8,128)(2,1)}) %all-gather.10.cloned.1.call-update) | async-done | bytes 2162704 | tf_op jit(solution)/shard_map/all_gather | solution.py:210
  179.2 11.6 %collective-permute-done.16 = bf16[512,2048]{1,0:T(8,128)(2,1)} collective-permute-done((bf16[512,2048]{1,0:T(8,128)(2,1)}, bf16[512,2048]{1,0:T(8,128)(2,1)}, u32[]{:S(2)}, u32[]{:S(2)}) %collective-permute-start.16) | collective-permute-done | bytes 2097184 | tf_op jit(solution)/shard_map/ppermute | solution.py:103
  190.8 44.8 %collective-permute-done.17 = bf16[512,2048]{1,0:T(8,128)(2,1)} collective-permute-done((bf16[512,2048]{1,0:T(8,128)(2,1)}, bf16[512,2048]{1,0:T(8,128)(2,1)}, u32[]{:S(2)}, u32[]{:S(2)}) %collective-permute-start.17) | collective-permute-done | bytes 2097184 | tf_op jit(solution)/shard_map/ppermute | solution.py:103
  243.1 12.9 %all-to-all-done = bf16[8,264,256]{2,1,0:T(8,128)(2,1)S(1)} async-done(((bf16[8,264,256]{2,1,0:T(8,128)(2,1)}), bf16[8,264,256]{2,1,0:T(8,128)(2,1)S(1)}, u32[]{:S(2)}, u32[]{:S(2)}) %all-to-all-start) | async-done | bytes 1081376 | tf_op jit(solution)/shard_map/all_to_all | solution.py:220
  310.7 14.7 %all-gather.12.cloned.1.call-done = bf16[512,2048]{1,0:T(8,128)(2,1)} async-done(((bf16[128,2048]{1,0:T(8,128)(2,1)}), bf16[512,2048]{1,0:T(8,128)(2,1)}) %all-gather.12.cloned.1.call-update) | async-done | bytes 2097168 | tf_op jit(solution)/shard_map/all_gather | solution.py:210
  344.5 10.0 convolution_convert_fusion.3
  354.5 19.3 %collective-permute-done.25 = bf16[512,2048]{1,0:T(8,128)(2,1)S(1)} collective-permute-done((bf16[512,2048]{1,0:T(8,128)(2,1)}, bf16[512,2048]{1,0:T(8,128)(2,1)S(1)}, u32[]{:S(2)}, u32[]{:S(2)}) %collective-permute-start.25) | collective-permute-done | bytes 2097184 | tf_op jit(solution)/shard_map/ppermute | solution.py:103
  394.3 10.5 %convolution_convert_fusion.2 = bf16[1024,2048]{1,0:T(8,128)(2,1)S(1)} fusion(bf16[1024,800]{0,1:T(8,128)(2,1)} %get-tuple-element.370, bf16[1024,800]{0,1:T(8,128)(2,1)} %get-tuple-element.369, bf16[96,2048]{1,0:T(8,128)(2,1)S(1)} %pad.16, bf16[704,2048]{1,0:T(8,128)(2,1)} %bitcast.380, bf16[96,2048]{1,0:T(8,128)(2,1)S(1)} %pad.15, ...), kind=kOutput, calls=%fused_computation.29 | convolution fusion | flops 6745751552 | bytes 14024704 | tf_op jit(solution)/shard_map/dot_general | solution.py:29
  407.5 23.2 %collective-permute-done.34 = bf16[256,2048]{1,0:T(8,128)(2,1)S(1)} collective-permute-done((bf16[256,2048]{1,0:T(8,128)(2,1)S(1)}, bf16[256,2048]{1,0:T(8,128)(2,1)S(1)}, u32[]{:S(2)}, u32[]{:S(2)}) %collective-permute-start.34) | collective-permute-done | bytes 1048608 | tf_op jit(solution)/shard_map/ppermute | solution.py:103
  449.0 10.7 %convolution_convert_fusion.1 = bf16[1024,2048]{1,0:T(8,128)(2,1)S(1)} fusion(bf16[1024,800]{0,1:T(8,128)(2,1)S(1)} %get-tuple-element.367, bf16[1024,800]{0,1:T(8,128)(2,1)} %get-tuple-element.366, bf16[96,2048]{1,0:T(8,128)(2,1)S(1)} %pad.16, bf16[704,2048]{1,0:T(8,128)(2,1)} %bitcast.381, bf16[96,2048]{1,0:T(8,128)(2,1)S(1)} %pad.15, ...), kind=kOutput, calls=%fused_computation.28 | convolution fusion | flops 6745751552 | bytes 14024704 | tf_op jit(solution)/shard_map/dot_general | solution.py:29
  499.0 11.2 %convolution_convert_fusion = bf16[1024,2048]{1,0:T(8,128)(2,1)S(1)} fusion(bf16[1024,800]{0,1:T(8,128)(2,1)S(1)} %get-tuple-element.364, bf16[1024,800]{0,1:T(8,128)(2,1)} %get-tuple-element.363, bf16[96,2048]{1,0:T(8,128)(2,1)S(1)} %pad.16, bf16[704,2048]{1,0:T(8,128)(2,1)} %bitcast.382, bf16[96,2048]{1,0:T(8,128)(2,1)S(1)} %pad.15, ...), kind=kOutput, calls=%fused_computation.27 | convolution fusion | flops 6745751552 | bytes 14024704 | tf_op jit(solution)/shard_map/dot_general | solution.py:29
  535.7 15.1 %add_add_fusion.2 = f32[800,2048]{1,0:T(8,128)} fusion(f32[800,2048]{1,0:T(8,128)} %fusion.155, f32[800,2048]{1,0:T(8,128)} %fusion.153, f32[800,2048]{1,0:T(8,128)} %fusion.154, bf16[1024,800]{0,1:T(8,128)(2,1)} %get-tuple-element.363, bf16[1024,2048]{1,0:T(8,128)(2,1)} %copy-done.53), kind=kOutput, calls=%fused_computation.6 | convolution fusion | flops 3360358400 | bytes 32047104 | tf_op jit(solution)/shard_map/dot_general | solution.py:33
  550.7 10.9 %add_add_fusion.1 = f32[800,2048]{1,0:T(8,128)} fusion(f32[800,2048]{1,0:T(8,128)} %fusion.158, f32[800,2048]{1,0:T(8,128)} %fusion.156, f32[800,2048]{1,0:T(8,128)} %fusion.157, bf16[1024,800]{0,1:T(8,128)(2,1)} %copy-done.167, bf16[1024,2048]{1,0:T(8,128)(2,1)S(1)} %copy-done.54), kind=kOutput, calls=%fused_computation.5 | convolution fusion | flops 3360358400 | bytes 32047104 | tf_op jit(solution)/shard_map/dot_general | solution.py:33
  561.7 52.3 %collective-permute-done.37 = bf16[512,2048]{1,0:T(8,128)(2,1)S(1)} collective-permute-done((bf16[512,2048]{1,0:T(8,128)(2,1)S(1)}, bf16[512,2048]{1,0:T(8,128)(2,1)S(1)}, u32[]{:S(2)}, u32[]{:S(2)}) %collective-permute-start.37) | collective-permute-done | bytes 2097184 | tf_op jit(solution)/shard_map/ppermute | solution.py:103
  614.0 11.5 %collective-permute-done.32 = bf16[512,2048]{1,0:T(8,128)(2,1)} collective-permute-done((bf16[512,2048]{1,0:T(8,128)(2,1)S(1)}, bf16[512,2048]{1,0:T(8,128)(2,1)}, u32[]{:S(2)}, u32[]{:S(2)}) %collective-permute-start.32) | collective-permute-done | bytes 2097184 | tf_op jit(solution)/shard_map/ppermute | solution.py:103
  659.3 13.8 %reduce-scatter.12.cloned.1.call-done = bf16[128,2048]{1,0:T(8,128)(2,1)} async-done(((bf16[512,2048]{1,0:T(8,128)(2,1)}), bf16[128,2048]{1,0:T(8,128)(2,1)}) %reduce-scatter.12.cloned.1.call-update) | async-done | bytes 524304 | tf_op jit(solution)/shard_map/reduce_scatter | solution.py:215
  704.0 12.2 %add_add_fusion = f32[800,2048]{1,0:T(8,128)} fusion(f32[800,2048]{1,0:T(8,128)} %fusion.161, f32[800,2048]{1,0:T(8,128)} %fusion.159, f32[800,2048]{1,0:T(8,128)} %fusion.160, bf16[1024,800]{0,1:T(8,128)(2,1)S(1)} %copy-done.166, bf16[1024,2048]{1,0:T(8,128)(2,1)} %constant_dynamic-update-slice_fusion.10), kind=kOutput, calls=%fused_computation.4 | convolution fusion | flops 3360358400 | bytes 32047104 | tf_op jit(solution)/shard_map/dot_general | solution.py:33
  837.5 69.7 %all-to-all-done.1 = bf16[8,264,256]{2,1,0:T(8,128)(2,1)S(1)} async-done(((bf16[8,264,256]{2,1,0:T(8,128)(2,1)}), bf16[8,264,256]{2,1,0:T(8,128)(2,1)S(1)}, u32[]{:S(2)}, u32[]{:S(2)}) %all-to-all-start.1) | async-done | bytes 1081376 | tf_op jit(solution)/shard_map/all_to_all | solution.py:220
  961.6 12.8 %collective-permute-done.51 = bf16[256,2115]{0,1:T(8,128)(2,1)} collective-permute-done((bf16[256,2115]{0,1:T(8,128)(2,1)}, bf16[256,2115]{0,1:T(8,128)(2,1)}, u32[]{:S(2)}, u32[]{:S(2)}) %collective-permute-start.51) | collective-permute-done | bytes 1082912 | tf_op jit(solution)/shard_map/ppermute | solution.py:103
  975.9 21.8 %collective-permute-done.49 = bf16[256,2115]{0,1:T(8,128)(2,1)} collective-permute-done((bf16[256,2115]{0,1:T(8,128)(2,1)}, bf16[256,2115]{0,1:T(8,128)(2,1)}, u32[]{:S(2)}, u32[]{:S(2)}) %collective-permute-start.49) | collective-permute-done | bytes 1082912 | tf_op jit(solution)/shard_map/ppermute | solution.py:103
  1002.5 23.7 %collective-permute-done.56 = bf16[64,5376]{1,0:T(8,128)(2,1)S(1)} collective-permute-done((bf16[64,5376]{1,0:T(8,128)(2,1)}, bf16[64,5376]{1,0:T(8,128)(2,1)S(1)}, u32[]{:S(2)}, u32[]{:S(2)}) %collective-permute-start.56) | collective-permute-done | bytes 688160 | tf_op jit(solution)/shard_map/ppermute | solution.py:103
  (828 shorter events, 561.7 us)
Async XLA Ops:
  11.6 96.5 %all-gather.8.cloned.1.call-start = ((), (), s32[]{:S(2)}) async-start(), calls=%async_computation.8 | async-start | bytes 2621440 | tf_op jit(solution)/shard_map/all_gather | solution.py:210
  61.7 94.6 %all-gather.10.cloned.1.call-start = ((), (), s32[]{:S(2)}) async-start(), calls=%async_computation.9 | async-start | bytes 2703360 | tf_op jit(solution)/shard_map/all_gather | solution.py:210
  108.0 170.2 %reduce-scatter.10.cloned.1.call-start = ((), (), s32[]{:S(2)}) async-start(), calls=%async_computation.10 | async-start | bytes 2621440 | tf_op jit(solution)/shard_map/reduce_scatter | solution.py:215
  143.4 92.2 %collective-permute-start.17 = (bf16[512,2048]{1,0:T(8,128)(2,1)}, bf16[512,2048]{1,0:T(8,128)(2,1)}, u32[]{:S(2)}, u32[]{:S(2)}) collective-permute-start(bf16[512,2048]{1,0:T(8,128)(2,1)} %all-gather.8.cloned.1.call-done), channel_id=1, source_target_pairs={{0,16},{4,20},{8,24},{12,28},{16,0},{20,4},{24,8},{28,12},{1,17},{... | collective-permute-start | bytes 6291464 | tf_op jit(solution)/shard_map/ppermute | solution.py:103
  144.9 90.7 %collective-permute-start.18 = (bf16[512,2048]{1,0:T(8,128)(2,1)}, bf16[512,2048]{1,0:T(8,128)(2,1)}, u32[]{:S(2)}, u32[]{:S(2)}) collective-permute-start(bf16[512,2048]{1,0:T(8,128)(2,1)} %all-gather.8.cloned.1.call-done), channel_id=1, source_target_pairs={{0,24},{4,28},{8,16},{12,20},{16,8},{20,12},{24,0},{28,4},{1,25},{... | collective-permute-start | bytes 6291464 | tf_op jit(solution)/shard_map/ppermute | solution.py:103
  240.3 85.1 %all-gather.12.cloned.1.call-start = ((), (), s32[]{:S(2)}) async-start(), calls=%async_computation.11 | async-start | bytes 2621440 | tf_op jit(solution)/shard_map/all_gather | solution.py:210
  281.4 391.6 %reduce-scatter.12.cloned.1.call-start = ((), (), s32[]{:S(2)}) async-start(), calls=%async_computation.12 | async-start | bytes 2621440 | tf_op jit(solution)/shard_map/reduce_scatter | solution.py:215
  467.9 146.1 %collective-permute-start.24 = (bf16[512,2048]{1,0:T(8,128)(2,1)S(1)}, bf16[512,2048]{1,0:T(8,128)(2,1)}, u32[]{:S(2)}, u32[]{:S(2)}) collective-permute-start(bf16[512,2048]{1,0:T(8,128)(2,1)S(1)} %slice.472), channel_id=1, source_target_pairs={{0,4},{4,0},{8,12},{12,8},{16,20},{20,16},{24,28},{28,24},{1,5},{5... | collective-permute-start | bytes 6291464 | tf_op jit(solution)/shard_map/ppermute | solution.py:103
  520.0 94.0 %collective-permute-start.29 = (bf16[512,2048]{1,0:T(8,128)(2,1)S(1)}, bf16[512,2048]{1,0:T(8,128)(2,1)S(1)}, u32[]{:S(2)}, u32[]{:S(2)}) collective-permute-start(bf16[512,2048]{1,0:T(8,128)(2,1)S(1)} %add_convert_fusion.9), channel_id=1, source_target_pairs={{0,8},{4,12},{8,0},{12,4},{16,24},{20,28},{24,16},{28,20},{1,9},{5... | collective-permute-start | bytes 6291464 | tf_op jit(solution)/shard_map/ppermute | solution.py:103
  532.8 92.8 %collective-permute-start.32 = (bf16[512,2048]{1,0:T(8,128)(2,1)S(1)}, bf16[512,2048]{1,0:T(8,128)(2,1)}, u32[]{:S(2)}, u32[]{:S(2)}) collective-permute-start(bf16[512,2048]{1,0:T(8,128)(2,1)S(1)} %add_convert_fusion.8), channel_id=1, source_target_pairs={{0,16},{4,20},{8,24},{12,28},{16,0},{20,4},{24,8},{28,12},{1,17},{... | collective-permute-start | bytes 6291464 | tf_op jit(solution)/shard_map/ppermute | solution.py:103
  535.0 78.9 %collective-permute-start.37 = (bf16[512,2048]{1,0:T(8,128)(2,1)S(1)}, bf16[512,2048]{1,0:T(8,128)(2,1)S(1)}, u32[]{:S(2)}, u32[]{:S(2)}) collective-permute-start(bf16[512,2048]{1,0:T(8,128)(2,1)S(1)} %add_convert_fusion.7), channel_id=1, source_target_pairs={{0,24},{4,28},{8,16},{12,20},{16,8},{20,12},{24,0},{28,4},{1,25},{... | collective-permute-start | bytes 6291464 | tf_op jit(solution)/shard_map/ppermute | solution.py:103
  631.4 89.7 %all-gather.14.cloned.1.call-start = ((), (), s32[]{:S(2)}) async-start(), calls=%async_computation.13 | async-start | bytes 2621440 | tf_op jit(solution)/shard_map/all_gather | solution.py:210
  676.1 240.3 %reduce-scatter.16.cloned.1.call-start = ((), (), s32[]{:S(2)}) async-start(), calls=%async_computation.15 | async-start | bytes 2785280
  681.5 110.2 %collective-permute-start.41 = (bf16[512,2048]{1,0:T(8,128)(2,1)}, bf16[512,2048]{1,0:T(8,128)(2,1)}, u32[]{:S(2)}, u32[]{:S(2)}) collective-permute-start(bf16[512,2048]{1,0:T(8,128)(2,1)} %slice.401), channel_id=1, source_target_pairs={{0,4},{4,0},{8,12},{12,8},{16,20},{20,16},{24,28},{28,24},{1,5},{5... | collective-permute-start | bytes 6291464 | tf_op jit(solution)/shard_map/ppermute | solution.py:103
  683.3 113.8 %collective-permute-start.39 = (bf16[512,2048]{1,0:T(8,128)(2,1)}, bf16[512,2048]{1,0:T(8,128)(2,1)}, u32[]{:S(2)}, u32[]{:S(2)}) collective-permute-start(bf16[512,2048]{1,0:T(8,128)(2,1)} %slice.399), channel_id=1, source_target_pairs={{0,4},{4,0},{8,12},{12,8},{16,20},{20,16},{24,28},{28,24},{1,5},{5... | collective-permute-start | bytes 6291464 | tf_op jit(solution)/shard_map/ppermute | solution.py:103
  684.9 223.2 %collective-permute-start.38 = (bf16[512,2048]{1,0:T(8,128)(2,1)}, bf16[512,2048]{1,0:T(8,128)(2,1)}, u32[]{:S(2)}, u32[]{:S(2)}) collective-permute-start(bf16[512,2048]{1,0:T(8,128)(2,1)} %slice.397), channel_id=1, source_target_pairs={{0,4},{4,0},{8,12},{12,8},{16,20},{20,16},{24,28},{28,24},{1,5},{5... | collective-permute-start | bytes 6291464 | tf_op jit(solution)/shard_map/ppermute | solution.py:103
  800.9 107.2 %collective-permute-start.44 = (bf16[512,2048]{1,0:T(8,128)(2,1)}, bf16[512,2048]{1,0:T(8,128)(2,1)}, u32[]{:S(2)}, u32[]{:S(2)}) collective-permute-start(bf16[512,2048]{1,0:T(8,128)(2,1)} %add_convert_fusion.2), channel_id=1, source_target_pairs={{0,24},{4,28},{8,16},{12,20},{16,8},{20,12},{24,0},{28,4},{1,25},{... | collective-permute-start | bytes 6291464 | tf_op jit(solution)/shard_map/ppermute | solution.py:103
  803.3 104.8 %collective-permute-start.42 = (bf16[512,2048]{1,0:T(8,128)(2,1)}, bf16[512,2048]{1,0:T(8,128)(2,1)}, u32[]{:S(2)}, u32[]{:S(2)}) collective-permute-start(bf16[512,2048]{1,0:T(8,128)(2,1)} %add_convert_fusion.3), channel_id=1, source_target_pairs={{0,16},{4,20},{8,24},{12,28},{16,0},{20,4},{24,8},{28,12},{1,17},{... | collective-permute-start | bytes 6291464 | tf_op jit(solution)/shard_map/ppermute | solution.py:103
  803.8 104.3 %collective-permute-start.40 = (bf16[512,2048]{1,0:T(8,128)(2,1)}, bf16[512,2048]{1,0:T(8,128)(2,1)}, u32[]{:S(2)}, u32[]{:S(2)}) collective-permute-start(bf16[512,2048]{1,0:T(8,128)(2,1)} %add_convert_fusion.4), channel_id=1, source_target_pairs={{0,8},{4,12},{8,0},{12,4},{16,24},{20,28},{24,16},{28,20},{1,9},{5... | collective-permute-start | bytes 6291464 | tf_op jit(solution)/shard_map/ppermute | solution.py:103
  810.8 96.3 %all-to-all-start.1 = ((bf16[8,264,256]{2,1,0:T(8,128)(2,1)}), bf16[8,264,256]{2,1,0:T(8,128)(2,1)S(1)}, u32[]{:S(2)}, u32[]{:S(2)}) async-start(bf16[8,264,256]{2,1,0:T(8,128)(2,1)} %bitcast.76), calls=%async_computation.4 | async-start | bytes 2162688 | tf_op jit(solution)/shard_map/all_to_all | solution.py:220
  814.4 143.6 %reduce-scatter.14.cloned.1.call-start = ((), (), s32[]{:S(2)}) async-start(), calls=%async_computation.14 | async-start | bytes 2621440 | tf_op jit(solution)/shard_map/reduce_scatter | solution.py:215
  835.4 167.1 %collective-permute-start.54 = (bf16[64,5376]{1,0:T(8,128)(2,1)}, bf16[64,5376]{1,0:T(8,128)(2,1)}, u32[]{:S(2)}, u32[]{:S(2)}) collective-permute-start(bf16[64,5376]{1,0:T(8,128)(2,1)} %get-tuple-element.376), channel_id=1, source_target_pairs={{0,8},{4,12},{8,0},{12,4},{16,24},{20,28},{24,16},{28,20},{1,9},{5... | collective-permute-start | bytes 2064392 | tf_op jit(solution)/shard_map/ppermute | solution.py:103
  916.0 115.2 %reduce-scatter.18.cloned.1.call-start = ((), (), s32[]{:S(2)}) async-start(), calls=%async_computation.16 | async-start | bytes 1392640
  960.1 66.0 %collective-permute-start.56 = (bf16[64,5376]{1,0:T(8,128)(2,1)}, bf16[64,5376]{1,0:T(8,128)(2,1)S(1)}, u32[]{:S(2)}, u32[]{:S(2)}) collective-permute-start(bf16[64,5376]{1,0:T(8,128)(2,1)} %get-tuple-element.375), channel_id=1, source_target_pairs={{0,16},{4,20},{8,24},{12,28},{16,0},{20,4},{24,8},{28,12},{1,17},{... | collective-permute-start | bytes 2064392 | tf_op jit(solution)/shard_map/ppermute | solution.py:103
  (230 other events, 3318.5 us)
Sparse Core Ops, SparseCore 0:
  11.7 31.8 all-gather.5
  61.9 46.1 all-gather.7
  110.2 46.1 all-gather.9
  179.3 41.8 reduce-scatter.9
  281.6 43.8 all-gather.11
  631.5 41.4 reduce-scatter.11
  676.2 44.8 all-gather.13
  778.3 44.4 reduce-scatter.15
  916.1 41.8 reduce-scatter.13
  1002.6 26.5 reduce-scatter.17
